TPU v7x, 128 devices: a whole 4x4x4 slice. The times are simulated.
128 devices in a mesh: dom: 16 (over y, x), sub: 8 (over z, core).
Axes of the slice: x: 4, y: 4, z: 4, core: 2. Of those that a mesh axis runs over, the one named last changes fastest.
Arguments:
- positions: float32 [8192, 3, 128], P(('dom', 'sub')), may hold values from -1 to 1
- masses: float32 [8192, 128], P(('dom', 'sub')), may hold values from 0.003 to 0.03
- owner: int32 [8192, 1], P(('dom', 'sub')), may hold values from 0 to 7; in each aligned block of 64 rows (0 to 63, 64 to 127, ...) at most 16 rows name the same one
- operators: float32 [165, 165, 128], replicated, may hold values from -0.0024414062 to 0.0024414062
- m2l_target: int32 [128, 8, 64, 128], P(('dom', 'sub')), may hold values from 0 to 127
- far_source: int32 [128, 7, 64, 128], P(('dom', 'sub')), may hold values from 0 to 31
- local_source: int32 [128, 64, 128], P(('dom', 'sub')), may hold values from 0 to 127
- export_slots: int32 [128, 7, 32], P(('dom', 'sub')), may hold values from 0 to 127
- near_target: int32 [128, 128], P(('dom', 'sub')), may hold values from 0 to 127
- near_source: int32 [128, 128], P(('dom', 'sub')), may hold values from 0 to 127
- near_offset: int32 [128, 128], P(('dom', 'sub')), may hold values from 0 to 26
Outputs:
- accel: float32 [16384, 4, 128], P(('dom', 'sub'))
Inputs may be any that keep to these rules, and one draw needn't show every extreme that they name: Among the 64 tiles of one device at most 16 share an owner, and some device has an owner named by exactly 16 of its tiles.
All inputs are finite; a program needn't handle non-finite values.
Results may differ from a plain program's by a relative error of at most 0.0003.
Values sent between devices are 32-bit elements; how exact they have to be, the bound alone decides.
No kernel may reach another device: no remote copies, remote signals or barrier semaphores. Data moves between devices by JAX's collectives and lax.ppermute only.
A program may use at most 256 MiB of HBM per device.

v0:
```python
import jax
import jax.numpy as jnp
import numpy as np
from jax import lax
from jax.sharding import PartitionSpec as P

ORDER = 8


softening = 0.01
highest = lax.Precision.HIGHEST


def swapped(array, axis, apart):
    return lax.ppermute(array, axis, [(i, i ^ 1 << apart) for i in range(lax.axis_size(axis))])


def term_tables():
    triples = []
    for degree in range(ORDER + 1):
        for power_x in range(degree, -1, -1):
            for power_y in range(degree - power_x, -1, -1):
                triples.append((power_x, power_y, degree - power_x - power_y))
    lookup = {triple: term_index for term_index, triple in enumerate(triples)}
    exponents = np.array(triples, dtype=np.int32)
    term_norms = np.sqrt(np.prod(2.0 * exponents + 1.0, axis=1))
    number_terms = len(triples)
    slopes = np.zeros((3, number_terms, number_terms), dtype=np.float32)
    for term_index, triple in enumerate(triples):
        for direction in range(3):
            raised = list(triple)
            raised[direction] += 1
            raised = tuple(raised)
            if raised in lookup:
                raised_index = lookup[raised]
                slopes[direction, term_index, raised_index] = (
                    raised[direction] * term_norms[raised_index] / term_norms[term_index]
                )
    return (exponents, term_norms.astype(np.float32), slopes)


def basis_values(places, exponents, term_norms):
    tables = []
    for direction in range(3):
        values = places[:, direction]
        powers = [jnp.ones_like(values)]
        for degree in range(ORDER):
            powers.append(powers[-1] * values)
        tables.append(jnp.stack(powers))
    result = tables[0][exponents[:, 0]] * tables[1][exponents[:, 1]] * tables[2][exponents[:, 2]]
    return result * jnp.asarray(term_norms).reshape(-1, 1, 1)


def pack_tiles(owners, places, weights, peer_count, capacity):
    onehot = (owners[:, None] == jnp.arange(peer_count, dtype=jnp.int32)[None, :]).astype(jnp.int32)
    earlier = jnp.cumsum(onehot, axis=0) - onehot
    rank_in = jnp.sum(earlier * onehot, axis=1)
    slot_index = owners * capacity + rank_in
    sent_places = (
        jnp.zeros((peer_count * capacity,) + places.shape[1:], jnp.float32)
        .at[slot_index]
        .set(places)
    )
    sent_weights = (
        jnp.zeros((peer_count * capacity,) + weights.shape[1:], jnp.float32)
        .at[slot_index]
        .set(weights)
    )
    return (sent_places, sent_weights)


def device_multipoles(places, weights, exponents, term_norms):
    slot_count = places.shape[0]
    bodies = places.shape[2]
    blocks = slot_count // 16

    def one_block(inputs):
        values = basis_values(inputs[0], exponents, term_norms)
        return jnp.einsum("nst,st->sn", values, inputs[1], precision=highest)

    result = lax.map(
        one_block, (places.reshape(blocks, 16, 3, bodies), weights.reshape(blocks, 16, bodies))
    )
    return result.reshape(slot_count, result.shape[2])


def translate(expansion, sources, operators, targets, rows):
    gathered = jnp.take(sources, rows, axis=0)
    translated = jnp.einsum("ijc,pcj->pci", operators, gathered, precision=highest)
    return expansion.at[targets.reshape(-1)].add(translated.reshape(-1, translated.shape[2]))


def near_block(places, weights, targets, sources, classes):
    shifts = 2.0 * jnp.stack(
        [classes // 9 - 1, classes // 3 % 3 - 1, classes % 3 - 1], axis=1
    ).astype(jnp.float32)
    source_places = places[sources] + shifts[:, :, None]
    target_places = places[targets]
    source_weights = weights[sources]
    separation = source_places[:, :, None, :] - target_places[:, :, :, None]
    inverse = lax.rsqrt(jnp.sum(separation * separation, axis=1) + softening)
    weighted = source_weights[:, None, :] * inverse
    potential = -jnp.sum(weighted, axis=2)
    cubed_inv = weighted * inverse * inverse
    pull_terms = jnp.sum(separation * cubed_inv[:, None], axis=3)
    return jnp.concatenate([potential[:, None], pull_terms], axis=1)


def device_field(
    places, weights, expansion, targets, sources, classes, exponents, term_norms, slopes
):
    slot_count = places.shape[0]
    bodies = places.shape[2]
    blocks = slot_count // 16
    terms_count = expansion.shape[1]
    gradients = jnp.einsum("aij,sj->asi", jnp.asarray(slopes), expansion, precision=highest)
    stacked = jnp.concatenate([expansion[None], -gradients], axis=0)
    stacked = jnp.moveaxis(stacked.reshape(4, blocks, 16, terms_count), 1, 0)

    def far_block(inputs):
        values = basis_values(inputs[0], exponents, term_norms)
        return jnp.einsum("csn,nst->sct", inputs[1], values, precision=highest)

    far_field = lax.map(far_block, (places.reshape(blocks, 16, 3, bodies), stacked)).reshape(
        slot_count, 4, bodies
    )
    pair_blocks = targets.shape[0] // 16

    def near_part(inputs):
        return near_block(places, weights, inputs[0], inputs[1], inputs[2])

    near_terms = lax.map(
        near_part,
        (
            targets.reshape(pair_blocks, 16),
            sources.reshape(pair_blocks, 16),
            classes.reshape(pair_blocks, 16),
        ),
    )
    near_field = (
        jnp.zeros((slot_count, 4, bodies), jnp.float32)
        .at[targets]
        .add(near_terms.reshape(-1, 4, bodies))
    )
    present = (weights[:, :1] > 0).astype(jnp.float32)[:, :, None]
    return (far_field + near_field) * present


def body(
    positions,
    masses,
    owner,
    operators,
    m2l_target,
    far_source,
    local_source,
    export_slots,
    near_target,
    near_source,
    near_offset,
):
    exponents, term_norms, slopes = term_tables()
    peer_count = lax.axis_size("sub")
    tile_count = positions.shape[0]
    capacity = 2 * tile_count // peer_count
    sent_places, sent_weights = pack_tiles(owner[:, 0], positions, masses, peer_count, capacity)
    places, weights = (
        lax.all_to_all(sent_places, "sub", split_axis=0, concat_axis=0, tiled=True),
        lax.all_to_all(sent_weights, "sub", split_axis=0, concat_axis=0, tiled=True),
    )
    multipoles = device_multipoles(places, weights, exponents, term_norms)
    levels = lax.axis_size(("dom", "sub")).bit_length() - 1
    expansion = jnp.zeros((places.shape[0], multipoles.shape[1]), jnp.float32)
    expansion = translate(expansion, multipoles, operators, m2l_target[0, levels], local_source[0])
    for bit_level in range(levels):
        wanted = export_slots[0, bit_level].astype(jnp.float32)
        partner_all, partner_wanted = swapped((multipoles, wanted), ("dom", "sub"), bit_level)
        sources = jnp.take(partner_all, partner_wanted.astype(jnp.int32), axis=0)
        expansion = translate(
            expansion, sources, operators, m2l_target[0, bit_level], far_source[0, bit_level]
        )
    return device_field(
        places,
        weights,
        expansion,
        near_target[0],
        near_source[0],
        near_offset[0],
        exponents,
        term_norms,
        slopes,
    )


def solution(mesh):
    in_specs = (
        P(("dom", "sub"), None, None),
        P(("dom", "sub"), None),
        P(("dom", "sub"), None),
        P(),
        P(("dom", "sub"), None, None, None),
        P(("dom", "sub"), None, None, None),
        P(("dom", "sub"), None, None),
        P(("dom", "sub"), None, None),
        P(("dom", "sub"), None),
        P(("dom", "sub"), None),
        P(("dom", "sub"), None),
    )
    out_specs = P(("dom", "sub"), None, None)
    return jax.shard_map(body, mesh=mesh, in_specs=in_specs, out_specs=out_specs, check_vma=False)
```

profile of v0, /device:TPU:0, one launch (start us, length us, event | category | flops | bytes accessed | tf_op | source)
XLA Modules:
  0.0 1245.9 jit_solution(5776618213303280933)
XLA Ops:
  24.2 21.7 %copy.111 = f32[165,165,128]{1,0,2:T(8,128)} copy(f32[165,165,128]{2,1,0:T(8,128)} %param.38) | data formatting | bytes 27878400 | tf_op args[3]
  85.9 75.1 %while.38 = (s32[]{:T(128)}, f32[8,16,165]{2,1,0:T(8,128)}, f32[8,16,3,128]{3,1,2,0:T(8,128)}, f32[8,16,128]{2,1,0:T(8,128)S(1)}, s32[]{:T(128)}, /*index=5*/s32...) while((s32[]{:T(128)}, f32[8,16,165]{2,1,0:T(8,128)}, ...), condition=%wide.region_5.6_spmd.clone.clone, body=%wide.region_4.5_spmd.sunk.clone.clone.sunk | while | flops 5243905 | bytes 15414525 | solution.py:81
  165.7 32.4 %gather_fusion.9 = f32[8192,165]{1,0:T(8,128)} fusion(f32[128,165]{1,0:T(8,128)} %bitcast.20, s32[8192]{0:T(1024)S(1)} %fusion.90), kind=kCustom, calls=%fused_computation.23 | custom fusion | bytes 10846208 | tf_op jit(solution)/shard_map/jit(_take)/gather | solution.py:88
  198.2 42.7 %while.37 = (s32[]{:T(128)}, f32[8,16,4,128]{3,2,1,0:T(4,128)S(1)}, s32[8,16]{1,0:T(8,128)S(1)}, f32[128,128]{1,0:T(8,128)S(1)}, f32[128,3,128]{2,1,0:T(4,128)S(...) while((s32[]{:T(128)}, f32[8,16,4,128]{3,2,1,0:T(4,128)S(1)}, s32[8,16]{1,0:T(8,128)S(1)}, ...), condition=%wide.region_20.23_spmd, body=%wide.region_16.22_spmd.sunk | while | flops 5778130 | bytes 4597609 | solution.py:132
  240.9 31.8 %fusion.77 = f32[64,128,165]{2,0,1:T(8,128)} fusion(f32[165,165,128]{1,0,2:T(8,128)} %copy.111, f32[64,128,165]{2,1,0:T(8,128)} %bitcast.445, pred[64,128]{0,1:T(8,128)(4,1)S(1)} %copy.107), kind=kOutput, calls=%fused_computation.215 | convolution fusion | flops 2677678080 | bytes 24760832 | tf_op jit(solution)/shard_map/ijc,pcj->pci/dot_general | solution.py:89
  272.7 11.6 copy.157
  284.3 45.2 %scatter_custom_fusion.2 = f32[128,165]{1,0:T(8,128)} fusion(s32[8192]{0:T(1024)S(1)} %bitcast.483, f32[8192,165]{1,0:T(8,128)} %bitcast.459, f32[]{:T(128)} %constant.183.clone.1), kind=kCustom, calls=%fused_computation.247 | custom fusion | flops 1351680 | bytes 84992 | tf_op jit(solution)/shard_map/scatter-add | solution.py:90
  330.3 31.8 %gather_fusion.11 = f32[8192,165]{1,0:T(8,128)} fusion(f32[32,165]{1,0:T(8,128)S(1)} %broadcast_select_fusion.6, s32[8192]{0:T(1024)S(1)} %get-tuple-element.445), kind=kCustom, calls=%fused_computation.1.clone | custom fusion | bytes 10846208 | tf_op jit(solution)/shard_map/jit(_take)/gather | solution.py:88
  362.1 31.6 %fusion.78 = f32[64,128,165]{2,0,1:T(8,128)} fusion(f32[165,165,128]{1,0,2:T(8,128)} %copy.111, f32[64,128,165]{2,1,0:T(8,128)} %bitcast.447, pred[64,128]{0,1:T(8,128)(4,1)S(1)} %copy.114), kind=kOutput, calls=%fused_computation.216 | convolution fusion | flops 2677678080 | bytes 24760832 | tf_op jit(solution)/shard_map/ijc,pcj->pci/dot_general | solution.py:89
  397.0 31.5 %gather_fusion.13 = f32[8192,165]{1,0:T(8,128)} fusion(f32[32,165]{1,0:T(8,128)S(1)} %broadcast_select_fusion.5, s32[8192]{0:T(1024)S(1)} %get-tuple-element.444), kind=kCustom, calls=%fused_computation.17.clone | custom fusion | bytes 10846208 | tf_op jit(solution)/shard_map/jit(_take)/gather | solution.py:88
  428.5 31.5 %fusion.79 = f32[64,128,165]{2,0,1:T(8,128)} fusion(f32[165,165,128]{1,0,2:T(8,128)} %copy.111, f32[64,128,165]{2,1,0:T(8,128)} %bitcast.448, pred[64,128]{0,1:T(8,128)(4,1)S(1)} %copy.119), kind=kOutput, calls=%fused_computation.217 | convolution fusion | flops 2677678080 | bytes 24760832 | tf_op jit(solution)/shard_map/ijc,pcj->pci/dot_general | solution.py:89
  460.7 31.4 %gather_fusion.15 = f32[8192,165]{1,0:T(8,128)} fusion(f32[32,165]{1,0:T(8,128)S(1)} %broadcast_select_fusion.4, s32[8192]{0:T(1024)S(1)} %get-tuple-element.443), kind=kCustom, calls=%fused_computation.18.clone | custom fusion | bytes 10846208 | tf_op jit(solution)/shard_map/jit(_take)/gather | solution.py:88
  492.1 31.8 %fusion.80 = f32[64,128,165]{2,0,1:T(8,128)} fusion(f32[165,165,128]{1,0,2:T(8,128)} %copy.111, f32[64,128,165]{2,1,0:T(8,128)} %bitcast.449, pred[64,128]{0,1:T(8,128)(4,1)S(1)} %copy-done.28), kind=kOutput, calls=%fused_computation.218 | convolution fusion | flops 2677678080 | bytes 24760832 | tf_op jit(solution)/shard_map/ijc,pcj->pci/dot_general | solution.py:89
  524.7 31.4 %gather_fusion.17 = f32[8192,165]{1,0:T(8,128)} fusion(f32[32,165]{1,0:T(8,128)S(1)} %broadcast_select_fusion.3, s32[8192]{0:T(1024)S(1)} %copy-done.7), kind=kCustom, calls=%fused_computation.19.clone | custom fusion | bytes 10846208 | tf_op jit(solution)/shard_map/jit(_take)/gather | solution.py:88
  556.2 31.6 %fusion.81 = f32[64,128,165]{2,0,1:T(8,128)} fusion(f32[165,165,128]{1,0,2:T(8,128)} %copy.111, f32[64,128,165]{2,1,0:T(8,128)} %bitcast.450, pred[64,128]{0,1:T(8,128)(4,1)S(1)} %copy-done.27), kind=kOutput, calls=%fused_computation.219 | convolution fusion | flops 2677678080 | bytes 24760832 | tf_op jit(solution)/shard_map/ijc,pcj->pci/dot_general | solution.py:89
  589.5 31.6 %gather_fusion.19 = f32[8192,165]{1,0:T(8,128)} fusion(f32[32,165]{1,0:T(8,128)S(1)} %broadcast_select_fusion.2, s32[8192]{0:T(1024)S(1)} %copy-done.6), kind=kCustom, calls=%fused_computation.20.clone | custom fusion | bytes 10846208 | tf_op jit(solution)/shard_map/jit(_take)/gather | solution.py:88
  621.1 31.6 %fusion.82 = f32[64,128,165]{2,0,1:T(8,128)} fusion(f32[165,165,128]{1,0,2:T(8,128)} %copy.111, f32[64,128,165]{2,1,0:T(8,128)} %bitcast.451, pred[64,128]{0,1:T(8,128)(4,1)S(1)} %copy-done.26), kind=kOutput, calls=%fused_computation.220 | convolution fusion | flops 2677678080 | bytes 24760832 | tf_op jit(solution)/shard_map/ijc,pcj->pci/dot_general | solution.py:89
  654.5 31.4 %gather_fusion.21 = f32[8192,165]{1,0:T(8,128)} fusion(f32[32,165]{1,0:T(8,128)S(1)} %broadcast_select_fusion.1, s32[8192]{0:T(1024)S(1)} %copy-done.5), kind=kCustom, calls=%fused_computation.21.clone | custom fusion | bytes 10846208 | tf_op jit(solution)/shard_map/jit(_take)/gather | solution.py:88
  685.9 32.1 %fusion.83 = f32[64,128,165]{2,0,1:T(8,128)} fusion(f32[165,165,128]{1,0,2:T(8,128)} %copy.111, f32[64,128,165]{2,1,0:T(8,128)} %bitcast.452, pred[64,128]{0,1:T(8,128)(4,1)S(1)} %copy-done.25), kind=kOutput, calls=%fused_computation.221 | convolution fusion | flops 2677678080 | bytes 24760832 | tf_op jit(solution)/shard_map/ijc,pcj->pci/dot_general | solution.py:89
  718.0 11.7 copy.158
  729.7 11.7 copy.159
  758.0 11.9 copy.162
  779.8 31.4 %gather_fusion.23 = f32[8192,165]{1,0:T(8,128)} fusion(f32[32,165]{1,0:T(8,128)S(1)} %broadcast_select_fusion, s32[8192]{0:T(1024)S(1)} %copy-done.4), kind=kCustom, calls=%fused_computation.22.clone | custom fusion | bytes 10846208 | tf_op jit(solution)/shard_map/jit(_take)/gather | solution.py:88
  811.2 32.0 %fusion.84 = f32[64,128,165]{2,0,1:T(8,128)} fusion(f32[165,165,128]{1,0,2:T(8,128)} %copy.111, f32[64,128,165]{2,1,0:T(8,128)} %bitcast.446, pred[64,128]{0,1:T(8,128)(4,1)S(1)} %copy-done.24), kind=kOutput, calls=%fused_computation.222 | convolution fusion | flops 2677678080 | bytes 24760832 | tf_op jit(solution)/shard_map/ijc,pcj->pci/dot_general | solution.py:89
  854.8 44.8 %scatter_fusion.1 = f32[128,165]{1,0:T(8,128)S(1)} fusion(f32[128,165]{1,0:T(8,128)S(1)} %copy-done, s32[8192]{0:T(1024)S(1)} %bitcast.468, f32[8192,165]{1,0:T(8,128)} %bitcast.443), kind=kCustom, calls=%fused_computation.27 | custom fusion | flops 1351680 | bytes 16252928 | tf_op jit(solution)/shard_map/scatter-add | solution.py:90
  899.6 44.7 %scatter_fusion.2 = f32[128,165]{1,0:T(8,128)S(1)} fusion(f32[128,165]{1,0:T(8,128)S(1)} %scatter_fusion.1, s32[8192]{0:T(1024)S(1)} %bitcast.469, f32[8192,165]{1,0:T(8,128)} %bitcast.442), kind=kCustom, calls=%fused_computation.28 | custom fusion | flops 1351680 | bytes 16252928 | tf_op jit(solution)/shard_map/scatter-add | solution.py:90
  944.3 44.7 %scatter_fusion.3 = f32[128,165]{1,0:T(8,128)S(1)} fusion(f32[128,165]{1,0:T(8,128)S(1)} %scatter_fusion.2, s32[8192]{0:T(1024)S(1)} %bitcast.470, f32[8192,165]{1,0:T(8,128)} %bitcast.441), kind=kCustom, calls=%fused_computation.29 | custom fusion | flops 1351680 | bytes 16252928 | tf_op jit(solution)/shard_map/scatter-add | solution.py:90
  989.1 44.7 %scatter_fusion.4 = f32[128,165]{1,0:T(8,128)S(1)} fusion(f32[128,165]{1,0:T(8,128)S(1)} %scatter_fusion.3, s32[8192]{0:T(1024)S(1)} %bitcast.471, f32[8192,165]{1,0:T(8,128)} %bitcast.440), kind=kCustom, calls=%fused_computation.30 | custom fusion | flops 1351680 | bytes 16252928 | tf_op jit(solution)/shard_map/scatter-add | solution.py:90
  1033.8 44.7 %scatter_fusion.5 = f32[128,165]{1,0:T(8,128)S(1)} fusion(f32[128,165]{1,0:T(8,128)S(1)} %scatter_fusion.4, s32[8192]{0:T(1024)S(1)} %bitcast.472, f32[8192,165]{1,0:T(8,128)} %bitcast.439), kind=kCustom, calls=%fused_computation.31 | custom fusion | flops 1351680 | bytes 16252928 | tf_op jit(solution)/shard_map/scatter-add | solution.py:90
  1078.5 44.9 %scatter_fusion.6 = f32[128,165]{1,0:T(8,128)S(1)} fusion(f32[128,165]{1,0:T(8,128)S(1)} %scatter_fusion.5, s32[8192]{0:T(1024)S(1)} %bitcast.473, f32[8192,165]{1,0:T(8,128)} %bitcast.438), kind=kCustom, calls=%fused_computation.32 | custom fusion | flops 1351680 | bytes 16252928 | tf_op jit(solution)/shard_map/scatter-add | solution.py:90
  1123.4 44.8 %scatter_fusion.7 = f32[128,165]{1,0:T(8,128)S(1)} fusion(f32[128,165]{1,0:T(8,128)S(1)} %scatter_fusion.6, s32[8192]{0:T(1024)S(1)} %bitcast.474, f32[8192,165]{1,0:T(8,128)} %bitcast.444), kind=kCustom, calls=%fused_computation.33 | custom fusion | flops 1351680 | bytes 16252928 | tf_op jit(solution)/shard_map/scatter-add | solution.py:90
  1170.0 69.8 %while.39 = (s32[]{:T(128)}, f32[8,16,4,128]{3,2,1,0:T(4,128)S(1)}, f32[8,4,16,165]{3,2,0,1:T(8,128)}, f32[8,16,3,128]{3,1,2,0:T(8,128)}, s32[]{:T(128)}, /*inde...) while((s32[]{:T(128)}, f32[8,16,4,128]{3,2,1,0:T(4,128)S(1)}, ...), condition=%wide.region_15.18_spmd.clone.clone, body=%wide.region_14.17_spmd.sunk.clone.clone.sunk | while | flops 17409024 | bytes 15535229 | solution.py:124
  (802 shorter events, 308.1 us)
Async XLA Ops:
  3.9 70.4 %all-to-all-start.1 = ((f32[8,16,128]{2,1,0:T(8,128)}), f32[8,16,128]{2,1,0:T(8,128)S(1)}, u32[]{:S(2)}, u32[]{:S(2)}) async-start(f32[8,16,128]{2,1,0:T(8,128)} %bitcast.19), calls=%async_computation.1 | async-start | bytes 131072 | tf_op jit(solution)/shard_map/all_to_all | solution.py:169
  10.0 55.4 %collective-permute-start.1 = (f32[32]{0:T(128)S(1)}, f32[32]{0:T(128)S(1)}, u32[]{:S(2)}, u32[]{:S(2)}) collective-permute-start(f32[32]{0:T(128)S(1)} %get-tuple-element.452), channel_id=1, source_target_pairs={{0,1},{1,0},{2,3},{3,2},{4,5},{5,4},{6,7},{7,6},{8,9},{9,8},{10,11... | collective-permute-start | bytes 392 | tf_op jit(solution)/shard_map/ppermute | solution.py:15
  10.6 56.4 %collective-permute-start.3 = (f32[32]{0:T(128)S(1)}, f32[32]{0:T(128)S(1)}, u32[]{:S(2)}, u32[]{:S(2)}) collective-permute-start(f32[32]{0:T(128)S(1)} %get-tuple-element.451), channel_id=1, source_target_pairs={{0,2},{1,3},{2,0},{3,1},{4,6},{5,7},{6,4},{7,5},{8,10},{9,11},{10,... | collective-permute-start | bytes 392 | tf_op jit(solution)/shard_map/ppermute | solution.py:15
  12.3 57.8 %collective-permute-start.5 = (f32[32]{0:T(128)S(1)}, f32[32]{0:T(128)S(1)}, u32[]{:S(2)}, u32[]{:S(2)}) collective-permute-start(f32[32]{0:T(128)S(1)} %get-tuple-element.450), channel_id=1, source_target_pairs={{0,4},{1,5},{2,6},{3,7},{4,0},{5,1},{6,2},{7,3},{8,12},{9,13},{10,... | collective-permute-start | bytes 392 | tf_op jit(solution)/shard_map/ppermute | solution.py:15
  14.9 55.2 %collective-permute-start.7 = (f32[32]{0:T(128)S(1)}, f32[32]{0:T(128)S(1)}, u32[]{:S(2)}, u32[]{:S(2)}) collective-permute-start(f32[32]{0:T(128)S(1)} %get-tuple-element.449), channel_id=1, source_target_pairs={{0,8},{1,9},{2,10},{3,11},{4,12},{5,13},{6,14},{7,15},{8,0},{9,1},... | collective-permute-start | bytes 392 | tf_op jit(solution)/shard_map/ppermute | solution.py:15
  16.4 54.2 %collective-permute-start.9 = (f32[32]{0:T(128)S(1)}, f32[32]{0:T(128)S(1)}, u32[]{:S(2)}, u32[]{:S(2)}) collective-permute-start(f32[32]{0:T(128)S(1)} %get-tuple-element.448), channel_id=1, source_target_pairs={{0,16},{1,17},{2,18},{3,19},{4,20},{5,21},{6,22},{7,23},{8,24},{9,... | collective-permute-start | bytes 392 | tf_op jit(solution)/shard_map/ppermute | solution.py:15
  24.2 61.7 %copy-start.15 = (f32[165]{0:T(256)S(1)}, f32[165]{0:T(256)}, u32[]{:S(2)}) copy-start(f32[165]{0:T(256)} %constant.192.clone..sunk.6) | copy-start | bytes 1984
  24.2 61.7 %copy-start.17 = (s32[165]{0:T(256)S(1)}, s32[165]{0:T(256)}, u32[]{:S(2)}) copy-start(s32[165]{0:T(256)} %constant.705) | copy-start | bytes 1984
  24.2 61.6 %copy-start.19 = (s32[165]{0:T(256)S(1)}, s32[165]{0:T(256)}, u32[]{:S(2)}) copy-start(s32[165]{0:T(256)} %constant.706) | copy-start | bytes 1984
  24.2 61.6 %copy-start.21 = (s32[165]{0:T(256)S(1)}, s32[165]{0:T(256)}, u32[]{:S(2)}) copy-start(s32[165]{0:T(256)} %constant.707) | copy-start | bytes 1984
  65.4 6.4 collective-permute-start.11
  67.0 6.0 collective-permute-start.13
  74.3 10.9 all-to-all-start
  161.0 168.5 %collective-permute-start = (f32[128,165]{1,0:T(8,128)}, f32[128,165]{1,0:T(8,128)S(1)}, u32[]{:S(2)}, u32[]{:S(2)}) collective-permute-start(f32[128,165]{1,0:T(8,128)} %bitcast.20), channel_id=1, source_target_pairs={{0,1},{1,0},{2,3},{3,2},{4,5},{5,4},{6,7},{7,6},{8,9},{9,8},{10,11... | collective-permute-start | bytes 253448 | tf_op jit(solution)/shard_map/ppermute | solution.py:15
  161.0 232.7 %collective-permute-start.2 = (f32[128,165]{1,0:T(8,128)}, f32[128,165]{1,0:T(8,128)S(1)}, u32[]{:S(2)}, u32[]{:S(2)}) collective-permute-start(f32[128,165]{1,0:T(8,128)} %bitcast.20), channel_id=1, source_target_pairs={{0,2},{1,3},{2,0},{3,1},{4,6},{5,7},{6,4},{7,5},{8,10},{9,11},{10,... | collective-permute-start | bytes 253448 | tf_op jit(solution)/shard_map/ppermute | solution.py:15
  161.6 298.4 %collective-permute-start.4 = (f32[128,165]{1,0:T(8,128)}, f32[128,165]{1,0:T(8,128)S(1)}, u32[]{:S(2)}, u32[]{:S(2)}) collective-permute-start(f32[128,165]{1,0:T(8,128)} %bitcast.20), channel_id=1, source_target_pairs={{0,4},{1,5},{2,6},{3,7},{4,0},{5,1},{6,2},{7,3},{8,12},{9,13},{10,... | collective-permute-start | bytes 253448 | tf_op jit(solution)/shard_map/ppermute | solution.py:15
  163.6 360.3 %collective-permute-start.6 = (f32[128,165]{1,0:T(8,128)}, f32[128,165]{1,0:T(8,128)S(1)}, u32[]{:S(2)}, u32[]{:S(2)}) collective-permute-start(f32[128,165]{1,0:T(8,128)} %bitcast.20), channel_id=1, source_target_pairs={{0,8},{1,9},{2,10},{3,11},{4,12},{5,13},{6,14},{7,15},{8,0},{9,1},... | collective-permute-start | bytes 253448 | tf_op jit(solution)/shard_map/ppermute | solution.py:15
  163.8 424.0 %collective-permute-start.8 = (f32[128,165]{1,0:T(8,128)}, f32[128,165]{1,0:T(8,128)}, u32[]{:S(2)}, u32[]{:S(2)}) collective-permute-start(f32[128,165]{1,0:T(8,128)} %bitcast.20), channel_id=1, source_target_pairs={{0,16},{1,17},{2,18},{3,19},{4,20},{5,21},{6,22},{7,23},{8,24},{9,... | collective-permute-start | bytes 253448 | tf_op jit(solution)/shard_map/ppermute | solution.py:15
  329.5 323.3 %collective-permute-start.10 = (f32[128,165]{1,0:T(8,128)}, f32[128,165]{1,0:T(8,128)}, u32[]{:S(2)}, u32[]{:S(2)}) collective-permute-start(f32[128,165]{1,0:T(8,128)} %bitcast.20), channel_id=1, source_target_pairs={{0,32},{1,33},{2,34},{3,35},{4,36},{5,37},{6,38},{7,39},{8,40},{9,... | collective-permute-start | bytes 253448 | tf_op jit(solution)/shard_map/ppermute | solution.py:15
  393.7 384.4 %collective-permute-start.12 = (f32[128,165]{1,0:T(8,128)}, f32[128,165]{1,0:T(8,128)}, u32[]{:S(2)}, u32[]{:S(2)}) collective-permute-start(f32[128,165]{1,0:T(8,128)} %bitcast.20), channel_id=1, source_target_pairs={{0,64},{1,65},{2,66},{3,67},{4,68},{5,69},{6,70},{7,71},{8,72},{9,... | collective-permute-start | bytes 253448 | tf_op jit(solution)/shard_map/ppermute | solution.py:15
  854.8 44.9 %copy-start.9 = (s32[8192,1]{0,1:T(1,128)S(1)}, s32[8192,1]{0,1:T(1,128)}, u32[]{:S(2)}) copy-start(s32[8192,1]{0,1:T(1,128)} %compare_select_fusion.7) | copy-start | bytes 98308
  899.6 44.7 %copy-start.10 = (s32[8192,1]{0,1:T(1,128)S(1)}, s32[8192,1]{0,1:T(1,128)}, u32[]{:S(2)}) copy-start(s32[8192,1]{0,1:T(1,128)} %compare_select_fusion.6) | copy-start | bytes 98308
  944.3 44.7 %copy-start.11 = (s32[8192,1]{0,1:T(1,128)S(1)}, s32[8192,1]{0,1:T(1,128)}, u32[]{:S(2)}) copy-start(s32[8192,1]{0,1:T(1,128)} %compare_select_fusion.5) | copy-start | bytes 98308
  1078.5 44.9 %copy-start.14 = (s32[8192,1]{0,1:T(1,128)S(1)}, s32[8192,1]{0,1:T(1,128)}, u32[]{:S(2)}) copy-start(s32[8192,1]{0,1:T(1,128)} %compare_select_fusion.2) | copy-start | bytes 98308
  1123.4 44.8 %copy-start.3 = (f32[3,165,165]{2,1,0:T(8,128)S(1)}, f32[3,165,165]{2,1,0:T(8,128)}, u32[]{:S(2)}) copy-start(f32[3,165,165]{2,1,0:T(8,128)} %constant.193.clone) | copy-start | bytes 980104
  1123.4 46.5 %copy-start.16 = (f32[165]{0:T(256)S(1)}, f32[165]{0:T(256)}, u32[]{:S(2)}) copy-start(f32[165]{0:T(256)} %constant.192.clone..sunk.6) | copy-start | bytes 1984
  1123.4 46.5 %copy-start.18 = (s32[165]{0:T(256)S(1)}, s32[165]{0:T(256)}, u32[]{:S(2)}) copy-start(s32[165]{0:T(256)} %constant.705) | copy-start | bytes 1984
  1123.4 46.5 %copy-start.20 = (s32[165]{0:T(256)S(1)}, s32[165]{0:T(256)}, u32[]{:S(2)}) copy-start(s32[165]{0:T(256)} %constant.706) | copy-start | bytes 1984
  1123.4 46.5 %copy-start.22 = (s32[165]{0:T(256)S(1)}, s32[165]{0:T(256)}, u32[]{:S(2)}) copy-start(s32[165]{0:T(256)} %constant.707) | copy-start | bytes 1984
  1169.9 69.9 %copy-start.2 = (f32[8,16,4,128]{3,2,1,0:T(4,128)S(1)}, f32[8,16,4,128]{3,2,1,0:T(4,128)}, u32[]{:S(2)}) copy-start(f32[8,16,4,128]{3,2,1,0:T(4,128)} %copy-done.1) | copy-start | bytes 786436
  1170.0 69.9 %copy-start.34 = (s32[128]{0:T(128)S(1)}, s32[128]{0:T(128)}, u32[]{:S(2)}) copy-start(s32[128]{0:T(128)} %fusion.95) | copy-start | bytes 1540
  1170.0 74.8 %copy-start.29 = (f32[128]{0:T(128)S(1)}, f32[128]{0:T(128)}, u32[]{:S(2)}) copy-start(f32[128]{0:T(128)} %convert_reduce_fusion) | copy-start | bytes 1540
  (28 other events, 732.2 us)
where the time goes:
time: 1260 us; the launch traced here: 1250 us
  local copies, waits for them, and re-layouts  477 us (38%)
  other arithmetic  442 us (35%)
  matrix products  287 us (23%)
  starting transfers between devices  29.9 us (2%)
    scatter-add x8, other arithmetic, translate(): expansion.at[targets.reshape(-1)]  358 us
    dot_general x8, matrix products, translate(): jnp.einsum('ijc,pcj->pci', operators, gathered, precision=highest)  254 us
    gather x8, local copies, waits for them, and re-layouts, translate(): gathered = jnp.take(sources, rows, axis=0)  253 us
    reshape x8, local copies, waits for them, and re-layouts, translate(): translated.reshape(-1, translated.shape[2])  83.1 us
    gather x16, local copies, waits for them, and re-layouts, basis_values(): tables[1][exponents[:, 1]]  30.8 us
    mul x16, other arithmetic, basis_values(): return result * jnp.asarray(term_norms).reshape(-1, 1, 1)  26.6 us
  transfers between devices with their start and end apart: 16, of which 1 were waited for; matrix products, arithmetic and copies ran while one was open for 53% of the time, Pallas kernels for 0%

commit v1 on v0

v1 whole, which is shorter than its diff:
```python
import functools

import jax
import jax.numpy as jnp
import numpy as np
from jax import lax
from jax.experimental import pallas as pl
from jax.experimental.pallas import tpu as pltpu
from jax.sharding import PartitionSpec as P

ORDER = 8
TERMS = 165
ROWS = 168
SOFT = 0.01
SLOTS = 128
BODIES = 128
KEXP = 32
LEVELS = 7
CLASSES = 128
SOURCES = SLOTS + LEVELS * KEXP
f32 = jnp.float32
bf16 = jnp.bfloat16
VMEM = pltpu.VMEM
SMEM = pltpu.SMEM


def term_list():
    triples = []
    for degree in range(ORDER + 1):
        for a in range(degree, -1, -1):
            for b in range(degree - a, -1, -1):
                triples.append((a, b, degree - a - b))
    return {t: n for n, t in enumerate(triples)}


TERM = term_list()
NORM = {t: float(np.float32(np.sqrt(np.prod(2.0 * np.array(t) + 1.0)))) for t in TERM}


def iota(shape, axis):
    return lax.broadcasted_iota(jnp.int32, shape, axis)


def dot(a, b):
    return jnp.dot(a, b, preferred_element_type=f32)


def dot_nt(a, b):
    return lax.dot_general(a, b, (((1,), (1,)), ((), ())), preferred_element_type=f32)


def dot_exact(a, b):
    return jnp.dot(a, b, preferred_element_type=f32, precision=lax.Precision.HIGHEST)


def pack_kernel(owner_ref, pos_ref, mass_ref, out_ref, count_ref, *slot_refs):
    for r in slot_refs:
        r[...] = jnp.zeros_like(r)
    for o in range(8):
        count_ref[o] = 0

    def step(i, carry):
        o = owner_ref[i, 0]
        rank = count_ref[o]
        count_ref[o] = rank + 1
        slot = o * 16 + rank
        tile = pos_ref[i]
        for a in range(3):
            slot_refs[a][pl.ds(slot, 1), :] = tile[a : a + 1, :]
        slot_refs[3][pl.ds(slot, 1), :] = mass_ref[pl.ds(i, 1), :]
        return carry

    lax.fori_loop(0, pos_ref.shape[0], step, 0)
    for a in range(4):
        out_ref[:, a * BODIES : (a + 1) * BODIES] = slot_refs[a][...]


def pack_tiles(owner, positions, masses):
    return pl.pallas_call(
        pack_kernel,
        out_shape=jax.ShapeDtypeStruct((SLOTS, 4 * BODIES), f32),
        in_specs=[
            pl.BlockSpec(memory_space=SMEM),
            pl.BlockSpec(memory_space=VMEM),
            pl.BlockSpec(memory_space=VMEM),
        ],
        out_specs=pl.BlockSpec(memory_space=VMEM),
        scratch_shapes=[pltpu.SMEM((8,), jnp.int32)] + [pltpu.VMEM((SLOTS, BODIES), f32)] * 4,
        name="pack",
    )(owner, positions, masses)


A_STEP = 8


def count_kernel(tgt_ref, far_ref, local_ref, out_ref, tt_ref, st_ref):
    step = pl.program_id(0)

    @pl.when(step == 0)
    def _():
        order = [7, 0, 1, 2, 3, 4, 5, 6]
        for pair in range(4):
            tgt, src = [], []
            for level in order[2 * pair : 2 * pair + 2]:
                tgt.append(tgt_ref[level].astype(f32))
                if level == 7:
                    src.append(local_ref[...].astype(f32))
                else:
                    offset = SLOTS + KEXP * level if level < 3 else KEXP * (level - 3)
                    src.append((far_ref[level] + offset).astype(f32))
            lanes = slice(pair * 128, pair * 128 + 128)
            tt_ref[:, lanes] = jnp.concatenate(tgt, axis=0).T
            st_ref[:, lanes] = jnp.concatenate(src, axis=0).T

    rows = pl.ds(pl.multiple_of(step * A_STEP, A_STEP), A_STEP)
    tt = tt_ref[rows, :]
    st = st_ref[rows, :]

    def onehot(row, size):
        ids = iota((size, 256), 0).astype(f32)
        return jnp.where(row == ids, 1.0, 0.0).astype(bf16)

    for k in range(A_STEP):
        for half, (first, size) in enumerate(((0, 224), (224, 128))):
            lanes = slice(half * 256, half * 256 + 256)
            target = onehot(tt[k : k + 1, lanes], 128)
            source = onehot(st[k : k + 1, lanes], size)
            counts = dot_nt(source, target)
            out_ref[k // 2, first : first + size, (k % 2) * 128 : (k % 2) * 128 + 128] = counts.astype(bf16)


def count_pairs(m2l_target, far_source, local_source):
    whole = lambda *shape: pl.BlockSpec(shape, lambda g: (0,) * len(shape))
    return pl.pallas_call(
        count_kernel,
        grid=(CLASSES // A_STEP,),
        out_shape=jax.ShapeDtypeStruct((CLASSES // 2, SOURCES, 256), bf16),
        in_specs=[whole(8, 64, 128), whole(7, 64, 128), whole(64, 128)],
        out_specs=pl.BlockSpec((A_STEP // 2, SOURCES, 256), lambda g: (g, 0, 0)),
        scratch_shapes=[pltpu.VMEM((128, 512), f32), pltpu.VMEM((128, 512), f32)],
        cost_estimate=pl.CostEstimate(flops=12 * 10**9, bytes_accessed=13 * 10**6, transcendentals=0),
        name="counts",
    )(m2l_target, far_source, local_source)


def multipole_kernel(recv_ref, slots_ref, mt_ref, post_ref, *rest):
    exp_refs, (acc_ref, m_ref, rows_ref) = rest[:LEVELS], rest[LEVELS:]
    for a in range(4):
        post_ref[a] = recv_ref[:, a * BODIES : (a + 1) * BODIES].T

    acc_ref[...] = jnp.zeros_like(acc_ref)

    def chunk(q, carry):
        rows = pl.ds(pl.multiple_of(q * 32, 32), 32)
        x, y, z, m = (post_ref[a, rows, :] for a in range(4))

        def fold(term, n):
            part = (term[0:8] + term[8:16]) + (term[16:24] + term[24:32])
            acc_ref[n] += part

        px = m
        for a in range(ORDER + 1):
            py = px
            for b in range(ORDER + 1 - a):
                pz = py
                for c in range(ORDER + 1 - a - b):
                    fold(pz, TERM[a, b, c])
                    if c < ORDER - a - b:
                        pz = pz * z
                if b < ORDER - a:
                    py = py * y
            if a < ORDER:
                px = px * x
        return carry

    lax.fori_loop(0, BODIES // 32, chunk, 0)
    mt_ref[TERMS - 5 :, :] = jnp.zeros((ROWS - TERMS + 5, SLOTS), f32)
    for (a, b, c), n in TERM.items():
        mt_ref[n : n + 1, :] = jnp.sum(acc_ref[n], axis=0, keepdims=True) * NORM[a, b, c]
    m_ref[0] = mt_ref[0:128, :].T
    m_ref[1] = jnp.concatenate([mt_ref[128:ROWS, :], jnp.zeros((256 - ROWS, SLOTS), f32)], axis=0).T
    for level in range(LEVELS):

        def row(k, carry):
            slot = slots_ref[level, k]
            for half in range(2):
                rows_ref[half, pl.ds(k, 1), :] = m_ref[half, pl.ds(slot, 1), :]
            return carry

        lax.fori_loop(0, KEXP, row, 0, unroll=8)
        for half in range(2):
            exp_refs[level][:, half * 128 : half * 128 + 128] = rows_ref[half]


def multipoles_of(recv, export_slots):
    vm = pl.BlockSpec(memory_space=VMEM)
    out = pl.pallas_call(
        multipole_kernel,
        out_shape=[
            jax.ShapeDtypeStruct((ROWS, SLOTS), f32),
            jax.ShapeDtypeStruct((4, BODIES, SLOTS), f32),
        ]
        + [jax.ShapeDtypeStruct((KEXP, 256), f32)] * LEVELS,
        in_specs=[vm, pl.BlockSpec(memory_space=SMEM)],
        out_specs=[vm] * (2 + LEVELS),
        scratch_shapes=[
            pltpu.VMEM((TERMS, 8, SLOTS), f32),
            pltpu.VMEM((2, SLOTS, 128), f32),
            pltpu.VMEM((2, KEXP, 128), f32),
        ],
        name="multipoles",
    )(recv, export_slots)
    return out[0], out[1], out[2:]


def near_kernel(recv_ref, tgt_ref, src_ref, off_ref, near_ref, s_ref, t_ref, a_ref):
    def column(ref):
        return jnp.broadcast_to(ref[...].astype(f32), (128, 128)).T

    lane = iota((128, 128), 1).astype(f32)
    pick_s = jnp.where(column(src_ref) == lane, 1.0, 0.0)
    pick_t = jnp.where(column(tgt_ref) == lane, 1.0, 0.0)
    s_ref[...] = dot_exact(pick_s, recv_ref[...])
    t_ref[...] = dot_exact(pick_t, recv_ref[:, 0:384])
    k = column(off_ref)
    one = jnp.ones_like(k)
    kx = jnp.where(k >= 9.0, one, 0.0) + jnp.where(k >= 18.0, one, 0.0)
    k = k - 9.0 * kx
    ky = jnp.where(k >= 3.0, one, 0.0) + jnp.where(k >= 6.0, one, 0.0)
    kz = k - 3.0 * ky
    for a, shift in enumerate((kx, ky, kz)):
        lanes = slice(a * 128, a * 128 + 128)
        s_ref[:, lanes] = s_ref[:, lanes] + 2.0 * (shift - 1.0)

    def group(g, carry):
        rows = pl.ds(pl.multiple_of(g * 32, 32), 32)
        tx, ty, tz = (t_ref[rows, a * 128 : a * 128 + 128] for a in range(3))

        def turn(i, state):
            sx, sy, sz, m, p, ax, ay, az = state
            rx, ry, rz = sx - tx, sy - ty, sz - tz
            inv = lax.rsqrt(rx * rx + ry * ry + rz * rz + SOFT)
            w = m * inv
            p = p - w
            w = w * inv * inv
            ax, ay, az = ax + rx * w, ay + ry * w, az + rz * w
            sx, sy, sz, m = (pltpu.roll(v, 1, 1) for v in (sx, sy, sz, m))
            return sx, sy, sz, m, p, ax, ay, az

        zero = jnp.zeros((32, 128), f32)
        start = tuple(s_ref[rows, a * 128 : a * 128 + 128] for a in range(4)) + (zero,) * 4
        done = lax.fori_loop(0, 128, turn, start, unroll=4)
        for a in range(4):
            a_ref[rows, a * 128 : a * 128 + 128] = done[4 + a]
        return carry

    lax.fori_loop(0, 4, group, 0)
    into = jnp.where(tgt_ref[...] == iota((128, 128), 0), 1.0, 0.0)
    near_ref[...] = dot_exact(into, a_ref[...])


def near_field(recv, target, source, offset):
    vm = pl.BlockSpec(memory_space=VMEM)
    return pl.pallas_call(
        near_kernel,
        out_shape=jax.ShapeDtypeStruct((SLOTS, 4 * BODIES), f32),
        in_specs=[vm] * 4,
        out_specs=vm,
        scratch_shapes=[
            pltpu.VMEM((128, 512), f32),
            pltpu.VMEM((128, 384), f32),
            pltpu.VMEM((128, 512), f32),
        ],
        cost_estimate=pl.CostEstimate(flops=8 * 10**9, bytes_accessed=10**6, transcendentals=2 * 10**6),
        name="near",
    )(recv, target, source, offset)


C_STEP = 4
PHASE1 = CLASSES // 2 // C_STEP
J_STEP = 8
PHASE2 = (TERMS + J_STEP - 1) // J_STEP


def split(v):
    high = v.astype(bf16)
    return high, (v - high.astype(f32)).astype(bf16)


def field_kernel(counts_ref, op_ref, mt_ref, *rest):
    far_refs, rest = rest[:LEVELS], rest[LEVELS:]
    post_ref, near_ref, recv_ref, out_ref, src_ref, bt_ref, acc_ref, e_ref, f_ref = rest
    step = pl.program_id(0)

    @pl.when(step == 0)
    def _():
        far = jnp.concatenate([r[...] for r in far_refs], axis=0)
        far = jnp.concatenate([far, jnp.zeros((32, 256), f32)], axis=0)
        own = mt_ref[...]
        parts = [own]
        for q in range(2):
            block = far[q * 128 : q * 128 + 128, :]
            parts.append(jnp.concatenate([block[:, 0:128].T, block[:, 128:256].T[0 : ROWS - 128]], axis=0))
        sources = jnp.concatenate(parts, axis=1)
        high = sources.astype(bf16).astype(f32)
        both = jnp.concatenate([high, sources - high], axis=0).astype(bf16)
        src_ref[...] = both[:, 0:SOURCES]

    @pl.when(step < PHASE1)
    def _():
        for q in range(C_STEP):
            moved = dot(src_ref[...], counts_ref[q])
            moved = moved[0:ROWS] + moved[ROWS : 2 * ROWS]
            for k in range(2):
                c = (step * C_STEP + q) * 2 + k
                bt_ref[pl.ds(c, ROWS, stride=CLASSES), :] = moved[:, k * 128 : k * 128 + 128]

    @pl.when(step >= PHASE1)
    def _():
        jb = step - PHASE1
        ops = op_ref.reshape(ROWS * J_STEP, CLASSES)
        left, right = [], []
        for j in range(J_STEP):
            o = ops[pl.ds(j, ROWS, stride=J_STEP), :]
            o = jnp.where(jb * J_STEP + j < TERMS, o, 0.0)
            high = o.astype(bf16).astype(f32)
            left.append(jnp.concatenate([high, o - high], axis=0).astype(bf16))
            b = bt_ref[pl.ds(pl.multiple_of((jb * J_STEP + j) * CLASSES, CLASSES), CLASSES), :]
            right.append(jnp.concatenate(split(b), axis=1))
        total = dot(jnp.concatenate(left, axis=1), jnp.concatenate(right, axis=0))

        @pl.when(jb == 0)
        def _():
            acc_ref[...] = total

        @pl.when(jb > 0)
        def _():
            acc_ref[...] += total

    @pl.when(step == PHASE1 + PHASE2 - 1)
    def _():
        acc = acc_ref[...]
        e_ref[...] = (acc[ROWS:, 128:] + acc[ROWS:, :128]) + acc[:ROWS, 128:] + acc[:ROWS, :128]

        def chunk(q, carry):
            rows = pl.ds(pl.multiple_of(q * 32, 32), 32)
            x, y, z = (post_ref[a, rows, :] for a in range(3))

            def coef(a, b, c):
                n = TERM[a, b, c]
                return jnp.broadcast_to(e_ref[n : n + 1, :] * NORM[a, b, c], (32, SLOTS))

            p = px = py = pz = None
            for a in range(ORDER, -1, -1):
                r = ry = rz = None
                for b in range(ORDER - a, -1, -1):
                    top = ORDER - a - b
                    v = coef(a, b, top)
                    vz = None
                    for c in range(top - 1, -1, -1):
                        vz = v if vz is None else vz * z + v
                        v = v * z + coef(a, b, c)
                    if r is None:
                        r = v
                    else:
                        ry = r if ry is None else ry * y + r
                        r = r * y + v
                        if vz is not None:
                            rz = vz if rz is None else rz * y + vz
                if p is None:
                    p = r
                else:
                    px = p if px is None else px * x + p
                    p = p * x + r
                    py = ry if py is None else py * x + ry
                    pz = rz if pz is None else pz * x + rz
            f_ref[0, rows, :] = p
            f_ref[1, rows, :] = -px
            f_ref[2, rows, :] = -py
            f_ref[3, rows, :] = -pz
            return carry

        lax.fori_loop(0, BODIES // 32, chunk, 0)
        present = recv_ref[:, 3 * BODIES : 3 * BODIES + 1] > 0.0
        present = jnp.where(present, jnp.ones((SLOTS, BODIES), f32), 0.0)
        for a in range(4):
            out_ref[:, a, :] = (f_ref[a].T + near_ref[:, a * BODIES : (a + 1) * BODIES]) * present


def field(counts, operators, mt, far, post, near, recv):
    whole = lambda *shape: pl.BlockSpec(shape, lambda g: (0,) * len(shape))
    return pl.pallas_call(
        field_kernel,
        grid=(PHASE1 + PHASE2,),
        out_shape=jax.ShapeDtypeStruct((SLOTS, 4, BODIES), f32),
        in_specs=[
            pl.BlockSpec((C_STEP, SOURCES, 256), lambda g: (jnp.minimum(g, PHASE1 - 1), 0, 0)),
            pl.BlockSpec((ROWS, J_STEP, CLASSES), lambda g: (0, jnp.maximum(g - PHASE1, 0), 0)),
            whole(ROWS, SLOTS),
        ]
        + [whole(KEXP, 256)] * LEVELS
        + [whole(4, BODIES, SLOTS), whole(SLOTS, 4 * BODIES), whole(SLOTS, 4 * BODIES)],
        out_specs=whole(SLOTS, 4, BODIES),
        scratch_shapes=[
            pltpu.VMEM((2 * ROWS, SOURCES), bf16),
            pltpu.VMEM((ROWS * CLASSES, SLOTS), f32),
            pltpu.VMEM((2 * ROWS, 256), f32),
            pltpu.VMEM((ROWS, SLOTS), f32),
            pltpu.VMEM((4, BODIES, SLOTS), f32),
        ],
        compiler_params=pltpu.CompilerParams(vmem_limit_bytes=48 * 2**20),
        cost_estimate=pl.CostEstimate(flops=40 * 10**9, bytes_accessed=26 * 10**6, transcendentals=0),
        name="field",
    )(counts, operators, mt, *far, post, near, recv)


def body(
    positions,
    masses,
    owner,
    operators,
    m2l_target,
    far_source,
    local_source,
    export_slots,
    near_target,
    near_source,
    near_offset,
):
    axes = ("dom", "sub")
    devices = lax.axis_size(axes)
    sent = pack_tiles(owner, positions, masses)
    recv = lax.all_to_all(sent, "sub", split_axis=0, concat_axis=0, tiled=True)
    counts = count_pairs(m2l_target[0], far_source[0], local_source[0])
    mt, post, exported = multipoles_of(recv, export_slots[0])
    far = [
        lax.ppermute(rows, axes, [(i, i ^ (1 << level)) for i in range(devices)])
        for level, rows in enumerate(exported)
    ]
    near = near_field(recv, near_target, near_source, near_offset)
    return field(counts, operators, mt, far, post, near, recv)


def solution(mesh):
    both = ("dom", "sub")
    in_specs = (
        P(both, None, None),
        P(both, None),
        P(both, None),
        P(),
        P(both, None, None, None),
        P(both, None, None, None),
        P(both, None, None),
        P(both, None, None),
        P(both, None),
        P(both, None),
        P(both, None),
    )
    out_specs = P(both, None, None)
    return jax.shard_map(body, mesh=mesh, in_specs=in_specs, out_specs=out_specs, check_vma=False)
```

time: 1260 us -> 126 us (0.10); the launches traced: 1250 us -> 125 us
  local copies, waits for them, and re-layouts: 477 us -> 5.91 us
  other arithmetic: 442 us -> 0 us
  matrix products: 287 us -> 0 us
  Pallas kernels: 0 us -> 96.2 us
  starting transfers between devices: 29.9 us -> 16.9 us
    scatter-add x9 -> x0, other arithmetic: 363 us -> none  [the longest x8 358 us: translate(): expansion.at[targets.reshape(-1)]]
    gather x87 -> x0, local copies, waits for them, and re-layouts: 332 us -> none  [the longest x8 253 us: translate(): gathered = jnp.take(sources, rows, axis=0)]
    dot_general x25 -> x0, matrix products: 287 us -> none  [the longest x8 254 us: translate(): jnp.einsum('ijc,pcj->pci', operators, gathered, precision=highest)]
    pallas_call x0 -> x5, Pallas kernels: none -> 96.2 us  [the longest x1 39.5 us: near_field(): pl.pallas_call(near_kernel, out_shape=jax.ShapeDtypeStruct((SLOTS, 4 * BO...]
    reshape x8 -> x0, local copies, waits for them, and re-layouts: 83.1 us -> none  [translate(): translated.reshape(-1, translated.shape[2])]
    mul x26 -> x0, other arithmetic: 28.3 us -> none  [the longest x16 26.6 us: basis_values(): return result * jnp.asarray(term_norms).reshape(-1, 1, 1)]
    reduce_sum x25 -> x0, other arithmetic: 26.9 us -> none  [the longest x8 14.9 us: near_block(): pull_terms = jnp.sum(separation * cubed_inv[:, None], axis=3)]
    unnamed x92 -> x23, local copies, waits for them, and re-layouts: 23.2 us -> 5.91 us
  transfers between devices with their start and end apart: 16 -> 8, of which waited for: 1 -> 1; matrix products, arithmetic and copies ran while one was open for 53% -> 1% of each run, Pallas kernels for 0% -> 42%
where the time goes in v1:
time: 126 us; the launch traced here: 125 us
  Pallas kernels  96.2 us (76%)
  starting transfers between devices  16.9 us (13%)
  waiting for transfers between devices  6.28 us (5%)
  local copies, waits for them, and re-layouts  5.91 us (5%)
    pallas_call x1, Pallas kernels, near_field(): pl.pallas_call(near_kernel, out_shape=jax.ShapeDtypeStruct((SLOTS, 4 * BO...  39.5 us
    pallas_call x1, Pallas kernels, field(): pl.pallas_call(field_kernel, grid=(PHASE1 + PHASE2,), out_shape=jax.Shape...  37.4 us
    pallas_call x1, Pallas kernels, count_pairs(): pl.pallas_call(count_kernel, grid=(CLASSES // A_STEP,), out_shape=jax.Sha...  13.3 us
    ppermute x7, starting transfers between devices, body(): lax.ppermute(rows, axes, [(i, i ^ 1 << level) for i in range(devices)])  11.5 us
    all_to_all x1, waiting for transfers between devices, body(): recv = lax.all_to_all(sent, 'sub', split_axis=0, concat_axis=0, tiled=True)  6.26 us
    unnamed x23, local copies, waits for them, and re-layouts  5.91 us
    all_to_all x1, starting transfers between devices, body(): recv = lax.all_to_all(sent, 'sub', split_axis=0, concat_axis=0, tiled=True)  5.4 us
    pallas_call x1, Pallas kernels, multipoles_of(): pl.pallas_call(multipole_kernel, out_shape=[jax.ShapeDtypeStruct((ROWS, S...  3.51 us
  transfers between devices with their start and end apart: 8, of which 1 were waited for; matrix products, arithmetic and copies ran while one was open for 1% of the time, Pallas kernels for 42%

profile of v1, /device:TPU:0, one launch (start us, length us, event | category | flops | bytes accessed | tf_op | source)
XLA Modules:
  0.0 125.4 jit_solution(14826154657641512859)
XLA Ops:
  0.0 1.3 %copy.12.owner_ref = s32[64,1]{1,0:T(8,128)} copy(s32[64,1]{0,1:T(1,128)} %param.13) | data formatting | bytes 512 | tf_op args[2]
  1.3 1.6 %copy.13.pos_ref = f32[64,3,128]{2,1,0:T(4,128)} copy(f32[64,3,128]{2,0,1:T(8,128)} %param.11) | data formatting | bytes 196608 | tf_op args[0]
  3.0 2.6 %pack.1 = f32[128,512]{1,0:T(8,128)} custom-call(s32[64,1]{1,0:T(8,128)} %copy.12.owner_ref, f32[64,3,128]{2,1,0:T(4,128)} %copy.13.pos_ref, f32[64,128]{1,0:T(8,128)} %mass_ref.1), custom_call_target="tpu_custom_call" | custom-call | tf_op jit(solution)/shard_map/pack/pallas_call | solution.py:79
  5.5 5.4 %all-to-all-start = ((f32[8,16,512]{2,1,0:T(8,128)}), f32[8,16,512]{2,1,0:T(8,128)S(1)}, u32[]{:S(2)}, u32[]{:S(2)}) async-start(f32[8,16,512]{2,1,0:T(8,128)} %bitcast.11), calls=%async_computation | async-start | bytes 524288 | tf_op jit(solution)/shard_map/all_to_all | solution.py:433
  10.9 1.3 %copy.16 = s32[1,7,32]{2,1,0:T(8,128)} copy(s32[1,7,32]{2,0,1:T(1,128)} %param.18) | data formatting | bytes 1792
  12.2 6.3 %all-to-all-done = f32[8,16,512]{2,1,0:T(8,128)S(1)} async-done(((f32[8,16,512]{2,1,0:T(8,128)}), f32[8,16,512]{2,1,0:T(8,128)S(1)}, u32[]{:S(2)}, u32[]{:S(2)}) %all-to-all-start) | async-done | bytes 262176 | tf_op jit(solution)/shard_map/all_to_all | solution.py:433
  18.5 0.7 copy-done
  19.2 3.5 %multipoles.1 = (f32[168,128]{1,0:T(8,128)}, f32[4,128,128]{2,1,0:T(8,128)}, f32[32,256]{1,0:T(8,128)}, f32[32,256]{1,0:T(8,128)}, f32[32,256]{1,0:T(8,128)}, /*...) custom-call(f32[128,512]{1,0:T(8,128)} %bitcast.8, s32[7,32]{1,0:T(8,128)} %bitcast.12), custom_call_target="tpu_custom_call" | custom-call | tf_op jit(solution)/shard_map/multipoles/pallas_call | solution.py:197
  22.7 0.0 collective-permute-start
  22.7 0.6 collective-permute-start.1
  23.3 13.3 %counts.1.counts_ref = bf16[64,352,256]{2,1,0:T(8,128)(2,1)} custom-call(s32[8,64,128]{2,1,0:T(8,128)} %bitcast.13, s32[7,64,128]{2,1,0:T(8,128)} %bitcast.14, s32[64,128]{1,0:T(8,128)} %bitcast.15), custom_call_target="tpu_custom_call" | custom-call | flops 12000000000 | bytes 13000000 | tf_op jit(solution)/shard_map/counts/pallas_call | solution.py:134
  36.7 2.1 %collective-permute-start.2 = (f32[32,256]{1,0:T(8,128)S(1)}, f32[32,256]{1,0:T(8,128)S(1)}, u32[]{:S(2)}, u32[]{:S(2)}) collective-permute-start(f32[32,256]{1,0:T(8,128)S(1)} %copy-done.9), channel_id=1, source_target_pairs={{0,4},{1,5},{2,6},{3,7},{4,0},{5,1},{6,2},{7,3},{8,12},{9,13},{10,... | collective-permute-start | bytes 98312 | tf_op jit(solution)/shard_map/ppermute | solution.py:437
  38.7 0.0 copy-done.8
  38.7 1.5 %collective-permute-start.3 = (f32[32,256]{1,0:T(8,128)S(1)}, f32[32,256]{1,0:T(8,128)S(1)}, u32[]{:S(2)}, u32[]{:S(2)}) collective-permute-start(f32[32,256]{1,0:T(8,128)S(1)} %copy-done.8), channel_id=1, source_target_pairs={{0,8},{1,9},{2,10},{3,11},{4,12},{5,13},{6,14},{7,15},{8,0},{9,1},... | collective-permute-start | bytes 98312 | tf_op jit(solution)/shard_map/ppermute | solution.py:437
  40.2 2.7 %collective-permute-start.4 = (f32[32,256]{1,0:T(8,128)S(1)}, f32[32,256]{1,0:T(8,128)S(1)}, u32[]{:S(2)}, u32[]{:S(2)}) collective-permute-start(f32[32,256]{1,0:T(8,128)S(1)} %copy-done.7), channel_id=1, source_target_pairs={{0,16},{1,17},{2,18},{3,19},{4,20},{5,21},{6,22},{7,23},{8,24},{9,... | collective-permute-start | bytes 98312 | tf_op jit(solution)/shard_map/ppermute | solution.py:437
  43.0 0.0 collective-permute-done.rest_0_
  43.0 0.0 copy-done.6
  43.0 1.6 %collective-permute-start.5 = (f32[32,256]{1,0:T(8,128)S(1)}, f32[32,256]{1,0:T(8,128)S(1)}, u32[]{:S(2)}, u32[]{:S(2)}) collective-permute-start(f32[32,256]{1,0:T(8,128)S(1)} %copy-done.6), channel_id=1, source_target_pairs={{0,32},{1,33},{2,34},{3,35},{4,36},{5,37},{6,38},{7,39},{8,40},{9,... | collective-permute-start | bytes 98312 | tf_op jit(solution)/shard_map/ppermute | solution.py:437
  44.5 0.0 collective-permute-done.1.rest_1_
  44.5 3.0 %collective-permute-start.6 = (f32[32,256]{1,0:T(8,128)S(1)}, f32[32,256]{1,0:T(8,128)S(1)}, u32[]{:S(2)}, u32[]{:S(2)}) collective-permute-start(f32[32,256]{1,0:T(8,128)S(1)} %copy-done.5), channel_id=1, source_target_pairs={{0,64},{1,65},{2,66},{3,67},{4,68},{5,69},{6,70},{7,71},{8,72},{9,... | collective-permute-start | bytes 98312 | tf_op jit(solution)/shard_map/ppermute | solution.py:437
  47.5 39.5 %near.1.rest_8_ = f32[128,512]{1,0:T(8,128)} custom-call(f32[128,512]{1,0:T(8,128)} %bitcast.9, s32[1,128]{1,0:T(1,128)} %tgt_ref.1, s32[1,128]{1,0:T(1,128)} %src_ref.1, s32[1,128]{1,0:T(1,128)} %off_ref.1), custom_call_target="tpu_custom_call" | custom-call | flops 8000000000 | bytes 1000000 | tf_op jit(solution)/shard_map/near/pallas_call | solution.py:264
  87.0 0.0 collective-permute-done.2.rest_2_
  87.0 0.0 collective-permute-done.3.rest_3_
  87.0 0.0 collective-permute-done.4.rest_4_
  87.0 0.0 collective-permute-done.5.rest_5_
  87.0 0.0 collective-permute-done.6.rest_6_
  87.0 0.0 copy-done.1
  87.0 0.0 copy-done.2
  87.0 0.0 copy-done.3
  87.0 0.0 copy-start.4
  87.1 0.9 copy-done.4
  88.0 37.4 %field.1 = f32[128,4,128]{2,1,0:T(4,128)} custom-call(bf16[64,352,256]{2,1,0:T(8,128)(2,1)} %counts.1.counts_ref, f32[165,165,128]{2,1,0:T(8,128)} %op_ref.1, f32[168,128]{1,0:T(8,128)S(1)} %copy-done.3, f32[32,256]{1,0:T(8,128)S(1)} %collective-permute-done.rest_0_, f32[32,256]{1,0:T(8,128)S(1)} %collective-permute-done.1.rest_1_, ...), custom_call_target="tpu_custom_call" | custom-call | flops 40000000000 | bytes 26000000 | tf_op jit(solution)/shard_map/field/pallas_call | solution.py:392
  (12 shorter events, 0.0 us)
Async XLA Ops:
  5.5 12.9 %all-to-all-start = ((f32[8,16,512]{2,1,0:T(8,128)}), f32[8,16,512]{2,1,0:T(8,128)S(1)}, u32[]{:S(2)}, u32[]{:S(2)}) async-start(f32[8,16,512]{2,1,0:T(8,128)} %bitcast.11), calls=%async_computation | async-start | bytes 524288 | tf_op jit(solution)/shard_map/all_to_all | solution.py:433
  18.4 0.7 copy-start
  22.7 20.3 %collective-permute-start = (f32[32,256]{1,0:T(8,128)}, f32[32,256]{1,0:T(8,128)S(1)}, u32[]{:S(2)}, u32[]{:S(2)}) collective-permute-start(f32[32,256]{1,0:T(8,128)} %get-tuple-element.15), channel_id=1, source_target_pairs={{0,1},{1,0},{2,3},{3,2},{4,5},{5,4},{6,7},{7,6},{8,9},{9,8},{10,11... | collective-permute-start | bytes 98312 | tf_op jit(solution)/shard_map/ppermute | solution.py:437
  22.7 21.9 %collective-permute-start.1 = (f32[32,256]{1,0:T(8,128)}, f32[32,256]{1,0:T(8,128)S(1)}, u32[]{:S(2)}, u32[]{:S(2)}) collective-permute-start(f32[32,256]{1,0:T(8,128)} %get-tuple-element.16), channel_id=1, source_target_pairs={{0,2},{1,3},{2,0},{3,1},{4,6},{5,7},{6,4},{7,5},{8,10},{9,11},{10,... | collective-permute-start | bytes 98312 | tf_op jit(solution)/shard_map/ppermute | solution.py:437
  23.3 13.4 %copy-start.9 = (f32[32,256]{1,0:T(8,128)S(1)}, f32[32,256]{1,0:T(8,128)}, u32[]{:S(2)}) copy-start(f32[32,256]{1,0:T(8,128)} %get-tuple-element.17) | copy-start | bytes 98308
  23.3 15.4 %copy-start.8 = (f32[32,256]{1,0:T(8,128)S(1)}, f32[32,256]{1,0:T(8,128)}, u32[]{:S(2)}) copy-start(f32[32,256]{1,0:T(8,128)} %get-tuple-element.18) | copy-start | bytes 98308
  23.3 16.9 %copy-start.7 = (f32[32,256]{1,0:T(8,128)S(1)}, f32[32,256]{1,0:T(8,128)}, u32[]{:S(2)}) copy-start(f32[32,256]{1,0:T(8,128)} %get-tuple-element.19) | copy-start | bytes 98308
  23.3 19.7 %copy-start.6 = (f32[32,256]{1,0:T(8,128)S(1)}, f32[32,256]{1,0:T(8,128)}, u32[]{:S(2)}) copy-start(f32[32,256]{1,0:T(8,128)} %get-tuple-element.20) | copy-start | bytes 98308
  23.3 21.2 %copy-start.5 = (f32[32,256]{1,0:T(8,128)S(1)}, f32[32,256]{1,0:T(8,128)}, u32[]{:S(2)}) copy-start(f32[32,256]{1,0:T(8,128)} %get-tuple-element.21) | copy-start | bytes 98308
  36.7 50.3 %collective-permute-start.2 = (f32[32,256]{1,0:T(8,128)S(1)}, f32[32,256]{1,0:T(8,128)S(1)}, u32[]{:S(2)}, u32[]{:S(2)}) collective-permute-start(f32[32,256]{1,0:T(8,128)S(1)} %copy-done.9), channel_id=1, source_target_pairs={{0,4},{1,5},{2,6},{3,7},{4,0},{5,1},{6,2},{7,3},{8,12},{9,13},{10,... | collective-permute-start | bytes 98312 | tf_op jit(solution)/shard_map/ppermute | solution.py:437
  38.7 48.3 %collective-permute-start.3 = (f32[32,256]{1,0:T(8,128)S(1)}, f32[32,256]{1,0:T(8,128)S(1)}, u32[]{:S(2)}, u32[]{:S(2)}) collective-permute-start(f32[32,256]{1,0:T(8,128)S(1)} %copy-done.8), channel_id=1, source_target_pairs={{0,8},{1,9},{2,10},{3,11},{4,12},{5,13},{6,14},{7,15},{8,0},{9,1},... | collective-permute-start | bytes 98312 | tf_op jit(solution)/shard_map/ppermute | solution.py:437
  40.2 46.8 %collective-permute-start.4 = (f32[32,256]{1,0:T(8,128)S(1)}, f32[32,256]{1,0:T(8,128)S(1)}, u32[]{:S(2)}, u32[]{:S(2)}) collective-permute-start(f32[32,256]{1,0:T(8,128)S(1)} %copy-done.7), channel_id=1, source_target_pairs={{0,16},{1,17},{2,18},{3,19},{4,20},{5,21},{6,22},{7,23},{8,24},{9,... | collective-permute-start | bytes 98312 | tf_op jit(solution)/shard_map/ppermute | solution.py:437
  43.0 44.0 %collective-permute-start.5 = (f32[32,256]{1,0:T(8,128)S(1)}, f32[32,256]{1,0:T(8,128)S(1)}, u32[]{:S(2)}, u32[]{:S(2)}) collective-permute-start(f32[32,256]{1,0:T(8,128)S(1)} %copy-done.6), channel_id=1, source_target_pairs={{0,32},{1,33},{2,34},{3,35},{4,36},{5,37},{6,38},{7,39},{8,40},{9,... | collective-permute-start | bytes 98312 | tf_op jit(solution)/shard_map/ppermute | solution.py:437
  44.5 42.5 %copy-start.1 = (f32[8,16,512]{2,1,0:T(8,128)S(1)}, f32[8,16,512]{2,1,0:T(8,128)}, u32[]{:S(2)}) copy-start(f32[8,16,512]{2,1,0:T(8,128)} %copy-done) | copy-start | bytes 786436
  44.5 42.5 %copy-start.2 = (f32[4,128,128]{2,1,0:T(8,128)S(1)}, f32[4,128,128]{2,1,0:T(8,128)}, u32[]{:S(2)}) copy-start(f32[4,128,128]{2,1,0:T(8,128)} %get-tuple-element.22.rest_7_) | copy-start | bytes 786436
  44.5 42.5 %copy-start.3 = (f32[168,128]{1,0:T(8,128)S(1)}, f32[168,128]{1,0:T(8,128)}, u32[]{:S(2)}) copy-start(f32[168,128]{1,0:T(8,128)} %get-tuple-element.14.mt_ref) | copy-start | bytes 258052
  44.5 42.5 %collective-permute-start.6 = (f32[32,256]{1,0:T(8,128)S(1)}, f32[32,256]{1,0:T(8,128)S(1)}, u32[]{:S(2)}, u32[]{:S(2)}) collective-permute-start(f32[32,256]{1,0:T(8,128)S(1)} %copy-done.5), channel_id=1, source_target_pairs={{0,64},{1,65},{2,66},{3,67},{4,68},{5,69},{6,70},{7,71},{8,72},{9,... | collective-permute-start | bytes 98312 | tf_op jit(solution)/shard_map/ppermute | solution.py:437
  87.0 1.0 copy-start.4

commit v2 on v1

v2 whole, which is shorter than its diff:
```python
import functools

import jax
import jax.numpy as jnp
import numpy as np
from jax import lax
from jax.experimental import pallas as pl
from jax.experimental.pallas import tpu as pltpu
from jax.sharding import PartitionSpec as P

ORDER = 8
TERMS = 165
ROWS = 168
TERMS_PAD = ROWS
SOFT = 0.01
SLOTS = 128
BODIES = 128
KEXP = 32
LEVELS = 7
CLASSES = 128
SOURCES = SLOTS + LEVELS * KEXP
f32 = jnp.float32
bf16 = jnp.bfloat16
VMEM = pltpu.VMEM
SMEM = pltpu.SMEM


def term_list():
    triples = []
    for degree in range(ORDER + 1):
        for a in range(degree, -1, -1):
            for b in range(degree - a, -1, -1):
                triples.append((a, b, degree - a - b))
    return {t: n for n, t in enumerate(triples)}


TERM = term_list()
NORM = {t: float(np.float32(np.sqrt(np.prod(2.0 * np.array(t) + 1.0)))) for t in TERM}


def small(mib):
    return pltpu.CompilerParams(vmem_limit_bytes=mib * 2**20)


def iota(shape, axis):
    return lax.broadcasted_iota(jnp.int32, shape, axis)


def split(v):
    high = v.astype(bf16)
    return high, (v - high.astype(f32)).astype(bf16)


def dot(a, b):
    return jnp.dot(a, b, preferred_element_type=f32)


def dot_nt(a, b):
    return lax.dot_general(a, b, (((1,), (1,)), ((), ())), preferred_element_type=f32)


def dot_exact(a, b):
    return jnp.dot(a, b, preferred_element_type=f32, precision=lax.Precision.HIGHEST)


def pack_kernel(owner_ref, pos_ref, mass_ref, out_ref, count_ref, *slot_refs):
    for r in slot_refs:
        r[...] = jnp.zeros_like(r)
    for o in range(8):
        count_ref[o] = 0

    def step(i, carry):
        o = owner_ref[0, i]
        rank = count_ref[o]
        count_ref[o] = rank + 1
        slot = o * 16 + rank
        for a in range(3):
            slot_refs[a][pl.ds(slot, 1), :] = pos_ref[a, pl.ds(i, 1), :]
        slot_refs[3][pl.ds(slot, 1), :] = mass_ref[pl.ds(i, 1), :]
        return carry

    lax.fori_loop(0, mass_ref.shape[0], step, 0)
    for a in range(4):
        out_ref[:, a * BODIES : (a + 1) * BODIES] = slot_refs[a][...]


def pack_tiles(owner, positions, masses):
    return pl.pallas_call(
        pack_kernel,
        out_shape=pltpu.HBM((SLOTS, 4 * BODIES), f32),
        in_specs=[
            pl.BlockSpec(memory_space=SMEM),
            pl.BlockSpec(memory_space=VMEM),
            pl.BlockSpec(memory_space=VMEM),
        ],
        out_specs=pl.BlockSpec(memory_space=VMEM),
        scratch_shapes=[pltpu.SMEM((8,), jnp.int32)] + [pltpu.VMEM((SLOTS, BODIES), f32)] * 4,
        compiler_params=small(2),
        name="pack",
    )(owner.T, positions.transpose(1, 0, 2), masses)


I_STEP = 16
I_FULL = TERMS // I_STEP
I_ROWS = (I_FULL + 1) * I_STEP
J_STEP = 8
PITCH = CLASSES + 1
J_BLOCKS = ROWS // J_STEP


def prepare_kernel(tgt_ref, far_ref, local_ref, op_ref, counts_ref, left_ref, tt_ref, st_ref, buf_ref, sem):
    def copy(q, size):
        return pltpu.make_async_copy(
            op_ref.at[pl.ds(q * I_STEP, size)], buf_ref.at[q, pl.ds(0, size), pl.ds(0, TERMS)], sem.at[q]
        )

    for q in range(I_FULL):
        copy(q, I_STEP).start()
    copy(I_FULL, TERMS - I_FULL * I_STEP).start()

    order = [7, 0, 1, 2, 3, 4, 5, 6]
    for pair in range(4):
        tgt, src = [], []
        for level in order[2 * pair : 2 * pair + 2]:
            tgt.append(tgt_ref[level].astype(f32))
            if level == 7:
                src.append(local_ref[...].astype(f32))
            else:
                offset = {0: SLOTS, 1: 0, 2: KEXP, 3: 0, 4: KEXP, 5: 0, 6: KEXP}[level]
                src.append((far_ref[level] + offset).astype(f32))
        tt_ref[pair] = jnp.concatenate(tgt, axis=0).T
        st_ref[pair] = jnp.concatenate(src, axis=0).T

    ids = iota((160, 128), 0).astype(f32).astype(bf16)

    def onehot(ref, part, c, first, size, total):
        row = jnp.broadcast_to(ref[part, pl.ds(c, 1), :].astype(bf16), (size, 128))
        hits = jnp.where(row == ids[0:size], jnp.ones((), bf16), jnp.zeros((), bf16))
        zeros = lambda n: [jnp.zeros((n, 128), bf16)] if n else []
        return jnp.concatenate(zeros(first) + [hits] + zeros(total - first - size), axis=0)

    def classes(p, carry):
        for k in range(2):
            c = 2 * p + k
            for half, (first, size) in enumerate(((0, 224), (224, 128))):
                cut = 160 if half == 0 else 64
                target = jnp.concatenate([onehot(tt_ref, 2 * half + i, c, 0, 128, 128) for i in range(2)], axis=1)
                source = jnp.concatenate(
                    [
                        onehot(st_ref, 2 * half, c, 0, cut, size),
                        onehot(st_ref, 2 * half + 1, c, cut, size - cut, size),
                    ],
                    axis=1,
                )
                counts = dot_nt(source, target)
                counts_ref[p, first : first + size, k * 128 : k * 128 + 128] = counts.astype(bf16)
        return carry

    lax.fori_loop(0, CLASSES // 2, classes, 0, unroll=16)

    for j in range(TERMS, ROWS):
        left_ref[J_BLOCKS - 1, :, (j % J_STEP) * 128 : (j % J_STEP) * 128 + 128] = jnp.zeros((2 * I_ROWS, 128), bf16)

    def relay(q):
        rows = buf_ref.at[q].reshape(I_STEP * TERMS_PAD, CLASSES)
        at = pl.multiple_of(q * I_STEP, I_STEP)
        for j in range(TERMS):
            v = rows[pl.ds(j, I_STEP, stride=TERMS_PAD), :]
            high, low = split(v)
            lanes = slice((j % J_STEP) * 128, (j % J_STEP) * 128 + 128)
            left_ref[j // J_STEP, pl.ds(at, I_STEP), lanes] = high
            left_ref[j // J_STEP, pl.ds(at + I_ROWS, I_STEP), lanes] = low

    def chunk(q, carry):
        copy(q, I_STEP).wait()
        relay(q)
        return carry

    lax.fori_loop(0, I_FULL, chunk, 0)
    copy(I_FULL, TERMS - I_FULL * I_STEP).wait()
    relay(I_FULL)


def prepare(m2l_target, far_source, local_source, operators):
    vm = pl.BlockSpec(memory_space=VMEM)
    return pl.pallas_call(
        prepare_kernel,
        out_shape=[
            VMEM((CLASSES // 2, SOURCES, 256), bf16),
            VMEM((J_BLOCKS, 2 * I_ROWS, J_STEP * CLASSES), bf16),
        ],
        in_specs=[vm, vm, vm, pl.BlockSpec(memory_space=pl.ANY)],
        out_specs=[vm, vm],
        scratch_shapes=[
            VMEM((4, 128, 128), f32),
            VMEM((4, 128, 128), f32),
            VMEM((I_FULL + 1, I_STEP, TERMS_PAD, CLASSES), f32),
            pltpu.SemaphoreType.DMA((I_FULL + 1,)),
        ],
        compiler_params=small(20),
        cost_estimate=pl.CostEstimate(flops=12 * 10**9, bytes_accessed=14 * 10**6, transcendentals=0),
        name="prepare",
    )(m2l_target, far_source, local_source, operators)


def multipole_kernel(recv_ref, slots_ref, mt_ref, post_ref, *rest):
    exp_refs, (acc_ref, m_ref, rows_ref) = rest[:LEVELS], rest[LEVELS:]
    for a in range(4):
        post_ref[a] = recv_ref[:, a * BODIES : (a + 1) * BODIES].T

    acc_ref[...] = jnp.zeros_like(acc_ref)

    def chunk(q, carry):
        rows = pl.ds(pl.multiple_of(q * 32, 32), 32)
        x, y, z, m = (post_ref[a, rows, :] for a in range(4))

        def fold(term, n):
            part = (term[0:8] + term[8:16]) + (term[16:24] + term[24:32])
            acc_ref[n] += part

        px = m
        for a in range(ORDER + 1):
            py = px
            for b in range(ORDER + 1 - a):
                pz = py
                for c in range(ORDER + 1 - a - b):
                    fold(pz, TERM[a, b, c])
                    if c < ORDER - a - b:
                        pz = pz * z
                if b < ORDER - a:
                    py = py * y
            if a < ORDER:
                px = px * x
        return carry

    lax.fori_loop(0, BODIES // 32, chunk, 0)
    mt_ref[TERMS - 5 :, :] = jnp.zeros((ROWS - TERMS + 5, SLOTS), f32)
    for (a, b, c), n in TERM.items():
        mt_ref[n : n + 1, :] = jnp.sum(acc_ref[n], axis=0, keepdims=True) * NORM[a, b, c]
    m_ref[0] = mt_ref[0:128, :].T
    m_ref[1] = jnp.concatenate([mt_ref[128:ROWS, :], jnp.zeros((256 - ROWS, SLOTS), f32)], axis=0).T
    for level in range(LEVELS):

        def row(k, carry):
            slot = slots_ref[level, 0, k]
            for half in range(2):
                rows_ref[half, pl.ds(k, 1), :] = m_ref[half, pl.ds(slot, 1), :]
            return carry

        lax.fori_loop(0, KEXP, row, 0, unroll=8)
        for half in range(2):
            exp_refs[level][:, half * 128 : half * 128 + 128] = rows_ref[half]


def multipoles_of(recv, export_slots):
    vm = pl.BlockSpec(memory_space=VMEM)
    out = pl.pallas_call(
        multipole_kernel,
        out_shape=[
            jax.ShapeDtypeStruct((ROWS, SLOTS), f32),
            jax.ShapeDtypeStruct((4, BODIES, SLOTS), f32),
        ]
        + [jax.ShapeDtypeStruct((KEXP, 256), f32)] * LEVELS,
        in_specs=[vm, pl.BlockSpec(memory_space=SMEM)],
        out_specs=[vm] * (2 + LEVELS),
        scratch_shapes=[
            pltpu.VMEM((TERMS, 8, SLOTS), f32),
            pltpu.VMEM((2, SLOTS, 128), f32),
            pltpu.VMEM((2, KEXP, 128), f32),
        ],
        compiler_params=small(4),
        name="multipoles",
    )(recv, export_slots.transpose(1, 0, 2))
    return out[0], out[1], out[2:]


def near_kernel(post_ref, tgt_ref, src_ref, off_ref, near_ref, s_ref, t_ref, a_ref):
    row = iota((128, 128), 0)
    pick_s = jnp.where(src_ref[...] == row, 1.0, 0.0)
    pick_t = jnp.where(tgt_ref[...] == row, 1.0, 0.0)
    k = off_ref[...].astype(f32)
    one, zero = jnp.ones_like(k), jnp.zeros_like(k)
    kx = jnp.where(k >= 9.0, one, zero) + jnp.where(k >= 18.0, one, zero)
    k = k - 9.0 * kx
    ky = jnp.where(k >= 3.0, one, zero) + jnp.where(k >= 6.0, one, zero)
    kz = k - 3.0 * ky
    for a, shift in enumerate((kx, ky, kz)):
        s_ref[a] = dot_exact(post_ref[a], pick_s) + 2.0 * (shift - 1.0)
        t_ref[a] = dot_exact(post_ref[a], pick_t)
    s_ref[3] = dot_exact(post_ref[3], pick_s)

    def chunk(q, carry):
        rows = pl.ds(pl.multiple_of(q * 32, 32), 32)
        tx, ty, tz = (t_ref[a, rows, :] for a in range(3))

        def source(j, state):
            p, ax, ay, az = state
            sx, sy, sz, m = (s_ref[a, pl.ds(j, 1), :] for a in range(4))
            rx, ry, rz = sx - tx, sy - ty, sz - tz
            inv = lax.rsqrt(rx * rx + ry * ry + rz * rz + SOFT)
            w = m * inv
            p = p - w
            w = w * (inv * inv)
            return p, ax + rx * w, ay + ry * w, az + rz * w

        done = lax.fori_loop(0, 128, source, (jnp.zeros((32, 128), f32),) * 4, unroll=8)
        for a in range(4):
            a_ref[a, rows, :] = done[a]
        return carry

    lax.fori_loop(0, 4, chunk, 0)
    into = pick_t.T
    for a in range(4):
        near_ref[a] = dot_exact(a_ref[a], into)


def near_field(post, target, source, offset):
    vm = pl.BlockSpec(memory_space=VMEM)
    return pl.pallas_call(
        near_kernel,
        out_shape=jax.ShapeDtypeStruct((4, BODIES, SLOTS), f32),
        in_specs=[vm] * 4,
        out_specs=vm,
        scratch_shapes=[VMEM((4, 128, 128), f32), VMEM((3, 128, 128), f32), VMEM((4, 128, 128), f32)],
        compiler_params=small(4),
        cost_estimate=pl.CostEstimate(flops=8 * 10**9, bytes_accessed=10**6, transcendentals=2 * 10**6),
        name="near",
    )(post, target, source, offset)


def field_kernel(counts_ref, left_ref, mt_ref, *rest):
    far_refs, rest = rest[:LEVELS], rest[LEVELS:]
    post_ref, near_ref, out_ref, src_ref, bt_ref, acc_ref, e_ref, f_ref = rest

    far = jnp.concatenate([r[...] for r in far_refs], axis=0)
    far = jnp.concatenate([far, jnp.zeros((32, 256), f32)], axis=0)
    parts = [mt_ref[...]]
    for q in range(2):
        block = far[q * 128 : q * 128 + 128, :]
        parts.append(jnp.concatenate([block[:, 0:128].T, block[:, 128:256].T[0 : ROWS - 128]], axis=0))
    sources = jnp.concatenate(parts, axis=1)
    high = sources.astype(bf16).astype(f32)
    both = jnp.concatenate([high, sources - high], axis=0).astype(bf16)
    src_ref[...] = both[:, 0:SOURCES]

    def move(p, carry):
        moved = dot(src_ref[...], counts_ref[p])
        moved = moved[0:ROWS] + moved[ROWS : 2 * ROWS]
        for k in range(2):
            bt_ref[pl.ds(2 * p + k, ROWS, stride=PITCH), :] = moved[:, k * 128 : k * 128 + 128]
        return carry

    lax.fori_loop(0, CLASSES // 2, move, 0, unroll=16)

    acc_ref[...] = jnp.zeros_like(acc_ref)

    def contract(jb, carry):
        right = [
            jnp.concatenate(split(bt_ref[pl.ds((jb * J_STEP + j) * PITCH, CLASSES), :]), axis=1)
            for j in range(J_STEP)
        ]
        acc_ref[...] += dot(left_ref[jb], jnp.concatenate(right, axis=0))
        return carry

    lax.fori_loop(0, J_BLOCKS, contract, 0, unroll=21)
    acc = acc_ref[...]
    e = (acc[I_ROWS:, 128:] + acc[I_ROWS:, :128]) + acc[:I_ROWS, 128:] + acc[:I_ROWS, :128]
    e_ref[...] = e[0:ROWS]

    present = jnp.where(post_ref[3, 0:1, :] > 0.0, 1.0, 0.0)

    def chunk(q, carry):
        rows = pl.ds(pl.multiple_of(q * 32, 32), 32)
        x, y, z = (post_ref[a, rows, :] for a in range(3))

        def coef(a, b, c):
            n = TERM[a, b, c]
            return jnp.broadcast_to(e_ref[n : n + 1, :] * NORM[a, b, c], (32, SLOTS))

        p = px = py = pz = None
        for a in range(ORDER, -1, -1):
            r = ry = rz = None
            for b in range(ORDER - a, -1, -1):
                top = ORDER - a - b
                v = coef(a, b, top)
                vz = None
                for c in range(top - 1, -1, -1):
                    vz = v if vz is None else vz * z + v
                    v = v * z + coef(a, b, c)
                if r is None:
                    r = v
                else:
                    ry = r if ry is None else ry * y + r
                    r = r * y + v
                    if vz is not None:
                        rz = vz if rz is None else rz * y + vz
            if p is None:
                p = r
            else:
                px = p if px is None else px * x + p
                p = p * x + r
                py = ry if py is None else py * x + ry
                pz = rz if pz is None else pz * x + rz
        for a, v in enumerate((p, -px, -py, -pz)):
            f_ref[a, rows, :] = (v + near_ref[a, rows, :]) * present
        return carry

    lax.fori_loop(0, BODIES // 32, chunk, 0)
    for a in range(4):
        out_ref[:, a, :] = f_ref[a].T


def field(counts, left, mt, far, post, near):
    vm = pl.BlockSpec(memory_space=VMEM)
    return pl.pallas_call(
        field_kernel,
        out_shape=jax.ShapeDtypeStruct((SLOTS, 4, BODIES), f32),
        in_specs=[vm] * (5 + LEVELS),
        out_specs=vm,
        scratch_shapes=[
            VMEM((2 * ROWS, SOURCES), bf16),
            VMEM((ROWS * PITCH, SLOTS), f32),
            VMEM((2 * I_ROWS, 256), f32),
            VMEM((ROWS, SLOTS), f32),
            VMEM((4, BODIES, SLOTS), f32),
        ],
        compiler_params=small(20),
        cost_estimate=pl.CostEstimate(flops=40 * 10**9, bytes_accessed=26 * 10**6, transcendentals=0),
        name="field",
    )(counts, left, mt, *far, post, near)


def body(
    positions,
    masses,
    owner,
    operators,
    m2l_target,
    far_source,
    local_source,
    export_slots,
    near_target,
    near_source,
    near_offset,
):
    axes = ("dom", "sub")
    devices = lax.axis_size(axes)
    sent = pack_tiles(owner, positions, masses)
    recv = lax.all_to_all(sent, "sub", split_axis=0, concat_axis=0, tiled=True)
    counts, left = prepare(m2l_target[0], far_source[0], local_source[0], operators)
    mt, post, exported = multipoles_of(recv, export_slots)
    far = [
        lax.ppermute(rows, axes, [(i, i ^ (1 << level)) for i in range(devices)])
        for level, rows in enumerate(exported)
    ]
    near = near_field(post, near_target, near_source, near_offset)
    return field(counts, left, mt, far, post, near)


def solution(mesh):
    both = ("dom", "sub")
    in_specs = (
        P(both, None, None),
        P(both, None),
        P(both, None),
        P(),
        P(both, None, None, None),
        P(both, None, None, None),
        P(both, None, None),
        P(both, None, None),
        P(both, None),
        P(both, None),
        P(both, None),
    )
    out_specs = P(both, None, None)
    return jax.shard_map(body, mesh=mesh, in_specs=in_specs, out_specs=out_specs, check_vma=False)
```

time: 126 us -> 66.4 us (0.53)
  Pallas kernels: 96.2 us -> 35.7 us
  blocking collectives: 0 us -> 12.9 us
  waiting for transfers between devices: 6.28 us -> 0.02 us
  starting transfers between devices: 16.9 us -> 11.6 us
    pallas_call x4, Pallas kernels: 92.7 us -> 33.4 us  [the longest x1 13.5 us: field(): pl.pallas_call(field_kernel, out_shape=jax.ShapeDtypeStruct((SLOTS, 4, BO...]
    all_to_all x0 -> x1, blocking collectives: none -> 12.9 us  [body(): recv = lax.all_to_all(sent, 'sub', split_axis=0, concat_axis=0, tiled=True)]
    all_to_all x1 -> x0, waiting for transfers between devices: 6.26 us -> none  [body(): recv = lax.all_to_all(sent, 'sub', split_axis=0, concat_axis=0, tiled=True)]
    all_to_all x1 -> x0, starting transfers between devices: 5.4 us -> none  [body(): recv = lax.all_to_all(sent, 'sub', split_axis=0, concat_axis=0, tiled=True)]
    unnamed x23 -> x20, local copies, waits for them, and re-layouts: 5.91 us -> 5.65 us
  transfers between devices with their start and end apart: 8 -> 7, of which waited for: 1 -> 0; matrix products, arithmetic and copies ran while one was open for 1% -> 0% of each run, Pallas kernels for 42% -> 27%
where the time goes in v2:
time: 66.4 us; the launch traced here: 66 us
  Pallas kernels  35.7 us (54%)
  blocking collectives  12.9 us (19%)
  starting transfers between devices  11.6 us (17%)
  local copies, waits for them, and re-layouts  5.65 us (9%)
    pallas_call x1, Pallas kernels, field(): pl.pallas_call(field_kernel, out_shape=jax.ShapeDtypeStruct((SLOTS, 4, BO...  13.5 us
    all_to_all x1, blocking collectives, body(): recv = lax.all_to_all(sent, 'sub', split_axis=0, concat_axis=0, tiled=True)  12.9 us
    ppermute x7, starting transfers between devices, body(): lax.ppermute(rows, axes, [(i, i ^ 1 << level) for i in range(devices)])  11.6 us
    pallas_call x1, Pallas kernels, prepare(): pl.pallas_call(prepare_kernel, out_shape=[VMEM((CLASSES // 2, SOURCES, 25...  10.9 us
    pallas_call x1, Pallas kernels, near_field(): pl.pallas_call(near_kernel, out_shape=jax.ShapeDtypeStruct((4, BODIES, SL...  7.11 us
    unnamed x20, local copies, waits for them, and re-layouts  5.65 us
    pallas_call x1, Pallas kernels, multipoles_of(): pl.pallas_call(multipole_kernel, out_shape=[jax.ShapeDtypeStruct((ROWS, S...  2.32 us
    pallas_call x1, Pallas kernels, pack_tiles(): pl.pallas_call(pack_kernel, out_shape=pltpu.HBM((SLOTS, 4 * BODIES), f32)...  1.86 us
  transfers between devices with their start and end apart: 7, of which 0 were waited for; matrix products, arithmetic and copies ran while one was open for 0% of the time, Pallas kernels for 27%

profile of v2, /device:TPU:0, one launch (start us, length us, event | category | flops | bytes accessed | tf_op | source)
XLA Modules:
  0.0 66.0 jit_solution(3712440606393949459)
XLA Ops:
  0.0 0.0 copy-start
  0.0 0.9 %copy-done = f32[64,3,128]{2,0,1:T(8,128)S(1)} copy-done((f32[64,3,128]{2,0,1:T(8,128)S(1)}, f32[64,3,128]{2,0,1:T(8,128)}, u32[]{:S(2)}) %copy-start) | copy-done | bytes 98328
  0.9 0.0 copy-start.1
  0.9 0.8 %copy-done.1 = f32[64,128]{1,0:T(8,128)S(1)} copy-done((f32[64,128]{1,0:T(8,128)S(1)}, f32[64,128]{1,0:T(8,128)}, u32[]{:S(2)}) %copy-start.1) | copy-done | bytes 32792
  1.7 0.7 copy-done.3
  2.3 1.9 %pack.1 = f32[128,512]{1,0:T(8,128)} custom-call(s32[1,64]{1,0:T(1,128)S(1)} %bitcast.11, f32[3,64,128]{2,1,0:T(8,128)S(1)} %bitcast.9, f32[64,128]{1,0:T(8,128)S(1)} %copy-done.1), custom_call_target="tpu_custom_call" | custom-call | tf_op jit(solution)/shard_map/pack/pallas_call | solution.py:88
  4.2 12.9 %all_to_all.11 = f32[8,16,512]{2,1,0:T(8,128)S(1)} all-to-all(f32[8,16,512]{2,1,0:T(8,128)} %bitcast.15), channel_id=1, replica_groups=mesh['dom'=16,'sub'=8] {'sub'}, dimensions={0} | all-to-all | bytes 524288 | tf_op jit(solution)/shard_map/all_to_all | solution.py:449
  17.1 0.7 %copy-done.2 = s32[1,7,32]{2,0,1:T(1,128)S(1)} copy-done((s32[1,7,32]{2,0,1:T(1,128)S(1)}, s32[1,7,32]{2,0,1:T(1,128)}, u32[]{:S(2)}) %copy-start.2) | copy-done | bytes 920
  17.8 2.3 %multipoles.1 = (f32[168,128]{1,0:T(8,128)S(1)}, f32[4,128,128]{2,1,0:T(8,128)S(1)}, f32[32,256]{1,0:T(8,128)S(1)}, f32[32,256]{1,0:T(8,128)S(1)}, f32[32,256]{1...) custom-call(f32[128,512]{1,0:T(8,128)S(1)} %bitcast.8, ...), custom_call_target="tpu_custom_call" | custom-call | tf_op jit(solution)/shard_map/multipoles/pallas_call | solution.py:257
  20.1 0.1 collective-permute-start
  20.2 0.6 collective-permute-start.1
  20.9 0.9 %copy-done.4 = s32[1,8,64,128]{3,2,1,0:T(8,128)S(1)} copy-done((s32[1,8,64,128]{3,2,1,0:T(8,128)S(1)}, s32[1,8,64,128]{3,2,1,0:T(8,128)}, u32[]{:S(2)}) %copy-start.4) | copy-done | bytes 262168
  21.8 0.9 %copy-done.5 = s32[1,7,64,128]{3,2,1,0:T(8,128)S(1)} copy-done((s32[1,7,64,128]{3,2,1,0:T(8,128)S(1)}, s32[1,7,64,128]{3,2,1,0:T(8,128)}, u32[]{:S(2)}) %copy-start.5) | copy-done | bytes 229400
  22.7 0.8 %copy-done.6 = s32[1,64,128]{2,1,0:T(8,128)S(1)} copy-done((s32[1,64,128]{2,1,0:T(8,128)S(1)}, s32[1,64,128]{2,1,0:T(8,128)}, u32[]{:S(2)}) %copy-start.6) | copy-done | bytes 32792
  23.5 10.9 %prepare.1 = (bf16[64,352,256]{2,1,0:T(8,128)(2,1)S(1)}, bf16[21,352,1024]{2,1,0:T(8,128)(2,1)S(1)}) custom-call(s32[8,64,128]{2,1,0:T(8,128)S(1)} %bitcast.12, s32[7,64,128]{2,1,0:T(8,128)S(1)} %bitcast.13, s32[64,128]{1,0:T(8,128)S(1)} %bitcast.14, f32[165,165,128]{2,1,0:T(8,128)} %op_ref.1), custom_call_target="tpu_custom_call" | custom-call | flops 12000000000 | bytes 14000000 | tf_op jit(solution)/shard_map/prepare/pallas_call | solution.py:186
  34.4 2.2 %collective-permute-start.2 = (f32[32,256]{1,0:T(8,128)S(1)}, f32[32,256]{1,0:T(8,128)S(1)}, u32[]{:S(2)}, u32[]{:S(2)}) collective-permute-start(f32[32,256]{1,0:T(8,128)S(1)} %get-tuple-element.21), channel_id=1, source_target_pairs={{0,4},{1,5},{2,6},{3,7},{4,0},{5,1},{6,2},{7,3},{8,12},{9,13},{10,... | collective-permute-start | bytes 98312 | tf_op jit(solution)/shard_map/ppermute | solution.py:453
  36.6 1.5 %collective-permute-start.3 = (f32[32,256]{1,0:T(8,128)S(1)}, f32[32,256]{1,0:T(8,128)S(1)}, u32[]{:S(2)}, u32[]{:S(2)}) collective-permute-start(f32[32,256]{1,0:T(8,128)S(1)} %get-tuple-element.22), channel_id=1, source_target_pairs={{0,8},{1,9},{2,10},{3,11},{4,12},{5,13},{6,14},{7,15},{8,0},{9,1},... | collective-permute-start | bytes 98312 | tf_op jit(solution)/shard_map/ppermute | solution.py:453
  38.1 2.7 %collective-permute-start.4 = (f32[32,256]{1,0:T(8,128)S(1)}, f32[32,256]{1,0:T(8,128)S(1)}, u32[]{:S(2)}, u32[]{:S(2)}) collective-permute-start(f32[32,256]{1,0:T(8,128)S(1)} %get-tuple-element.23), channel_id=1, source_target_pairs={{0,16},{1,17},{2,18},{3,19},{4,20},{5,21},{6,22},{7,23},{8,24},{9,... | collective-permute-start | bytes 98312 | tf_op jit(solution)/shard_map/ppermute | solution.py:453
  40.8 0.0 collective-permute-done.rest_0_
  40.8 1.6 %collective-permute-start.5 = (f32[32,256]{1,0:T(8,128)S(1)}, f32[32,256]{1,0:T(8,128)S(1)}, u32[]{:S(2)}, u32[]{:S(2)}) collective-permute-start(f32[32,256]{1,0:T(8,128)S(1)} %get-tuple-element.24), channel_id=1, source_target_pairs={{0,32},{1,33},{2,34},{3,35},{4,36},{5,37},{6,38},{7,39},{8,40},{9,... | collective-permute-start | bytes 98312 | tf_op jit(solution)/shard_map/ppermute | solution.py:453
  42.4 0.0 collective-permute-done.1.rest_1_
  42.4 2.9 %collective-permute-start.6 = (f32[32,256]{1,0:T(8,128)S(1)}, f32[32,256]{1,0:T(8,128)S(1)}, u32[]{:S(2)}, u32[]{:S(2)}) collective-permute-start(f32[32,256]{1,0:T(8,128)S(1)} %get-tuple-element.25), channel_id=1, source_target_pairs={{0,64},{1,65},{2,66},{3,67},{4,68},{5,69},{6,70},{7,71},{8,72},{9,... | collective-permute-start | bytes 98312 | tf_op jit(solution)/shard_map/ppermute | solution.py:453
  45.3 0.0 copy-done.7
  45.3 0.0 copy-done.8
  45.3 0.0 copy-done.9
  45.3 7.1 %near.1.rest_8_ = f32[4,128,128]{2,1,0:T(8,128)S(1)} custom-call(f32[4,128,128]{2,1,0:T(8,128)S(1)} %get-tuple-element.26.post_ref.rest_7_, s32[1,128]{1,0:T(1,128)S(1)} %copy-done.7, s32[1,128]{1,0:T(1,128)S(1)} %copy-done.8, s32[1,128]{1,0:T(1,128)S(1)} %copy-done.9), custom_call_target="tpu_custom_call" | custom-call | flops 8000000000 | bytes 1000000 | tf_op jit(solution)/shard_map/near/pallas_call | solution.py:319
  52.4 0.0 collective-permute-done.2.rest_2_
  52.4 0.0 collective-permute-done.3.rest_3_
  52.4 0.0 collective-permute-done.4.rest_4_
  52.4 0.0 collective-permute-done.5.rest_5_
  52.4 0.0 collective-permute-done.6.rest_6_
  52.4 13.5 %field.1 = f32[128,4,128]{2,1,0:T(4,128)} custom-call(bf16[64,352,256]{2,1,0:T(8,128)(2,1)S(1)} %get-tuple-element.16.counts_ref, bf16[21,352,1024]{2,1,0:T(8,128)(2,1)S(1)} %get-tuple-element.17.left_ref, f32[168,128]{1,0:T(8,128)S(1)} %get-tuple-element.18.mt_ref, f32[32,256]{1,0:T(8,128)S(1)} %collective-permute-done.rest_0_, ...), custom_call_target="tpu_custom_call" | custom-call | flops 40000000000 | bytes 26000000 | tf_op jit(solution)/shard_map/field/pallas_call | solution.py:415
  (8 shorter events, 0.0 us)
Async XLA Ops:
  0.0 0.9 %copy-start = (f32[64,3,128]{2,0,1:T(8,128)S(1)}, f32[64,3,128]{2,0,1:T(8,128)}, u32[]{:S(2)}) copy-start(f32[64,3,128]{2,0,1:T(8,128)} %param.11) | copy-start | bytes 294916
  0.9 0.8 %copy-start.1 = (f32[64,128]{1,0:T(8,128)S(1)}, f32[64,128]{1,0:T(8,128)}, u32[]{:S(2)}) copy-start(f32[64,128]{1,0:T(8,128)} %mass_ref.1) | copy-start | bytes 98308
  1.7 0.7 copy-start.3
  17.1 0.7 %copy-start.2 = (s32[1,7,32]{2,0,1:T(1,128)S(1)}, s32[1,7,32]{2,0,1:T(1,128)}, u32[]{:S(2)}) copy-start(s32[1,7,32]{2,0,1:T(1,128)} %param.18) | copy-start | bytes 2692
  20.1 20.7 %collective-permute-start = (f32[32,256]{1,0:T(8,128)S(1)}, f32[32,256]{1,0:T(8,128)S(1)}, u32[]{:S(2)}, u32[]{:S(2)}) collective-permute-start(f32[32,256]{1,0:T(8,128)S(1)} %get-tuple-element.19), channel_id=1, source_target_pairs={{0,1},{1,0},{2,3},{3,2},{4,5},{5,4},{6,7},{7,6},{8,9},{9,8},{10,11... | collective-permute-start | bytes 98312 | tf_op jit(solution)/shard_map/ppermute | solution.py:453
  20.2 22.1 %collective-permute-start.1 = (f32[32,256]{1,0:T(8,128)S(1)}, f32[32,256]{1,0:T(8,128)S(1)}, u32[]{:S(2)}, u32[]{:S(2)}) collective-permute-start(f32[32,256]{1,0:T(8,128)S(1)} %get-tuple-element.20), channel_id=1, source_target_pairs={{0,2},{1,3},{2,0},{3,1},{4,6},{5,7},{6,4},{7,5},{8,10},{9,11},{10,... | collective-permute-start | bytes 98312 | tf_op jit(solution)/shard_map/ppermute | solution.py:453
  20.8 0.9 %copy-start.4 = (s32[1,8,64,128]{3,2,1,0:T(8,128)S(1)}, s32[1,8,64,128]{3,2,1,0:T(8,128)}, u32[]{:S(2)}) copy-start(s32[1,8,64,128]{3,2,1,0:T(8,128)} %param.15) | copy-start | bytes 786436
  21.8 0.9 %copy-start.5 = (s32[1,7,64,128]{3,2,1,0:T(8,128)S(1)}, s32[1,7,64,128]{3,2,1,0:T(8,128)}, u32[]{:S(2)}) copy-start(s32[1,7,64,128]{3,2,1,0:T(8,128)} %param.16) | copy-start | bytes 688132
  22.7 0.8 %copy-start.6 = (s32[1,64,128]{2,1,0:T(8,128)S(1)}, s32[1,64,128]{2,1,0:T(8,128)}, u32[]{:S(2)}) copy-start(s32[1,64,128]{2,1,0:T(8,128)} %param.17) | copy-start | bytes 98308
  23.5 21.8 %copy-start.7 = (s32[1,128]{1,0:T(1,128)S(1)}, s32[1,128]{1,0:T(1,128)}, u32[]{:S(2)}) copy-start(s32[1,128]{1,0:T(1,128)} %tgt_ref.1) | copy-start | bytes 1540
  23.5 21.8 %copy-start.8 = (s32[1,128]{1,0:T(1,128)S(1)}, s32[1,128]{1,0:T(1,128)}, u32[]{:S(2)}) copy-start(s32[1,128]{1,0:T(1,128)} %src_ref.1) | copy-start | bytes 1540
  23.5 21.8 %copy-start.9 = (s32[1,128]{1,0:T(1,128)S(1)}, s32[1,128]{1,0:T(1,128)}, u32[]{:S(2)}) copy-start(s32[1,128]{1,0:T(1,128)} %off_ref.1) | copy-start | bytes 1540
  34.4 18.0 %collective-permute-start.2 = (f32[32,256]{1,0:T(8,128)S(1)}, f32[32,256]{1,0:T(8,128)S(1)}, u32[]{:S(2)}, u32[]{:S(2)}) collective-permute-start(f32[32,256]{1,0:T(8,128)S(1)} %get-tuple-element.21), channel_id=1, source_target_pairs={{0,4},{1,5},{2,6},{3,7},{4,0},{5,1},{6,2},{7,3},{8,12},{9,13},{10,... | collective-permute-start | bytes 98312 | tf_op jit(solution)/shard_map/ppermute | solution.py:453
  36.6 15.8 %collective-permute-start.3 = (f32[32,256]{1,0:T(8,128)S(1)}, f32[32,256]{1,0:T(8,128)S(1)}, u32[]{:S(2)}, u32[]{:S(2)}) collective-permute-start(f32[32,256]{1,0:T(8,128)S(1)} %get-tuple-element.22), channel_id=1, source_target_pairs={{0,8},{1,9},{2,10},{3,11},{4,12},{5,13},{6,14},{7,15},{8,0},{9,1},... | collective-permute-start | bytes 98312 | tf_op jit(solution)/shard_map/ppermute | solution.py:453
  38.1 14.4 %collective-permute-start.4 = (f32[32,256]{1,0:T(8,128)S(1)}, f32[32,256]{1,0:T(8,128)S(1)}, u32[]{:S(2)}, u32[]{:S(2)}) collective-permute-start(f32[32,256]{1,0:T(8,128)S(1)} %get-tuple-element.23), channel_id=1, source_target_pairs={{0,16},{1,17},{2,18},{3,19},{4,20},{5,21},{6,22},{7,23},{8,24},{9,... | collective-permute-start | bytes 98312 | tf_op jit(solution)/shard_map/ppermute | solution.py:453
  40.8 11.6 %collective-permute-start.5 = (f32[32,256]{1,0:T(8,128)S(1)}, f32[32,256]{1,0:T(8,128)S(1)}, u32[]{:S(2)}, u32[]{:S(2)}) collective-permute-start(f32[32,256]{1,0:T(8,128)S(1)} %get-tuple-element.24), channel_id=1, source_target_pairs={{0,32},{1,33},{2,34},{3,35},{4,36},{5,37},{6,38},{7,39},{8,40},{9,... | collective-permute-start | bytes 98312 | tf_op jit(solution)/shard_map/ppermute | solution.py:453
  42.4 10.1 %collective-permute-start.6 = (f32[32,256]{1,0:T(8,128)S(1)}, f32[32,256]{1,0:T(8,128)S(1)}, u32[]{:S(2)}, u32[]{:S(2)}) collective-permute-start(f32[32,256]{1,0:T(8,128)S(1)} %get-tuple-element.25), channel_id=1, source_target_pairs={{0,64},{1,65},{2,66},{3,67},{4,68},{5,69},{6,70},{7,71},{8,72},{9,... | collective-permute-start | bytes 98312 | tf_op jit(solution)/shard_map/ppermute | solution.py:453

commit v3 on v2

--- a/solution.py
+++ b/solution.py
@@ -42,6 +42,10 @@
     return pltpu.CompilerParams(vmem_limit_bytes=mib * 2**20)
 
 
+def in_hbm(x):
+    return pltpu.with_memory_space_constraint(x, pltpu.HBM)
+
+
 def iota(shape, axis):
     return lax.broadcasted_iota(jnp.int32, shape, axis)
 
@@ -63,11 +67,19 @@
     return jnp.dot(a, b, preferred_element_type=f32, precision=lax.Precision.HIGHEST)
 
 
-def pack_kernel(owner_ref, pos_ref, mass_ref, out_ref, count_ref, *slot_refs):
+def pack_kernel(owner_hbm, pos_hbm, mass_hbm, out_ref, owner_ref, pos_ref, mass_ref, sem, count_ref, *slot_refs):
+    copies = [
+        pltpu.make_async_copy(a, b, sem.at[k])
+        for k, (a, b) in enumerate(((owner_hbm, owner_ref), (pos_hbm, pos_ref), (mass_hbm, mass_ref)))
+    ]
+    for c in copies:
+        c.start()
     for r in slot_refs:
         r[...] = jnp.zeros_like(r)
     for o in range(8):
         count_ref[o] = 0
+    for c in copies:
+        c.wait()
 
     def step(i, carry):
         o = owner_ref[0, i]
@@ -88,35 +100,60 @@
     return pl.pallas_call(
         pack_kernel,
         out_shape=pltpu.HBM((SLOTS, 4 * BODIES), f32),
-        in_specs=[
-            pl.BlockSpec(memory_space=SMEM),
-            pl.BlockSpec(memory_space=VMEM),
-            pl.BlockSpec(memory_space=VMEM),
-        ],
+        in_specs=[pl.BlockSpec(memory_space=pltpu.HBM)] * 3,
         out_specs=pl.BlockSpec(memory_space=VMEM),
-        scratch_shapes=[pltpu.SMEM((8,), jnp.int32)] + [pltpu.VMEM((SLOTS, BODIES), f32)] * 4,
+        scratch_shapes=[
+            pltpu.SMEM((1, owner.shape[0]), jnp.int32),
+            VMEM((3, owner.shape[0], BODIES), f32),
+            VMEM((owner.shape[0], BODIES), f32),
+            pltpu.SemaphoreType.DMA((3,)),
+            pltpu.SMEM((8,), jnp.int32),
+        ]
+        + [VMEM((SLOTS, BODIES), f32)] * 4,
         compiler_params=small(2),
         name="pack",
-    )(owner.T, positions.transpose(1, 0, 2), masses)
+    )(*map(in_hbm, (owner.T, positions.transpose(1, 0, 2), masses)))
 
 
 I_STEP = 16
 I_FULL = TERMS // I_STEP
+PAIR_STEP = 16
+GROUPS = CLASSES // 2 // PAIR_STEP
 I_ROWS = (I_FULL + 1) * I_STEP
 J_STEP = 8
 PITCH = CLASSES + 1
 J_BLOCKS = ROWS // J_STEP
 
 
-def prepare_kernel(tgt_ref, far_ref, local_ref, op_ref, counts_ref, left_ref, tt_ref, st_ref, buf_ref, sem):
+def prepare_kernel(
+    tgt_hbm, far_hbm, local_hbm, op_hbm, counts_hbm, left_hbm, done_ref,
+    tgt_ref, far_ref, local_ref, tt_ref, st_ref, buf_ref, counts_ref, left_ref, in_sem, sem, counts_sem, left_sem,
+):
+    lists = [
+        pltpu.make_async_copy(a, b, in_sem.at[k])
+        for k, (a, b) in enumerate(((tgt_hbm, tgt_ref), (far_hbm, far_ref), (local_hbm, local_ref)))
+    ]
+    for c in lists:
+        c.start()
+
     def copy(q, size):
         return pltpu.make_async_copy(
-            op_ref.at[pl.ds(q * I_STEP, size)], buf_ref.at[q, pl.ds(0, size), pl.ds(0, TERMS)], sem.at[q]
+            op_hbm.at[pl.ds(q * I_STEP, size)], buf_ref.at[q, pl.ds(0, size), pl.ds(0, TERMS)], sem.at[q]
         )
+
+    def counts_out(g):
+        pairs = pl.ds(g * PAIR_STEP, PAIR_STEP)
+        return pltpu.make_async_copy(counts_ref.at[pairs], counts_hbm.at[pairs], counts_sem.at[g])
+
+    def left_out(q, part):
+        rows = pl.ds(pl.multiple_of(part * I_ROWS + q * I_STEP, I_STEP), I_STEP)
+        return pltpu.make_async_copy(left_ref.at[:, rows], left_hbm.at[:, rows], left_sem.at[part, q])
 
     for q in range(I_FULL):
         copy(q, I_STEP).start()
     copy(I_FULL, TERMS - I_FULL * I_STEP).start()
+    for c in lists:
+        c.wait()
 
     order = [7, 0, 1, 2, 3, 4, 5, 6]
     for pair in range(4):
@@ -139,7 +176,7 @@
         zeros = lambda n: [jnp.zeros((n, 128), bf16)] if n else []
         return jnp.concatenate(zeros(first) + [hits] + zeros(total - first - size), axis=0)
 
-    def classes(p, carry):
+    def classes(p):
         for k in range(2):
             c = 2 * p + k
             for half, (first, size) in enumerate(((0, 224), (224, 128))):
@@ -154,9 +191,14 @@
                 )
                 counts = dot_nt(source, target)
                 counts_ref[p, first : first + size, k * 128 : k * 128 + 128] = counts.astype(bf16)
-        return carry
-
-    lax.fori_loop(0, CLASSES // 2, classes, 0, unroll=16)
+
+    def group(g, carry):
+        for i in range(PAIR_STEP):
+            classes(g * PAIR_STEP + i)
+        counts_out(g).start()
+        return carry
+
+    lax.fori_loop(0, GROUPS - 1, group, 0)
 
     for j in range(TERMS, ROWS):
         left_ref[J_BLOCKS - 1, :, (j % J_STEP) * 128 : (j % J_STEP) * 128 + 128] = jnp.zeros((2 * I_ROWS, 128), bf16)
@@ -174,37 +216,56 @@
     def chunk(q, carry):
         copy(q, I_STEP).wait()
         relay(q)
+        for part in range(2):
+            left_out(q, part).start()
         return carry
 
     lax.fori_loop(0, I_FULL, chunk, 0)
     copy(I_FULL, TERMS - I_FULL * I_STEP).wait()
     relay(I_FULL)
+    for part in range(2):
+        left_out(I_FULL, part).start()
+    group(GROUPS - 1, 0)
+    done_ref[...] = jnp.zeros_like(done_ref)
+    for g in range(GROUPS):
+        counts_out(g).wait()
+    for part in range(2):
+        for q in range(I_FULL + 1):
+            left_out(q, part).wait()
 
 
 def prepare(m2l_target, far_source, local_source, operators):
-    vm = pl.BlockSpec(memory_space=VMEM)
+    hbm = pl.BlockSpec(memory_space=pltpu.HBM)
+    counts, left = (CLASSES // 2, SOURCES, 256), (J_BLOCKS, 2 * I_ROWS, J_STEP * CLASSES)
     return pl.pallas_call(
         prepare_kernel,
-        out_shape=[
-            VMEM((CLASSES // 2, SOURCES, 256), bf16),
-            VMEM((J_BLOCKS, 2 * I_ROWS, J_STEP * CLASSES), bf16),
-        ],
-        in_specs=[vm, vm, vm, pl.BlockSpec(memory_space=pl.ANY)],
-        out_specs=[vm, vm],
+        out_shape=[pltpu.HBM(counts, bf16), pltpu.HBM(left, bf16), jax.ShapeDtypeStruct((8, 128), f32)],
+        in_specs=[hbm] * 4,
+        out_specs=[hbm, hbm, pl.BlockSpec(memory_space=VMEM)],
         scratch_shapes=[
+            VMEM(m2l_target.shape, jnp.int32),
+            VMEM(far_source.shape, jnp.int32),
+            VMEM(local_source.shape, jnp.int32),
             VMEM((4, 128, 128), f32),
             VMEM((4, 128, 128), f32),
             VMEM((I_FULL + 1, I_STEP, TERMS_PAD, CLASSES), f32),
+            VMEM(counts, bf16),
+            VMEM(left, bf16),
+            pltpu.SemaphoreType.DMA((3,)),
             pltpu.SemaphoreType.DMA((I_FULL + 1,)),
+            pltpu.SemaphoreType.DMA((GROUPS,)),
+            pltpu.SemaphoreType.DMA((2, I_FULL + 1)),
         ],
-        compiler_params=small(20),
-        cost_estimate=pl.CostEstimate(flops=12 * 10**9, bytes_accessed=14 * 10**6, transcendentals=0),
+        compiler_params=small(48),
+        cost_estimate=pl.CostEstimate(flops=12 * 10**9, bytes_accessed=40 * 10**6, transcendentals=0),
         name="prepare",
-    )(m2l_target, far_source, local_source, operators)
-
-
-def multipole_kernel(recv_ref, slots_ref, mt_ref, post_ref, *rest):
-    exp_refs, (acc_ref, m_ref, rows_ref) = rest[:LEVELS], rest[LEVELS:]
+    )(*map(in_hbm, (m2l_target, far_source, local_source, operators)))
+
+
+def multipole_kernel(recv_ref, slots_hbm, done_ref, mt_ref, post_ref, *rest):
+    exp_refs, (acc_ref, m_ref, rows_ref, slots_ref, sem) = rest[:LEVELS], rest[LEVELS:]
+    slots_copy = pltpu.make_async_copy(slots_hbm, slots_ref, sem)
+    slots_copy.start()
     for a in range(4):
         post_ref[a] = recv_ref[:, a * BODIES : (a + 1) * BODIES].T
 
@@ -239,6 +300,7 @@
         mt_ref[n : n + 1, :] = jnp.sum(acc_ref[n], axis=0, keepdims=True) * NORM[a, b, c]
     m_ref[0] = mt_ref[0:128, :].T
     m_ref[1] = jnp.concatenate([mt_ref[128:ROWS, :], jnp.zeros((256 - ROWS, SLOTS), f32)], axis=0).T
+    slots_copy.wait()
     for level in range(LEVELS):
 
         def row(k, carry):
@@ -252,7 +314,7 @@
             exp_refs[level][:, half * 128 : half * 128 + 128] = rows_ref[half]
 
 
-def multipoles_of(recv, export_slots):
+def multipoles_of(recv, export_slots, after):
     vm = pl.BlockSpec(memory_space=VMEM)
     out = pl.pallas_call(
         multipole_kernel,
@@ -261,16 +323,18 @@
             jax.ShapeDtypeStruct((4, BODIES, SLOTS), f32),
         ]
         + [jax.ShapeDtypeStruct((KEXP, 256), f32)] * LEVELS,
-        in_specs=[vm, pl.BlockSpec(memory_space=SMEM)],
+        in_specs=[vm, pl.BlockSpec(memory_space=pltpu.HBM), vm],
         out_specs=[vm] * (2 + LEVELS),
         scratch_shapes=[
             pltpu.VMEM((TERMS, 8, SLOTS), f32),
             pltpu.VMEM((2, SLOTS, 128), f32),
             pltpu.VMEM((2, KEXP, 128), f32),
+            pltpu.SMEM((LEVELS, 1, KEXP), jnp.int32),
+            pltpu.SemaphoreType.DMA,
         ],
         compiler_params=small(4),
         name="multipoles",
-    )(recv, export_slots.transpose(1, 0, 2))
+    )(recv, in_hbm(export_slots.transpose(1, 0, 2)), after)
     return out[0], out[1], out[2:]
 
 
@@ -447,8 +511,8 @@
     devices = lax.axis_size(axes)
     sent = pack_tiles(owner, positions, masses)
     recv = lax.all_to_all(sent, "sub", split_axis=0, concat_axis=0, tiled=True)
-    counts, left = prepare(m2l_target[0], far_source[0], local_source[0], operators)
-    mt, post, exported = multipoles_of(recv, export_slots)
+    counts, left, done = prepare(m2l_target[0], far_source[0], local_source[0], operators)
+    mt, post, exported = multipoles_of(recv, export_slots, done)
     far = [
         lax.ppermute(rows, axes, [(i, i ^ (1 << level)) for i in range(devices)])
         for level, rows in enumerate(exported)

time: 66.4 us -> 63.4 us (0.955)
  blocking collectives: 12.9 us -> 0 us
  starting transfers between devices: 11.6 us -> 19.1 us
  Pallas kernels: 35.7 us -> 42.5 us
  local copies, waits for them, and re-layouts: 5.65 us -> 1.4 us
    all_to_all x1 -> x0, blocking collectives: 12.9 us -> none  [body(): recv = lax.all_to_all(sent, 'sub', split_axis=0, concat_axis=0, tiled=True)]
    pallas_call x1, Pallas kernels: 10.9 us -> 17.9 us  [prepare(): pl.pallas_call(prepare_kernel, out_shape=[pltpu.HBM(counts, bf16), pltpu....]
    all_to_all x0 -> x1, starting transfers between devices: none -> 5.41 us  [body(): recv = lax.all_to_all(sent, 'sub', split_axis=0, concat_axis=0, tiled=True)]
    unnamed x20 -> x10, local copies, waits for them, and re-layouts: 5.65 us -> 1.4 us
    ppermute x7, starting transfers between devices: 11.6 us -> 13.6 us  [body(): lax.ppermute(rows, axes, [(i, i ^ 1 << level) for i in range(devices)])]
  transfers between devices with their start and end apart: 7 -> 8, of which waited for: 0 -> 0; matrix products, arithmetic and copies ran while one was open for 0% -> 0% of each run, Pallas kernels for 27% -> 40%
where the time goes in v3:
time: 63.4 us; the launch traced here: 63.1 us
  Pallas kernels  42.5 us (67%)
  starting transfers between devices  19.1 us (30%)
  local copies, waits for them, and re-layouts  1.4 us (2%)
    pallas_call x1, Pallas kernels, prepare(): pl.pallas_call(prepare_kernel, out_shape=[pltpu.HBM(counts, bf16), pltpu....  17.9 us
    ppermute x7, starting transfers between devices, body(): lax.ppermute(rows, axes, [(i, i ^ 1 << level) for i in range(devices)])  13.6 us
    pallas_call x1, Pallas kernels, field(): pl.pallas_call(field_kernel, out_shape=jax.ShapeDtypeStruct((SLOTS, 4, BO...  13.6 us
    pallas_call x1, Pallas kernels, near_field(): pl.pallas_call(near_kernel, out_shape=jax.ShapeDtypeStruct((4, BODIES, SL...  7.12 us
    all_to_all x1, starting transfers between devices, body(): recv = lax.all_to_all(sent, 'sub', split_axis=0, concat_axis=0, tiled=True)  5.41 us
    pallas_call x1, Pallas kernels, pack_tiles(): pl.pallas_call(pack_kernel, out_shape=pltpu.HBM((SLOTS, 4 * BODIES), f32)...  2.21 us
    pallas_call x1, Pallas kernels, multipoles_of(): pl.pallas_call(multipole_kernel, out_shape=[jax.ShapeDtypeStruct((ROWS, S...  1.75 us
    unnamed x10, local copies, waits for them, and re-layouts  1.4 us
  transfers between devices with their start and end apart: 8, of which 0 were waited for; matrix products, arithmetic and copies ran while one was open for 0% of the time, Pallas kernels for 40%

profile of v3, /device:TPU:0, one launch (start us, length us, event | category | flops | bytes accessed | tf_op | source)
XLA Modules:
  0.0 63.1 jit_solution(16905913237638950372)
XLA Ops:
  0.0 2.2 %pack.1 = f32[128,512]{1,0:T(8,128)} custom-call(s32[1,64]{1,0:T(1,128)} %bitcast.12, f32[3,64,128]{2,1,0:T(8,128)} %bitcast.10, f32[64,128]{1,0:T(8,128)} %mass_hbm.1), custom_call_target="tpu_custom_call" | custom-call | tf_op jit(solution)/shard_map/pack/pallas_call | solution.py:100
  2.2 5.4 %all-to-all-start = ((f32[8,16,512]{2,1,0:T(8,128)}), f32[8,16,512]{2,1,0:T(8,128)S(1)}, u32[]{:S(2)}, u32[]{:S(2)}) async-start(f32[8,16,512]{2,1,0:T(8,128)} %bitcast.9), calls=%async_computation | async-start | bytes 524288 | tf_op jit(solution)/shard_map/all_to_all | solution.py:513
  7.6 0.0 copy-start
  7.6 0.0 copy-start.1
  7.6 0.0 copy-start.2
  7.7 17.9 %prepare.1 = (bf16[64,352,256]{2,1,0:T(8,128)(2,1)}, bf16[21,352,1024]{2,1,0:T(8,128)(2,1)}, f32[8,128]{1,0:T(8,128)S(1)}) custom-call(s32[8,64,128]{2,1,0:T(8,128)} %bitcast.13, s32[7,64,128]{2,1,0:T(8,128)} %bitcast.14, s32[64,128]{1,0:T(8,128)} %bitcast.15, f32[165,165,128]{2,1,0:T(8,128)} %op_hbm.1), custom_call_target="tpu_custom_call" | custom-call | flops 12000000000 | bytes 40000000 | tf_op jit(solution)/shard_map/prepare/pallas_call | solution.py:240
  25.5 0.0 all-to-all-done
  25.5 1.8 %multipoles.1 = (f32[168,128]{1,0:T(8,128)S(1)}, f32[4,128,128]{2,1,0:T(8,128)S(1)}, f32[32,256]{1,0:T(8,128)S(1)}, f32[32,256]{1,0:T(8,128)S(1)}, f32[32,256]{1...) custom-call(f32[128,512]{1,0:T(8,128)S(1)} %bitcast.8, ...), custom_call_target="tpu_custom_call" | custom-call | tf_op jit(solution)/shard_map/multipoles/pallas_call | solution.py:319
  27.3 0.6 collective-permute-start
  27.9 1.7 %collective-permute-start.1 = (f32[32,256]{1,0:T(8,128)S(1)}, f32[32,256]{1,0:T(8,128)S(1)}, u32[]{:S(2)}, u32[]{:S(2)}) collective-permute-start(f32[32,256]{1,0:T(8,128)S(1)} %get-tuple-element.22), channel_id=1, source_target_pairs={{0,2},{1,3},{2,0},{3,1},{4,6},{5,7},{6,4},{7,5},{8,10},{9,11},{10,... | collective-permute-start | bytes 98312 | tf_op jit(solution)/shard_map/ppermute | solution.py:517
  29.5 2.7 %collective-permute-start.2 = (f32[32,256]{1,0:T(8,128)S(1)}, f32[32,256]{1,0:T(8,128)S(1)}, u32[]{:S(2)}, u32[]{:S(2)}) collective-permute-start(f32[32,256]{1,0:T(8,128)S(1)} %get-tuple-element.23), channel_id=1, source_target_pairs={{0,4},{1,5},{2,6},{3,7},{4,0},{5,1},{6,2},{7,3},{8,12},{9,13},{10,... | collective-permute-start | bytes 98312 | tf_op jit(solution)/shard_map/ppermute | solution.py:517
  32.2 1.5 %collective-permute-start.3 = (f32[32,256]{1,0:T(8,128)S(1)}, f32[32,256]{1,0:T(8,128)S(1)}, u32[]{:S(2)}, u32[]{:S(2)}) collective-permute-start(f32[32,256]{1,0:T(8,128)S(1)} %get-tuple-element.24), channel_id=1, source_target_pairs={{0,8},{1,9},{2,10},{3,11},{4,12},{5,13},{6,14},{7,15},{8,0},{9,1},... | collective-permute-start | bytes 98312 | tf_op jit(solution)/shard_map/ppermute | solution.py:517
  33.7 2.7 %collective-permute-start.4 = (f32[32,256]{1,0:T(8,128)S(1)}, f32[32,256]{1,0:T(8,128)S(1)}, u32[]{:S(2)}, u32[]{:S(2)}) collective-permute-start(f32[32,256]{1,0:T(8,128)S(1)} %get-tuple-element.25), channel_id=1, source_target_pairs={{0,16},{1,17},{2,18},{3,19},{4,20},{5,21},{6,22},{7,23},{8,24},{9,... | collective-permute-start | bytes 98312 | tf_op jit(solution)/shard_map/ppermute | solution.py:517
  36.4 0.0 collective-permute-done.rest_0_
  36.5 1.6 %collective-permute-start.5 = (f32[32,256]{1,0:T(8,128)S(1)}, f32[32,256]{1,0:T(8,128)S(1)}, u32[]{:S(2)}, u32[]{:S(2)}) collective-permute-start(f32[32,256]{1,0:T(8,128)S(1)} %get-tuple-element.26), channel_id=1, source_target_pairs={{0,32},{1,33},{2,34},{3,35},{4,36},{5,37},{6,38},{7,39},{8,40},{9,... | collective-permute-start | bytes 98312 | tf_op jit(solution)/shard_map/ppermute | solution.py:517
  38.0 0.0 collective-permute-done.1.rest_1_
  38.0 2.9 %collective-permute-start.6 = (f32[32,256]{1,0:T(8,128)S(1)}, f32[32,256]{1,0:T(8,128)S(1)}, u32[]{:S(2)}, u32[]{:S(2)}) collective-permute-start(f32[32,256]{1,0:T(8,128)S(1)} %get-tuple-element.27), channel_id=1, source_target_pairs={{0,64},{1,65},{2,66},{3,67},{4,68},{5,69},{6,70},{7,71},{8,72},{9,... | collective-permute-start | bytes 98312 | tf_op jit(solution)/shard_map/ppermute | solution.py:517
  40.9 0.0 copy-done
  40.9 0.0 copy-done.1
  40.9 0.0 copy-done.2
  40.9 0.0 copy-start.3
  40.9 0.0 copy-start.4
  41.0 7.1 %near.1.rest_8_ = f32[4,128,128]{2,1,0:T(8,128)S(1)} custom-call(f32[4,128,128]{2,1,0:T(8,128)S(1)} %get-tuple-element.28.post_ref.rest_7_, s32[1,128]{1,0:T(1,128)S(1)} %copy-done, s32[1,128]{1,0:T(1,128)S(1)} %copy-done.1, s32[1,128]{1,0:T(1,128)S(1)} %copy-done.2), custom_call_target="tpu_custom_call" | custom-call | flops 8000000000 | bytes 1000000 | tf_op jit(solution)/shard_map/near/pallas_call | solution.py:383
  48.1 0.0 collective-permute-done.2.rest_2_
  48.1 0.0 collective-permute-done.3.rest_3_
  48.1 0.0 collective-permute-done.4.rest_4_
  48.1 0.0 collective-permute-done.5.rest_5_
  48.1 0.0 collective-permute-done.6.rest_6_
  48.1 0.0 copy-done.3
  48.1 1.4 %copy-done.4 = bf16[64,352,256]{2,1,0:T(8,128)(2,1)S(1)} copy-done((bf16[64,352,256]{2,1,0:T(8,128)(2,1)S(1)}, bf16[64,352,256]{2,1,0:T(8,128)(2,1)}, u32[]{:S(2)}) %copy-start.4) | copy-done | bytes 11534360
  49.5 13.6 %field.1 = f32[128,4,128]{2,1,0:T(4,128)} custom-call(bf16[64,352,256]{2,1,0:T(8,128)(2,1)S(1)} %copy-done.4, bf16[21,352,1024]{2,1,0:T(8,128)(2,1)S(1)} %copy-done.3, f32[168,128]{1,0:T(8,128)S(1)} %get-tuple-element.20.mt_ref, f32[32,256]{1,0:T(8,128)S(1)} %collective-permute-done.rest_0_, f32[32,256]{1,0:T(8,128)S(1)} %collective-permute-done.1.rest_1_, ...), custom_call_target="tpu_custom_call" | custom-call | flops 40000000000 | bytes 26000000 | tf_op jit(solution)/shard_map/field/pallas_call | solution.py:479
Async XLA Ops:
  2.2 23.3 %all-to-all-start = ((f32[8,16,512]{2,1,0:T(8,128)}), f32[8,16,512]{2,1,0:T(8,128)S(1)}, u32[]{:S(2)}, u32[]{:S(2)}) async-start(f32[8,16,512]{2,1,0:T(8,128)} %bitcast.9), calls=%async_computation | async-start | bytes 524288 | tf_op jit(solution)/shard_map/all_to_all | solution.py:513
  7.6 33.3 %copy-start = (s32[1,128]{1,0:T(1,128)S(1)}, s32[1,128]{1,0:T(1,128)}, u32[]{:S(2)}) copy-start(s32[1,128]{1,0:T(1,128)} %tgt_ref.1) | copy-start | bytes 1540
  7.6 33.3 %copy-start.1 = (s32[1,128]{1,0:T(1,128)S(1)}, s32[1,128]{1,0:T(1,128)}, u32[]{:S(2)}) copy-start(s32[1,128]{1,0:T(1,128)} %src_ref.1) | copy-start | bytes 1540
  7.6 33.3 %copy-start.2 = (s32[1,128]{1,0:T(1,128)S(1)}, s32[1,128]{1,0:T(1,128)}, u32[]{:S(2)}) copy-start(s32[1,128]{1,0:T(1,128)} %off_ref.1) | copy-start | bytes 1540
  27.3 9.2 %collective-permute-start = (f32[32,256]{1,0:T(8,128)S(1)}, f32[32,256]{1,0:T(8,128)S(1)}, u32[]{:S(2)}, u32[]{:S(2)}) collective-permute-start(f32[32,256]{1,0:T(8,128)S(1)} %get-tuple-element.21), channel_id=1, source_target_pairs={{0,1},{1,0},{2,3},{3,2},{4,5},{5,4},{6,7},{7,6},{8,9},{9,8},{10,11... | collective-permute-start | bytes 98312 | tf_op jit(solution)/shard_map/ppermute | solution.py:517
  27.9 10.2 %collective-permute-start.1 = (f32[32,256]{1,0:T(8,128)S(1)}, f32[32,256]{1,0:T(8,128)S(1)}, u32[]{:S(2)}, u32[]{:S(2)}) collective-permute-start(f32[32,256]{1,0:T(8,128)S(1)} %get-tuple-element.22), channel_id=1, source_target_pairs={{0,2},{1,3},{2,0},{3,1},{4,6},{5,7},{6,4},{7,5},{8,10},{9,11},{10,... | collective-permute-start | bytes 98312 | tf_op jit(solution)/shard_map/ppermute | solution.py:517
  29.5 18.5 %collective-permute-start.2 = (f32[32,256]{1,0:T(8,128)S(1)}, f32[32,256]{1,0:T(8,128)S(1)}, u32[]{:S(2)}, u32[]{:S(2)}) collective-permute-start(f32[32,256]{1,0:T(8,128)S(1)} %get-tuple-element.23), channel_id=1, source_target_pairs={{0,4},{1,5},{2,6},{3,7},{4,0},{5,1},{6,2},{7,3},{8,12},{9,13},{10,... | collective-permute-start | bytes 98312 | tf_op jit(solution)/shard_map/ppermute | solution.py:517
  32.2 15.9 %collective-permute-start.3 = (f32[32,256]{1,0:T(8,128)S(1)}, f32[32,256]{1,0:T(8,128)S(1)}, u32[]{:S(2)}, u32[]{:S(2)}) collective-permute-start(f32[32,256]{1,0:T(8,128)S(1)} %get-tuple-element.24), channel_id=1, source_target_pairs={{0,8},{1,9},{2,10},{3,11},{4,12},{5,13},{6,14},{7,15},{8,0},{9,1},... | collective-permute-start | bytes 98312 | tf_op jit(solution)/shard_map/ppermute | solution.py:517
  33.7 14.4 %collective-permute-start.4 = (f32[32,256]{1,0:T(8,128)S(1)}, f32[32,256]{1,0:T(8,128)S(1)}, u32[]{:S(2)}, u32[]{:S(2)}) collective-permute-start(f32[32,256]{1,0:T(8,128)S(1)} %get-tuple-element.25), channel_id=1, source_target_pairs={{0,16},{1,17},{2,18},{3,19},{4,20},{5,21},{6,22},{7,23},{8,24},{9,... | collective-permute-start | bytes 98312 | tf_op jit(solution)/shard_map/ppermute | solution.py:517
  36.5 11.7 %collective-permute-start.5 = (f32[32,256]{1,0:T(8,128)S(1)}, f32[32,256]{1,0:T(8,128)S(1)}, u32[]{:S(2)}, u32[]{:S(2)}) collective-permute-start(f32[32,256]{1,0:T(8,128)S(1)} %get-tuple-element.26), channel_id=1, source_target_pairs={{0,32},{1,33},{2,34},{3,35},{4,36},{5,37},{6,38},{7,39},{8,40},{9,... | collective-permute-start | bytes 98312 | tf_op jit(solution)/shard_map/ppermute | solution.py:517
  38.0 10.1 %collective-permute-start.6 = (f32[32,256]{1,0:T(8,128)S(1)}, f32[32,256]{1,0:T(8,128)S(1)}, u32[]{:S(2)}, u32[]{:S(2)}) collective-permute-start(f32[32,256]{1,0:T(8,128)S(1)} %get-tuple-element.27), channel_id=1, source_target_pairs={{0,64},{1,65},{2,66},{3,67},{4,68},{5,69},{6,70},{7,71},{8,72},{9,... | collective-permute-start | bytes 98312 | tf_op jit(solution)/shard_map/ppermute | solution.py:517
  40.9 7.2 %copy-start.3 = (bf16[21,352,1024]{2,1,0:T(8,128)(2,1)S(1)}, bf16[21,352,1024]{2,1,0:T(8,128)(2,1)}, u32[]{:S(2)}) copy-start(bf16[21,352,1024]{2,1,0:T(8,128)(2,1)} %get-tuple-element.18.left_ref) | copy-start | bytes 45416452
  40.9 8.6 %copy-start.4 = (bf16[64,352,256]{2,1,0:T(8,128)(2,1)S(1)}, bf16[64,352,256]{2,1,0:T(8,128)(2,1)}, u32[]{:S(2)}) copy-start(bf16[64,352,256]{2,1,0:T(8,128)(2,1)} %get-tuple-element.17.counts_ref) | copy-start | bytes 34603012

commit v4 on v3

--- a/solution.py
+++ b/solution.py
@@ -14,6 +14,8 @@
 TERMS_PAD = ROWS
 SOFT = 0.01
 SLOTS = 128
+PEERS = 8
+CAP = SLOTS // PEERS
 BODIES = 128
 KEXP = 32
 LEVELS = 7
@@ -67,7 +69,8 @@
     return jnp.dot(a, b, preferred_element_type=f32, precision=lax.Precision.HIGHEST)
 
 
-def pack_kernel(owner_hbm, pos_hbm, mass_hbm, out_ref, owner_ref, pos_ref, mass_ref, sem, count_ref, *slot_refs):
+def pack_kernel(owner_hbm, pos_hbm, mass_hbm, *rest):
+    out_refs, (owner_ref, pos_ref, mass_ref, sem, count_ref), slot_refs = rest[:PEERS], rest[PEERS:-4], rest[-4:]
     copies = [
         pltpu.make_async_copy(a, b, sem.at[k])
         for k, (a, b) in enumerate(((owner_hbm, owner_ref), (pos_hbm, pos_ref), (mass_hbm, mass_ref)))
@@ -76,8 +79,9 @@
         c.start()
     for r in slot_refs:
         r[...] = jnp.zeros_like(r)
-    for o in range(8):
+    for o in range(PEERS):
         count_ref[o] = 0
+    me = lax.axis_index("sub")
     for c in copies:
         c.wait()
 
@@ -85,29 +89,30 @@
         o = owner_ref[0, i]
         rank = count_ref[o]
         count_ref[o] = rank + 1
-        slot = o * 16 + rank
+        slot = (o ^ me) * CAP + rank
         for a in range(3):
             slot_refs[a][pl.ds(slot, 1), :] = pos_ref[a, pl.ds(i, 1), :]
         slot_refs[3][pl.ds(slot, 1), :] = mass_ref[pl.ds(i, 1), :]
         return carry
 
     lax.fori_loop(0, mass_ref.shape[0], step, 0)
-    for a in range(4):
-        out_ref[:, a * BODIES : (a + 1) * BODIES] = slot_refs[a][...]
+    for k in range(PEERS):
+        for a in range(4):
+            out_refs[k][:, a * BODIES : (a + 1) * BODIES] = slot_refs[a][k * CAP : (k + 1) * CAP, :]
 
 
 def pack_tiles(owner, positions, masses):
     return pl.pallas_call(
         pack_kernel,
-        out_shape=pltpu.HBM((SLOTS, 4 * BODIES), f32),
+        out_shape=[jax.ShapeDtypeStruct((CAP, 4 * BODIES), f32)] * PEERS,
         in_specs=[pl.BlockSpec(memory_space=pltpu.HBM)] * 3,
-        out_specs=pl.BlockSpec(memory_space=VMEM),
+        out_specs=[pl.BlockSpec(memory_space=VMEM)] * PEERS,
         scratch_shapes=[
             pltpu.SMEM((1, owner.shape[0]), jnp.int32),
             VMEM((3, owner.shape[0], BODIES), f32),
             VMEM((owner.shape[0], BODIES), f32),
             pltpu.SemaphoreType.DMA((3,)),
-            pltpu.SMEM((8,), jnp.int32),
+            pltpu.SMEM((PEERS,), jnp.int32),
         ]
         + [VMEM((SLOTS, BODIES), f32)] * 4,
         compiler_params=small(2),
@@ -118,7 +123,6 @@
 I_STEP = 16
 I_FULL = TERMS // I_STEP
 PAIR_STEP = 16
-GROUPS = CLASSES // 2 // PAIR_STEP
 I_ROWS = (I_FULL + 1) * I_STEP
 J_STEP = 8
 PITCH = CLASSES + 1
@@ -126,8 +130,8 @@
 
 
 def prepare_kernel(
-    tgt_hbm, far_hbm, local_hbm, op_hbm, counts_hbm, left_hbm, done_ref,
-    tgt_ref, far_ref, local_ref, tt_ref, st_ref, buf_ref, counts_ref, left_ref, in_sem, sem, counts_sem, left_sem,
+    tgt_hbm, far_hbm, local_hbm, op_hbm, counts_ref, left_ref, done_ref,
+    tgt_ref, far_ref, local_ref, tt_ref, st_ref, buf_ref, in_sem, sem,
 ):
     lists = [
         pltpu.make_async_copy(a, b, in_sem.at[k])
@@ -140,14 +144,6 @@
         return pltpu.make_async_copy(
             op_hbm.at[pl.ds(q * I_STEP, size)], buf_ref.at[q, pl.ds(0, size), pl.ds(0, TERMS)], sem.at[q]
         )
-
-    def counts_out(g):
-        pairs = pl.ds(g * PAIR_STEP, PAIR_STEP)
-        return pltpu.make_async_copy(counts_ref.at[pairs], counts_hbm.at[pairs], counts_sem.at[g])
-
-    def left_out(q, part):
-        rows = pl.ds(pl.multiple_of(part * I_ROWS + q * I_STEP, I_STEP), I_STEP)
-        return pltpu.make_async_copy(left_ref.at[:, rows], left_hbm.at[:, rows], left_sem.at[part, q])
 
     for q in range(I_FULL):
         copy(q, I_STEP).start()
@@ -195,11 +191,9 @@
     def group(g, carry):
         for i in range(PAIR_STEP):
             classes(g * PAIR_STEP + i)
-        counts_out(g).start()
-        return carry
-
-    lax.fori_loop(0, GROUPS - 1, group, 0)
-
+        return carry
+
+    lax.fori_loop(0, CLASSES // 2 // PAIR_STEP, group, 0)
     for j in range(TERMS, ROWS):
         left_ref[J_BLOCKS - 1, :, (j % J_STEP) * 128 : (j % J_STEP) * 128 + 128] = jnp.zeros((2 * I_ROWS, 128), bf16)
 
@@ -216,22 +210,12 @@
     def chunk(q, carry):
         copy(q, I_STEP).wait()
         relay(q)
-        for part in range(2):
-            left_out(q, part).start()
         return carry
 
     lax.fori_loop(0, I_FULL, chunk, 0)
     copy(I_FULL, TERMS - I_FULL * I_STEP).wait()
     relay(I_FULL)
-    for part in range(2):
-        left_out(I_FULL, part).start()
-    group(GROUPS - 1, 0)
     done_ref[...] = jnp.zeros_like(done_ref)
-    for g in range(GROUPS):
-        counts_out(g).wait()
-    for part in range(2):
-        for q in range(I_FULL + 1):
-            left_out(q, part).wait()
 
 
 def prepare(m2l_target, far_source, local_source, operators):
@@ -239,9 +223,9 @@
     counts, left = (CLASSES // 2, SOURCES, 256), (J_BLOCKS, 2 * I_ROWS, J_STEP * CLASSES)
     return pl.pallas_call(
         prepare_kernel,
-        out_shape=[pltpu.HBM(counts, bf16), pltpu.HBM(left, bf16), jax.ShapeDtypeStruct((8, 128), f32)],
+        out_shape=[VMEM(counts, bf16), VMEM(left, bf16), VMEM((8, 128), f32)],
         in_specs=[hbm] * 4,
-        out_specs=[hbm, hbm, pl.BlockSpec(memory_space=VMEM)],
+        out_specs=[pl.BlockSpec(memory_space=VMEM)] * 3,
         scratch_shapes=[
             VMEM(m2l_target.shape, jnp.int32),
             VMEM(far_source.shape, jnp.int32),
@@ -249,25 +233,28 @@
             VMEM((4, 128, 128), f32),
             VMEM((4, 128, 128), f32),
             VMEM((I_FULL + 1, I_STEP, TERMS_PAD, CLASSES), f32),
-            VMEM(counts, bf16),
-            VMEM(left, bf16),
             pltpu.SemaphoreType.DMA((3,)),
             pltpu.SemaphoreType.DMA((I_FULL + 1,)),
-            pltpu.SemaphoreType.DMA((GROUPS,)),
-            pltpu.SemaphoreType.DMA((2, I_FULL + 1)),
         ],
-        compiler_params=small(48),
-        cost_estimate=pl.CostEstimate(flops=12 * 10**9, bytes_accessed=40 * 10**6, transcendentals=0),
+        compiler_params=small(20),
+        cost_estimate=pl.CostEstimate(flops=12 * 10**9, bytes_accessed=14 * 10**6, transcendentals=0),
         name="prepare",
     )(*map(in_hbm, (m2l_target, far_source, local_source, operators)))
 
 
-def multipole_kernel(recv_ref, slots_hbm, done_ref, mt_ref, post_ref, *rest):
-    exp_refs, (acc_ref, m_ref, rows_ref, slots_ref, sem) = rest[:LEVELS], rest[LEVELS:]
+def multipole_kernel(*refs):
+    pieces, refs = refs[:PEERS], refs[PEERS:]
+    slots_hbm, _, mt_ref, post_ref, *refs = refs
+    exp_refs, (acc_ref, m_ref, rows_ref, slots_ref, sem, recv_ref) = refs[:LEVELS], refs[LEVELS:]
     slots_copy = pltpu.make_async_copy(slots_hbm, slots_ref, sem)
     slots_copy.start()
+    me = lax.axis_index("sub")
+    for k in range(PEERS):
+        rows = pl.ds(pl.multiple_of((me ^ k) * CAP, CAP), CAP)
+        for a in range(4):
+            recv_ref[a, rows, :] = pieces[k][:, a * BODIES : (a + 1) * BODIES]
     for a in range(4):
-        post_ref[a] = recv_ref[:, a * BODIES : (a + 1) * BODIES].T
+        post_ref[a] = recv_ref[a].T
 
     acc_ref[...] = jnp.zeros_like(acc_ref)
 
@@ -314,7 +301,7 @@
             exp_refs[level][:, half * 128 : half * 128 + 128] = rows_ref[half]
 
 
-def multipoles_of(recv, export_slots, after):
+def multipoles_of(pieces, export_slots, after):
     vm = pl.BlockSpec(memory_space=VMEM)
     out = pl.pallas_call(
         multipole_kernel,
@@ -323,7 +310,7 @@
             jax.ShapeDtypeStruct((4, BODIES, SLOTS), f32),
         ]
         + [jax.ShapeDtypeStruct((KEXP, 256), f32)] * LEVELS,
-        in_specs=[vm, pl.BlockSpec(memory_space=pltpu.HBM), vm],
+        in_specs=[vm] * PEERS + [pl.BlockSpec(memory_space=pltpu.HBM), vm],
         out_specs=[vm] * (2 + LEVELS),
         scratch_shapes=[
             pltpu.VMEM((TERMS, 8, SLOTS), f32),
@@ -331,10 +318,11 @@
             pltpu.VMEM((2, KEXP, 128), f32),
             pltpu.SMEM((LEVELS, 1, KEXP), jnp.int32),
             pltpu.SemaphoreType.DMA,
+            VMEM((4, SLOTS, BODIES), f32),
         ],
         compiler_params=small(4),
         name="multipoles",
-    )(recv, in_hbm(export_slots.transpose(1, 0, 2)), after)
+    )(*pieces, in_hbm(export_slots.transpose(1, 0, 2)), after)
     return out[0], out[1], out[2:]
 
 
@@ -509,10 +497,12 @@
 ):
     axes = ("dom", "sub")
     devices = lax.axis_size(axes)
-    sent = pack_tiles(owner, positions, masses)
-    recv = lax.all_to_all(sent, "sub", split_axis=0, concat_axis=0, tiled=True)
+    pieces = pack_tiles(owner, positions, masses)
+    pieces = list(pieces[:1]) + [
+        lax.ppermute(pieces[k], "sub", [(i, i ^ k) for i in range(PEERS)]) for k in range(1, PEERS)
+    ]
     counts, left, done = prepare(m2l_target[0], far_source[0], local_source[0], operators)
-    mt, post, exported = multipoles_of(recv, export_slots, done)
+    mt, post, exported = multipoles_of(pieces, export_slots, done)
     far = [
         lax.ppermute(rows, axes, [(i, i ^ (1 << level)) for i in range(devices)])
         for level, rows in enumerate(exported)

time: 63.4 us -> 62.7 us (0.989)
  starting transfers between devices: 19.1 us -> 22.9 us
  Pallas kernels: 42.5 us -> 39.5 us
  local copies, waits for them, and re-layouts: 1.4 us -> 0.01 us
    ppermute x0 -> x7, starting transfers between devices: none -> 9.41 us  [body(): lax.ppermute(pieces[k], 'sub', [(i, i ^ k) for i in range(PEERS)])]
    all_to_all x1 -> x0, starting transfers between devices: 5.41 us -> none  [body(): recv = lax.all_to_all(sent, 'sub', split_axis=0, concat_axis=0, tiled=True)]
    pallas_call x2, Pallas kernels: 20.1 us -> 17.3 us  [the longest x1 15.8 us: prepare(): pl.pallas_call(prepare_kernel, out_shape=[VMEM(counts, bf16), VMEM(left,...]
    unnamed x10 -> x6, local copies, waits for them, and re-layouts: 1.4 us -> 0.01 us
  transfers between devices with their start and end apart: 8 -> 14, of which waited for: 0 -> 0; matrix products, arithmetic and copies ran while one was open for 0% -> 0% of each run, Pallas kernels for 40% -> 37%
where the time goes in v4:
time: 62.7 us; the launch traced here: 62.6 us
  Pallas kernels  39.5 us (63%)
  starting transfers between devices  22.9 us (37%)
    pallas_call x1, Pallas kernels, prepare(): pl.pallas_call(prepare_kernel, out_shape=[VMEM(counts, bf16), VMEM(left,...  15.8 us
    ppermute x7, starting transfers between devices, body(): lax.ppermute(rows, axes, [(i, i ^ 1 << level) for i in range(devices)])  13.5 us
    pallas_call x1, Pallas kernels, field(): pl.pallas_call(field_kernel, out_shape=jax.ShapeDtypeStruct((SLOTS, 4, BO...  13.3 us
    ppermute x7, starting transfers between devices, body(): lax.ppermute(pieces[k], 'sub', [(i, i ^ k) for i in range(PEERS)])  9.41 us
    pallas_call x1, Pallas kernels, near_field(): pl.pallas_call(near_kernel, out_shape=jax.ShapeDtypeStruct((4, BODIES, SL...  7.11 us
    pallas_call x1, Pallas kernels, multipoles_of(): pl.pallas_call(multipole_kernel, out_shape=[jax.ShapeDtypeStruct((ROWS, S...  1.79 us
    pallas_call x1, Pallas kernels, pack_tiles(): pl.pallas_call(pack_kernel, out_shape=[jax.ShapeDtypeStruct((CAP, 4 * BOD...  1.5 us
  transfers between devices with their start and end apart: 14, of which 0 were waited for; matrix products, arithmetic and copies ran while one was open for 0% of the time, Pallas kernels for 37%

profile of v4, /device:TPU:0, one launch (start us, length us, event | category | flops | bytes accessed | tf_op | source)
XLA Modules:
  0.0 62.6 jit_solution(16196622038874176687)
XLA Ops:
  0.0 1.5 %pack.1 = (f32[16,512]{1,0:T(8,128)S(1)}, f32[16,512]{1,0:T(8,128)S(1)}, f32[16,512]{1,0:T(8,128)S(1)}, f32[16,512]{1,0:T(8,128)S(1)}, f32[16,512]{1,0:T(8,128)S...) custom-call(s32[1,64]{1,0:T(1,128)} %bitcast.8, f32[3,64,128]{2,1,0:T(8,128)} %bitcast.6, ...), custom_call_target="tpu_custom_call" | custom-call | tf_op jit(solution)/shard_map/pack/pallas_call | solution.py:105
  1.5 0.1 collective-permute-start
  1.6 2.1 %collective-permute-start.1 = (f32[16,512]{1,0:T(8,128)S(1)}, f32[16,512]{1,0:T(8,128)S(1)}, u32[]{:S(2)}, u32[]{:S(2)}) collective-permute-start(f32[16,512]{1,0:T(8,128)S(1)} %get-tuple-element.29), channel_id=1, source_target_pairs={{0,2},{1,3},{2,0},{3,1},{4,6},{5,7},{6,4},{7,5},{8,10},{9,11},{10,... | collective-permute-start | bytes 98312 | tf_op jit(solution)/shard_map/ppermute | solution.py:502
  3.7 0.1 collective-permute-start.2
  3.7 3.7 %collective-permute-start.3 = (f32[16,512]{1,0:T(8,128)S(1)}, f32[16,512]{1,0:T(8,128)S(1)}, u32[]{:S(2)}, u32[]{:S(2)}) collective-permute-start(f32[16,512]{1,0:T(8,128)S(1)} %get-tuple-element.31), channel_id=1, source_target_pairs={{0,4},{1,5},{2,6},{3,7},{4,0},{5,1},{6,2},{7,3},{8,12},{9,13},{10,... | collective-permute-start | bytes 98312 | tf_op jit(solution)/shard_map/ppermute | solution.py:502
  7.4 0.0 collective-permute-start.4
  7.4 0.0 collective-permute-done.refs_1_
  7.4 3.4 %collective-permute-start.5 = (f32[16,512]{1,0:T(8,128)S(1)}, f32[16,512]{1,0:T(8,128)S(1)}, u32[]{:S(2)}, u32[]{:S(2)}) collective-permute-start(f32[16,512]{1,0:T(8,128)S(1)} %get-tuple-element.33), channel_id=1, source_target_pairs={{0,6},{1,7},{2,4},{3,5},{4,2},{5,3},{6,0},{7,1},{8,14},{9,15},{10,... | collective-permute-start | bytes 98312 | tf_op jit(solution)/shard_map/ppermute | solution.py:502
  10.8 0.0 collective-permute-done.1.refs_2_
  10.8 0.1 collective-permute-start.6
  10.9 15.8 %prepare.1 = (bf16[64,352,256]{2,1,0:T(8,128)(2,1)S(1)}, bf16[21,352,1024]{2,1,0:T(8,128)(2,1)S(1)}, f32[8,128]{1,0:T(8,128)S(1)}) custom-call(s32[8,64,128]{2,1,0:T(8,128)} %bitcast.9, s32[7,64,128]{2,1,0:T(8,128)} %bitcast.10, s32[64,128]{1,0:T(8,128)} %bitcast.11, f32[165,165,128]{2,1,0:T(8,128)} %op_hbm.1), custom_call_target="tpu_custom_call" | custom-call | flops 12000000000 | bytes 14000000 | tf_op jit(solution)/shard_map/prepare/pallas_call | solution.py:224
  26.8 0.0 collective-permute-done.2.refs_3_
  26.8 0.0 collective-permute-done.3.refs_4_
  26.8 0.0 collective-permute-done.4.refs_5_
  26.8 0.0 collective-permute-done.5.refs_6_
  26.8 0.0 collective-permute-done.6.refs_7_
  26.8 1.8 %multipoles.1 = (f32[168,128]{1,0:T(8,128)S(1)}, f32[4,128,128]{2,1,0:T(8,128)S(1)}, f32[32,256]{1,0:T(8,128)S(1)}, f32[32,256]{1,0:T(8,128)S(1)}, f32[32,256]{1...) custom-call(f32[16,512]{1,0:T(8,128)S(1)} %get-tuple-element.27.refs, ...), custom_call_target="tpu_custom_call" | custom-call | tf_op jit(solution)/shard_map/multipoles/pallas_call | solution.py:306
  28.6 0.2 collective-permute-start.7
  28.8 0.0 collective-permute-start.8
  28.8 4.6 %collective-permute-start.9 = (f32[32,256]{1,0:T(8,128)S(1)}, f32[32,256]{1,0:T(8,128)S(1)}, u32[]{:S(2)}, u32[]{:S(2)}) collective-permute-start(f32[32,256]{1,0:T(8,128)S(1)} %get-tuple-element.39), channel_id=1, source_target_pairs={{0,4},{1,5},{2,6},{3,7},{4,0},{5,1},{6,2},{7,3},{8,12},{9,13},{10,... | collective-permute-start | bytes 98312 | tf_op jit(solution)/shard_map/ppermute | solution.py:507
  33.4 1.5 %collective-permute-start.10 = (f32[32,256]{1,0:T(8,128)S(1)}, f32[32,256]{1,0:T(8,128)S(1)}, u32[]{:S(2)}, u32[]{:S(2)}) collective-permute-start(f32[32,256]{1,0:T(8,128)S(1)} %get-tuple-element.40), channel_id=1, source_target_pairs={{0,8},{1,9},{2,10},{3,11},{4,12},{5,13},{6,14},{7,15},{8,0},{9,1},... | collective-permute-start | bytes 98312 | tf_op jit(solution)/shard_map/ppermute | solution.py:507
  34.9 2.7 %collective-permute-start.11 = (f32[32,256]{1,0:T(8,128)S(1)}, f32[32,256]{1,0:T(8,128)S(1)}, u32[]{:S(2)}, u32[]{:S(2)}) collective-permute-start(f32[32,256]{1,0:T(8,128)S(1)} %get-tuple-element.41), channel_id=1, source_target_pairs={{0,16},{1,17},{2,18},{3,19},{4,20},{5,21},{6,22},{7,23},{8,24},{9,... | collective-permute-start | bytes 98312 | tf_op jit(solution)/shard_map/ppermute | solution.py:507
  37.6 0.0 collective-permute-done.7.rest_0_
  37.6 1.6 %collective-permute-start.12 = (f32[32,256]{1,0:T(8,128)S(1)}, f32[32,256]{1,0:T(8,128)S(1)}, u32[]{:S(2)}, u32[]{:S(2)}) collective-permute-start(f32[32,256]{1,0:T(8,128)S(1)} %get-tuple-element.42), channel_id=1, source_target_pairs={{0,32},{1,33},{2,34},{3,35},{4,36},{5,37},{6,38},{7,39},{8,40},{9,... | collective-permute-start | bytes 98312 | tf_op jit(solution)/shard_map/ppermute | solution.py:507
  39.2 0.0 collective-permute-done.8.rest_1_
  39.2 2.9 %collective-permute-start.13 = (f32[32,256]{1,0:T(8,128)S(1)}, f32[32,256]{1,0:T(8,128)S(1)}, u32[]{:S(2)}, u32[]{:S(2)}) collective-permute-start(f32[32,256]{1,0:T(8,128)S(1)} %get-tuple-element.43), channel_id=1, source_target_pairs={{0,64},{1,65},{2,66},{3,67},{4,68},{5,69},{6,70},{7,71},{8,72},{9,... | collective-permute-start | bytes 98312 | tf_op jit(solution)/shard_map/ppermute | solution.py:507
  42.1 7.1 %near.1.rest_8_ = f32[4,128,128]{2,1,0:T(8,128)S(1)} custom-call(f32[4,128,128]{2,1,0:T(8,128)S(1)} %get-tuple-element.44.post_ref.rest_7_, s32[1,128]{1,0:T(1,128)S(1)} %copy-done, s32[1,128]{1,0:T(1,128)S(1)} %copy-done.1, s32[1,128]{1,0:T(1,128)S(1)} %copy-done.2), custom_call_target="tpu_custom_call" | custom-call | flops 8000000000 | bytes 1000000 | tf_op jit(solution)/shard_map/near/pallas_call | solution.py:371
  49.2 0.0 collective-permute-done.9.rest_2_
  49.3 0.0 collective-permute-done.10.rest_3_
  49.3 0.0 collective-permute-done.11.rest_4_
  49.3 0.0 collective-permute-done.12.rest_5_
  49.3 13.3 %field.1 = f32[128,4,128]{2,1,0:T(4,128)} custom-call(bf16[64,352,256]{2,1,0:T(8,128)(2,1)S(1)} %get-tuple-element.25.counts_ref, bf16[21,352,1024]{2,1,0:T(8,128)(2,1)S(1)} %get-tuple-element.26.left_ref, f32[168,128]{1,0:T(8,128)S(1)} %get-tuple-element.36.mt_ref, f32[32,256]{1,0:T(8,128)S(1)} %collective-permute-done.7.rest_0_, ...), custom_call_target="tpu_custom_call" | custom-call | flops 40000000000 | bytes 26000000 | tf_op jit(solution)/shard_map/field/pallas_call | solution.py:467
  (7 shorter events, 0.0 us)
Async XLA Ops:
  1.5 5.9 %collective-permute-start = (f32[16,512]{1,0:T(8,128)S(1)}, f32[16,512]{1,0:T(8,128)S(1)}, u32[]{:S(2)}, u32[]{:S(2)}) collective-permute-start(f32[16,512]{1,0:T(8,128)S(1)} %get-tuple-element.28), channel_id=1, source_target_pairs={{0,1},{1,0},{2,3},{3,2},{4,5},{5,4},{6,7},{7,6},{8,9},{9,8},{10,11... | collective-permute-start | bytes 98312 | tf_op jit(solution)/shard_map/ppermute | solution.py:502
  1.6 9.2 %collective-permute-start.1 = (f32[16,512]{1,0:T(8,128)S(1)}, f32[16,512]{1,0:T(8,128)S(1)}, u32[]{:S(2)}, u32[]{:S(2)}) collective-permute-start(f32[16,512]{1,0:T(8,128)S(1)} %get-tuple-element.29), channel_id=1, source_target_pairs={{0,2},{1,3},{2,0},{3,1},{4,6},{5,7},{6,4},{7,5},{8,10},{9,11},{10,... | collective-permute-start | bytes 98312 | tf_op jit(solution)/shard_map/ppermute | solution.py:502
  3.7 23.1 %collective-permute-start.2 = (f32[16,512]{1,0:T(8,128)S(1)}, f32[16,512]{1,0:T(8,128)S(1)}, u32[]{:S(2)}, u32[]{:S(2)}) collective-permute-start(f32[16,512]{1,0:T(8,128)S(1)} %get-tuple-element.30), channel_id=1, source_target_pairs={{0,3},{1,2},{2,1},{3,0},{4,7},{5,6},{6,5},{7,4},{8,11},{9,10},{10,... | collective-permute-start | bytes 98312 | tf_op jit(solution)/shard_map/ppermute | solution.py:502
  3.7 23.1 %collective-permute-start.3 = (f32[16,512]{1,0:T(8,128)S(1)}, f32[16,512]{1,0:T(8,128)S(1)}, u32[]{:S(2)}, u32[]{:S(2)}) collective-permute-start(f32[16,512]{1,0:T(8,128)S(1)} %get-tuple-element.31), channel_id=1, source_target_pairs={{0,4},{1,5},{2,6},{3,7},{4,0},{5,1},{6,2},{7,3},{8,12},{9,13},{10,... | collective-permute-start | bytes 98312 | tf_op jit(solution)/shard_map/ppermute | solution.py:502
  7.4 19.4 %collective-permute-start.4 = (f32[16,512]{1,0:T(8,128)S(1)}, f32[16,512]{1,0:T(8,128)S(1)}, u32[]{:S(2)}, u32[]{:S(2)}) collective-permute-start(f32[16,512]{1,0:T(8,128)S(1)} %get-tuple-element.32), channel_id=1, source_target_pairs={{0,5},{1,4},{2,7},{3,6},{4,1},{5,0},{6,3},{7,2},{8,13},{9,12},{10,... | collective-permute-start | bytes 98312 | tf_op jit(solution)/shard_map/ppermute | solution.py:502
  7.4 19.4 %collective-permute-start.5 = (f32[16,512]{1,0:T(8,128)S(1)}, f32[16,512]{1,0:T(8,128)S(1)}, u32[]{:S(2)}, u32[]{:S(2)}) collective-permute-start(f32[16,512]{1,0:T(8,128)S(1)} %get-tuple-element.33), channel_id=1, source_target_pairs={{0,6},{1,7},{2,4},{3,5},{4,2},{5,3},{6,0},{7,1},{8,14},{9,15},{10,... | collective-permute-start | bytes 98312 | tf_op jit(solution)/shard_map/ppermute | solution.py:502
  10.8 16.0 %collective-permute-start.6 = (f32[16,512]{1,0:T(8,128)S(1)}, f32[16,512]{1,0:T(8,128)S(1)}, u32[]{:S(2)}, u32[]{:S(2)}) collective-permute-start(f32[16,512]{1,0:T(8,128)S(1)} %get-tuple-element.34), channel_id=1, source_target_pairs={{0,7},{1,6},{2,5},{3,4},{4,3},{5,2},{6,1},{7,0},{8,15},{9,14},{10,... | collective-permute-start | bytes 98312 | tf_op jit(solution)/shard_map/ppermute | solution.py:502
  10.9 31.2 %copy-start = (s32[1,128]{1,0:T(1,128)S(1)}, s32[1,128]{1,0:T(1,128)}, u32[]{:S(2)}) copy-start(s32[1,128]{1,0:T(1,128)} %tgt_ref.1) | copy-start | bytes 1540
  10.9 31.2 %copy-start.1 = (s32[1,128]{1,0:T(1,128)S(1)}, s32[1,128]{1,0:T(1,128)}, u32[]{:S(2)}) copy-start(s32[1,128]{1,0:T(1,128)} %src_ref.1) | copy-start | bytes 1540
  10.9 31.2 %copy-start.2 = (s32[1,128]{1,0:T(1,128)S(1)}, s32[1,128]{1,0:T(1,128)}, u32[]{:S(2)}) copy-start(s32[1,128]{1,0:T(1,128)} %off_ref.1) | copy-start | bytes 1540
  28.6 9.0 %collective-permute-start.7 = (f32[32,256]{1,0:T(8,128)S(1)}, f32[32,256]{1,0:T(8,128)S(1)}, u32[]{:S(2)}, u32[]{:S(2)}) collective-permute-start(f32[32,256]{1,0:T(8,128)S(1)} %get-tuple-element.37), channel_id=1, source_target_pairs={{0,1},{1,0},{2,3},{3,2},{4,5},{5,4},{6,7},{7,6},{8,9},{9,8},{10,11... | collective-permute-start | bytes 98312 | tf_op jit(solution)/shard_map/ppermute | solution.py:507
  28.8 10.4 %collective-permute-start.8 = (f32[32,256]{1,0:T(8,128)S(1)}, f32[32,256]{1,0:T(8,128)S(1)}, u32[]{:S(2)}, u32[]{:S(2)}) collective-permute-start(f32[32,256]{1,0:T(8,128)S(1)} %get-tuple-element.38), channel_id=1, source_target_pairs={{0,2},{1,3},{2,0},{3,1},{4,6},{5,7},{6,4},{7,5},{8,10},{9,11},{10,... | collective-permute-start | bytes 98312 | tf_op jit(solution)/shard_map/ppermute | solution.py:507
  28.8 20.4 %collective-permute-start.9 = (f32[32,256]{1,0:T(8,128)S(1)}, f32[32,256]{1,0:T(8,128)S(1)}, u32[]{:S(2)}, u32[]{:S(2)}) collective-permute-start(f32[32,256]{1,0:T(8,128)S(1)} %get-tuple-element.39), channel_id=1, source_target_pairs={{0,4},{1,5},{2,6},{3,7},{4,0},{5,1},{6,2},{7,3},{8,12},{9,13},{10,... | collective-permute-start | bytes 98312 | tf_op jit(solution)/shard_map/ppermute | solution.py:507
  33.4 15.9 %collective-permute-start.10 = (f32[32,256]{1,0:T(8,128)S(1)}, f32[32,256]{1,0:T(8,128)S(1)}, u32[]{:S(2)}, u32[]{:S(2)}) collective-permute-start(f32[32,256]{1,0:T(8,128)S(1)} %get-tuple-element.40), channel_id=1, source_target_pairs={{0,8},{1,9},{2,10},{3,11},{4,12},{5,13},{6,14},{7,15},{8,0},{9,1},... | collective-permute-start | bytes 98312 | tf_op jit(solution)/shard_map/ppermute | solution.py:507
  34.9 14.4 %collective-permute-start.11 = (f32[32,256]{1,0:T(8,128)S(1)}, f32[32,256]{1,0:T(8,128)S(1)}, u32[]{:S(2)}, u32[]{:S(2)}) collective-permute-start(f32[32,256]{1,0:T(8,128)S(1)} %get-tuple-element.41), channel_id=1, source_target_pairs={{0,16},{1,17},{2,18},{3,19},{4,20},{5,21},{6,22},{7,23},{8,24},{9,... | collective-permute-start | bytes 98312 | tf_op jit(solution)/shard_map/ppermute | solution.py:507
  37.6 11.7 %collective-permute-start.12 = (f32[32,256]{1,0:T(8,128)S(1)}, f32[32,256]{1,0:T(8,128)S(1)}, u32[]{:S(2)}, u32[]{:S(2)}) collective-permute-start(f32[32,256]{1,0:T(8,128)S(1)} %get-tuple-element.42), channel_id=1, source_target_pairs={{0,32},{1,33},{2,34},{3,35},{4,36},{5,37},{6,38},{7,39},{8,40},{9,... | collective-permute-start | bytes 98312 | tf_op jit(solution)/shard_map/ppermute | solution.py:507
  39.2 10.1 %collective-permute-start.13 = (f32[32,256]{1,0:T(8,128)S(1)}, f32[32,256]{1,0:T(8,128)S(1)}, u32[]{:S(2)}, u32[]{:S(2)}) collective-permute-start(f32[32,256]{1,0:T(8,128)S(1)} %get-tuple-element.43), channel_id=1, source_target_pairs={{0,64},{1,65},{2,66},{3,67},{4,68},{5,69},{6,70},{7,71},{8,72},{9,... | collective-permute-start | bytes 98312 | tf_op jit(solution)/shard_map/ppermute | solution.py:507

commit v5 on v4

--- a/solution.py
+++ b/solution.py
@@ -23,6 +23,7 @@
 SOURCES = SLOTS + LEVELS * KEXP
 f32 = jnp.float32
 bf16 = jnp.bfloat16
+f8 = jnp.float8_e4m3fn
 VMEM = pltpu.VMEM
 SMEM = pltpu.SMEM
 
@@ -65,17 +66,27 @@
     return lax.dot_general(a, b, (((1,), (1,)), ((), ())), preferred_element_type=f32)
 
 
-def dot_exact(a, b):
-    return jnp.dot(a, b, preferred_element_type=f32, precision=lax.Precision.HIGHEST)
-
-
-def pack_kernel(owner_hbm, pos_hbm, mass_hbm, *rest):
+def dot_parts(a, b):
+    high = a.astype(bf16).astype(f32)
+    rest = a - high
+    middle = rest.astype(bf16).astype(f32)
+    parts = dot(jnp.concatenate([high, middle, rest - middle], axis=0).astype(bf16), b)
+    n = a.shape[0]
+    return (parts[2 * n :] + parts[n : 2 * n]) + parts[:n]
+
+
+def pack_kernel(owner_hbm, pos_hbm, mass_hbm, tgt_hbm, far_hbm, local_hbm, *rest):
+    list_refs, rest = rest[:3], rest[3:]
     out_refs, (owner_ref, pos_ref, mass_ref, sem, count_ref), slot_refs = rest[:PEERS], rest[PEERS:-4], rest[-4:]
     copies = [
         pltpu.make_async_copy(a, b, sem.at[k])
         for k, (a, b) in enumerate(((owner_hbm, owner_ref), (pos_hbm, pos_ref), (mass_hbm, mass_ref)))
     ]
-    for c in copies:
+    lists = [
+        pltpu.make_async_copy(a, b, sem.at[3 + k])
+        for k, (a, b) in enumerate(zip((tgt_hbm, far_hbm, local_hbm), list_refs))
+    ]
+    for c in copies + lists:
         c.start()
     for r in slot_refs:
         r[...] = jnp.zeros_like(r)
@@ -99,30 +110,34 @@
     for k in range(PEERS):
         for a in range(4):
             out_refs[k][:, a * BODIES : (a + 1) * BODIES] = slot_refs[a][k * CAP : (k + 1) * CAP, :]
-
-
-def pack_tiles(owner, positions, masses):
-    return pl.pallas_call(
+    for c in lists:
+        c.wait()
+
+
+def pack_tiles(owner, positions, masses, lists):
+    out = pl.pallas_call(
         pack_kernel,
-        out_shape=[jax.ShapeDtypeStruct((CAP, 4 * BODIES), f32)] * PEERS,
-        in_specs=[pl.BlockSpec(memory_space=pltpu.HBM)] * 3,
-        out_specs=[pl.BlockSpec(memory_space=VMEM)] * PEERS,
+        out_shape=[VMEM(x.shape, x.dtype) for x in lists]
+        + [jax.ShapeDtypeStruct((CAP, 4 * BODIES), f32)] * PEERS,
+        in_specs=[pl.BlockSpec(memory_space=pltpu.HBM)] * 6,
+        out_specs=[pl.BlockSpec(memory_space=VMEM)] * (3 + PEERS),
         scratch_shapes=[
             pltpu.SMEM((1, owner.shape[0]), jnp.int32),
             VMEM((3, owner.shape[0], BODIES), f32),
             VMEM((owner.shape[0], BODIES), f32),
-            pltpu.SemaphoreType.DMA((3,)),
+            pltpu.SemaphoreType.DMA((6,)),
             pltpu.SMEM((PEERS,), jnp.int32),
         ]
         + [VMEM((SLOTS, BODIES), f32)] * 4,
         compiler_params=small(2),
         name="pack",
-    )(*map(in_hbm, (owner.T, positions.transpose(1, 0, 2), masses)))
+    )(*map(in_hbm, (owner.T, positions.transpose(1, 0, 2), masses, *lists)))
+    return out[:3], list(out[3:])
 
 
 I_STEP = 16
 I_FULL = TERMS // I_STEP
-PAIR_STEP = 16
+PAIR_STEP = 32
 I_ROWS = (I_FULL + 1) * I_STEP
 J_STEP = 8
 PITCH = CLASSES + 1
@@ -130,16 +145,8 @@
 
 
 def prepare_kernel(
-    tgt_hbm, far_hbm, local_hbm, op_hbm, counts_ref, left_ref, done_ref,
-    tgt_ref, far_ref, local_ref, tt_ref, st_ref, buf_ref, in_sem, sem,
+    tgt_ref, far_ref, local_ref, op_hbm, counts_ref, left_ref, done_ref, tt_ref, st_ref, buf_ref, sem
 ):
-    lists = [
-        pltpu.make_async_copy(a, b, in_sem.at[k])
-        for k, (a, b) in enumerate(((tgt_hbm, tgt_ref), (far_hbm, far_ref), (local_hbm, local_ref)))
-    ]
-    for c in lists:
-        c.start()
-
     def copy(q, size):
         return pltpu.make_async_copy(
             op_hbm.at[pl.ds(q * I_STEP, size)], buf_ref.at[q, pl.ds(0, size), pl.ds(0, TERMS)], sem.at[q]
@@ -148,8 +155,6 @@
     for q in range(I_FULL):
         copy(q, I_STEP).start()
     copy(I_FULL, TERMS - I_FULL * I_STEP).start()
-    for c in lists:
-        c.wait()
 
     order = [7, 0, 1, 2, 3, 4, 5, 6]
     for pair in range(4):
@@ -185,7 +190,7 @@
                     ],
                     axis=1,
                 )
-                counts = dot_nt(source, target)
+                counts = dot_nt(source.astype(f8), target.astype(f8))
                 counts_ref[p, first : first + size, k * 128 : k * 128 + 128] = counts.astype(bf16)
 
     def group(g, carry):
@@ -219,27 +224,23 @@
 
 
 def prepare(m2l_target, far_source, local_source, operators):
-    hbm = pl.BlockSpec(memory_space=pltpu.HBM)
+    vm = pl.BlockSpec(memory_space=VMEM)
     counts, left = (CLASSES // 2, SOURCES, 256), (J_BLOCKS, 2 * I_ROWS, J_STEP * CLASSES)
     return pl.pallas_call(
         prepare_kernel,
         out_shape=[VMEM(counts, bf16), VMEM(left, bf16), VMEM((8, 128), f32)],
-        in_specs=[hbm] * 4,
-        out_specs=[pl.BlockSpec(memory_space=VMEM)] * 3,
+        in_specs=[vm] * 3 + [pl.BlockSpec(memory_space=pltpu.HBM)],
+        out_specs=[vm] * 3,
         scratch_shapes=[
-            VMEM(m2l_target.shape, jnp.int32),
-            VMEM(far_source.shape, jnp.int32),
-            VMEM(local_source.shape, jnp.int32),
             VMEM((4, 128, 128), f32),
             VMEM((4, 128, 128), f32),
             VMEM((I_FULL + 1, I_STEP, TERMS_PAD, CLASSES), f32),
-            pltpu.SemaphoreType.DMA((3,)),
             pltpu.SemaphoreType.DMA((I_FULL + 1,)),
         ],
         compiler_params=small(20),
         cost_estimate=pl.CostEstimate(flops=12 * 10**9, bytes_accessed=14 * 10**6, transcendentals=0),
         name="prepare",
-    )(*map(in_hbm, (m2l_target, far_source, local_source, operators)))
+    )(m2l_target, far_source, local_source, in_hbm(operators))
 
 
 def multipole_kernel(*refs):
@@ -336,10 +337,13 @@
     k = k - 9.0 * kx
     ky = jnp.where(k >= 3.0, one, zero) + jnp.where(k >= 6.0, one, zero)
     kz = k - 3.0 * ky
-    for a, shift in enumerate((kx, ky, kz)):
-        s_ref[a] = dot_exact(post_ref[a], pick_s) + 2.0 * (shift - 1.0)
-        t_ref[a] = dot_exact(post_ref[a], pick_t)
-    s_ref[3] = dot_exact(post_ref[3], pick_s)
+    picks = jnp.concatenate([pick_s, pick_t], axis=1).astype(bf16)
+    shifts = (kx, ky, kz)
+    for a in range(4):
+        picked = dot_parts(post_ref[a], picks)
+        s_ref[a] = picked[:, 0:128] + 2.0 * (shifts[a] - 1.0) if a < 3 else picked[:, 0:128]
+        if a < 3:
+            t_ref[a] = picked[:, 128:256]
 
     def chunk(q, carry):
         rows = pl.ds(pl.multiple_of(q * 32, 32), 32)
@@ -355,15 +359,15 @@
             w = w * (inv * inv)
             return p, ax + rx * w, ay + ry * w, az + rz * w
 
-        done = lax.fori_loop(0, 128, source, (jnp.zeros((32, 128), f32),) * 4, unroll=8)
+        done = lax.fori_loop(0, 128, source, (jnp.zeros((32, 128), f32),) * 4, unroll=32)
         for a in range(4):
             a_ref[a, rows, :] = done[a]
         return carry
 
     lax.fori_loop(0, 4, chunk, 0)
-    into = pick_t.T
+    into = pick_t.T.astype(bf16)
     for a in range(4):
-        near_ref[a] = dot_exact(a_ref[a], into)
+        near_ref[a] = dot_parts(a_ref[a], into)
 
 
 def near_field(post, target, source, offset):
@@ -392,12 +396,12 @@
         parts.append(jnp.concatenate([block[:, 0:128].T, block[:, 128:256].T[0 : ROWS - 128]], axis=0))
     sources = jnp.concatenate(parts, axis=1)
     high = sources.astype(bf16).astype(f32)
-    both = jnp.concatenate([high, sources - high], axis=0).astype(bf16)
-    src_ref[...] = both[:, 0:SOURCES]
+    high, low = high.astype(bf16), (sources - high).astype(bf16)
+    src_ref[...] = jnp.concatenate([high, low], axis=1)
 
     def move(p, carry):
-        moved = dot(src_ref[...], counts_ref[p])
-        moved = moved[0:ROWS] + moved[ROWS : 2 * ROWS]
+        counts = counts_ref[p]
+        moved = dot(src_ref[...], jnp.concatenate([counts, jnp.zeros((32, 256), bf16), counts, jnp.zeros((32, 256), bf16)], axis=0))
         for k in range(2):
             bt_ref[pl.ds(2 * p + k, ROWS, stride=PITCH), :] = moved[:, k * 128 : k * 128 + 128]
         return carry
@@ -470,7 +474,7 @@
         in_specs=[vm] * (5 + LEVELS),
         out_specs=vm,
         scratch_shapes=[
-            VMEM((2 * ROWS, SOURCES), bf16),
+            VMEM((ROWS, 768), bf16),
             VMEM((ROWS * PITCH, SLOTS), f32),
             VMEM((2 * I_ROWS, 256), f32),
             VMEM((ROWS, SLOTS), f32),
@@ -497,11 +501,11 @@
 ):
     axes = ("dom", "sub")
     devices = lax.axis_size(axes)
-    pieces = pack_tiles(owner, positions, masses)
-    pieces = list(pieces[:1]) + [
+    lists, pieces = pack_tiles(owner, positions, masses, (m2l_target[0], far_source[0], local_source[0]))
+    pieces = pieces[:1] + [
         lax.ppermute(pieces[k], "sub", [(i, i ^ k) for i in range(PEERS)]) for k in range(1, PEERS)
     ]
-    counts, left, done = prepare(m2l_target[0], far_source[0], local_source[0], operators)
+    counts, left, done = prepare(*lists, operators)
     mt, post, exported = multipoles_of(pieces, export_slots, done)
     far = [
         lax.ppermute(rows, axes, [(i, i ^ (1 << level)) for i in range(devices)])

time: 62.7 us -> 53.1 us (0.85)
  Pallas kernels: 39.5 us -> 29.9 us
    pallas_call x1, Pallas kernels: 15.8 us -> 8.13 us  [prepare(): pl.pallas_call(prepare_kernel, out_shape=[VMEM(counts, bf16), VMEM(left,...]
    pallas_call x1, Pallas kernels: 13.3 us -> 12.1 us  [field(): pl.pallas_call(field_kernel, out_shape=jax.ShapeDtypeStruct((SLOTS, 4, BO...]
    pallas_call x1, Pallas kernels: 7.11 us -> 6.31 us  [near_field(): pl.pallas_call(near_kernel, out_shape=jax.ShapeDtypeStruct((4, BODIES, SL...]
  transfers between devices with their start and end apart: 14 -> 14, of which waited for: 0 -> 0; matrix products, arithmetic and copies ran while one was open for 0% -> 0% of each run, Pallas kernels for 37% -> 27%
where the time goes in v5:
time: 53.1 us; the launch traced here: 53 us
  Pallas kernels  29.9 us (56%)
  starting transfers between devices  22.9 us (43%)
    ppermute x7, starting transfers between devices, body(): lax.ppermute(rows, axes, [(i, i ^ 1 << level) for i in range(devices)])  13.5 us
    pallas_call x1, Pallas kernels, field(): pl.pallas_call(field_kernel, out_shape=jax.ShapeDtypeStruct((SLOTS, 4, BO...  12.1 us
    ppermute x7, starting transfers between devices, body(): lax.ppermute(pieces[k], 'sub', [(i, i ^ k) for i in range(PEERS)])  9.42 us
    pallas_call x1, Pallas kernels, prepare(): pl.pallas_call(prepare_kernel, out_shape=[VMEM(counts, bf16), VMEM(left,...  8.13 us
    pallas_call x1, Pallas kernels, near_field(): pl.pallas_call(near_kernel, out_shape=jax.ShapeDtypeStruct((4, BODIES, SL...  6.31 us
    pallas_call x1, Pallas kernels, multipoles_of(): pl.pallas_call(multipole_kernel, out_shape=[jax.ShapeDtypeStruct((ROWS, S...  1.79 us
    pallas_call x1, Pallas kernels, pack_tiles(): pl.pallas_call(pack_kernel, out_shape=[VMEM(x.shape, x.dtype) for x in li...  1.53 us
  transfers between devices with their start and end apart: 14, of which 0 were waited for; matrix products, arithmetic and copies ran while one was open for 0% of the time, Pallas kernels for 27%

profile of v5, /device:TPU:0, one launch (start us, length us, event | category | flops | bytes accessed | tf_op | source)
XLA Modules:
  0.0 53.0 jit_solution(11126743792150729032)
XLA Ops:
  0.0 1.5 %pack.1 = (s32[8,64,128]{2,1,0:T(8,128)S(1)}, s32[7,64,128]{2,1,0:T(8,128)S(1)}, s32[64,128]{1,0:T(8,128)S(1)}, f32[16,512]{1,0:T(8,128)S(1)}, f32[16,512]{1,0:T...) custom-call(s32[1,64]{1,0:T(1,128)} %bitcast.11, ...), custom_call_target="tpu_custom_call" | custom-call | tf_op jit(solution)/shard_map/pack/pallas_call | solution.py:118
  1.5 0.1 collective-permute-start
  1.6 2.1 %collective-permute-start.1 = (f32[16,512]{1,0:T(8,128)S(1)}, f32[16,512]{1,0:T(8,128)S(1)}, u32[]{:S(2)}, u32[]{:S(2)}) collective-permute-start(f32[16,512]{1,0:T(8,128)S(1)} %get-tuple-element.35), channel_id=1, source_target_pairs={{0,2},{1,3},{2,0},{3,1},{4,6},{5,7},{6,4},{7,5},{8,10},{9,11},{10,... | collective-permute-start | bytes 98312 | tf_op jit(solution)/shard_map/ppermute | solution.py:506
  3.7 0.1 collective-permute-start.2
  3.8 3.7 %collective-permute-start.3 = (f32[16,512]{1,0:T(8,128)S(1)}, f32[16,512]{1,0:T(8,128)S(1)}, u32[]{:S(2)}, u32[]{:S(2)}) collective-permute-start(f32[16,512]{1,0:T(8,128)S(1)} %get-tuple-element.37), channel_id=1, source_target_pairs={{0,4},{1,5},{2,6},{3,7},{4,0},{5,1},{6,2},{7,3},{8,12},{9,13},{10,... | collective-permute-start | bytes 98312 | tf_op jit(solution)/shard_map/ppermute | solution.py:506
  7.5 0.0 collective-permute-start.4
  7.5 0.0 collective-permute-done.refs_1_
  7.5 3.4 %collective-permute-start.5 = (f32[16,512]{1,0:T(8,128)S(1)}, f32[16,512]{1,0:T(8,128)S(1)}, u32[]{:S(2)}, u32[]{:S(2)}) collective-permute-start(f32[16,512]{1,0:T(8,128)S(1)} %get-tuple-element.39), channel_id=1, source_target_pairs={{0,6},{1,7},{2,4},{3,5},{4,2},{5,3},{6,0},{7,1},{8,14},{9,15},{10,... | collective-permute-start | bytes 98312 | tf_op jit(solution)/shard_map/ppermute | solution.py:506
  10.8 0.0 collective-permute-done.1.refs_2_
  10.8 0.1 collective-permute-start.6
  11.0 8.1 %prepare.1 = (bf16[64,352,256]{2,1,0:T(8,128)(2,1)S(1)}, bf16[21,352,1024]{2,1,0:T(8,128)(2,1)S(1)}, f32[8,128]{1,0:T(8,128)S(1)}) custom-call(s32[8,64,128]{2,1,0:T(8,128)S(1)} %get-tuple-element.28.tgt_ref, s32[7,64,128]{2,1,0:T(8,128)S(1)} %get-tuple-element.29.far_ref, s32[64,128]{1,0:T(8,128)S(1)} %get-tuple-element.30.local_ref, f32[165,165,128]{2,1,0:T(8,128)} %op_hbm.1), custom_call_target="tpu_custom_call" | custom-call | flops 12000000000 | bytes 14000000 | tf_op jit(solution)/shard_map/prepare/pallas_call | solution.py:229
  19.1 0.0 collective-permute-done.2.refs_3_
  19.1 0.0 collective-permute-done.3.refs_4_
  19.1 0.0 collective-permute-done.4.refs_5_
  19.1 0.0 collective-permute-done.5.refs_6_
  19.2 0.0 collective-permute-done.6.refs_7_
  19.2 1.8 %multipoles.1 = (f32[168,128]{1,0:T(8,128)S(1)}, f32[4,128,128]{2,1,0:T(8,128)S(1)}, f32[32,256]{1,0:T(8,128)S(1)}, f32[32,256]{1,0:T(8,128)S(1)}, f32[32,256]{1...) custom-call(f32[16,512]{1,0:T(8,128)S(1)} %get-tuple-element.33.refs, ...), custom_call_target="tpu_custom_call" | custom-call | tf_op jit(solution)/shard_map/multipoles/pallas_call | solution.py:307
  21.0 0.2 collective-permute-start.7
  21.1 0.0 collective-permute-start.8
  21.2 4.6 %collective-permute-start.9 = (f32[32,256]{1,0:T(8,128)S(1)}, f32[32,256]{1,0:T(8,128)S(1)}, u32[]{:S(2)}, u32[]{:S(2)}) collective-permute-start(f32[32,256]{1,0:T(8,128)S(1)} %get-tuple-element.45), channel_id=1, source_target_pairs={{0,4},{1,5},{2,6},{3,7},{4,0},{5,1},{6,2},{7,3},{8,12},{9,13},{10,... | collective-permute-start | bytes 98312 | tf_op jit(solution)/shard_map/ppermute | solution.py:511
  25.7 1.5 %collective-permute-start.10 = (f32[32,256]{1,0:T(8,128)S(1)}, f32[32,256]{1,0:T(8,128)S(1)}, u32[]{:S(2)}, u32[]{:S(2)}) collective-permute-start(f32[32,256]{1,0:T(8,128)S(1)} %get-tuple-element.46), channel_id=1, source_target_pairs={{0,8},{1,9},{2,10},{3,11},{4,12},{5,13},{6,14},{7,15},{8,0},{9,1},... | collective-permute-start | bytes 98312 | tf_op jit(solution)/shard_map/ppermute | solution.py:511
  27.2 2.7 %collective-permute-start.11 = (f32[32,256]{1,0:T(8,128)S(1)}, f32[32,256]{1,0:T(8,128)S(1)}, u32[]{:S(2)}, u32[]{:S(2)}) collective-permute-start(f32[32,256]{1,0:T(8,128)S(1)} %get-tuple-element.47), channel_id=1, source_target_pairs={{0,16},{1,17},{2,18},{3,19},{4,20},{5,21},{6,22},{7,23},{8,24},{9,... | collective-permute-start | bytes 98312 | tf_op jit(solution)/shard_map/ppermute | solution.py:511
  29.9 0.0 collective-permute-done.7.rest_0_
  30.0 1.6 %collective-permute-start.12 = (f32[32,256]{1,0:T(8,128)S(1)}, f32[32,256]{1,0:T(8,128)S(1)}, u32[]{:S(2)}, u32[]{:S(2)}) collective-permute-start(f32[32,256]{1,0:T(8,128)S(1)} %get-tuple-element.48), channel_id=1, source_target_pairs={{0,32},{1,33},{2,34},{3,35},{4,36},{5,37},{6,38},{7,39},{8,40},{9,... | collective-permute-start | bytes 98312 | tf_op jit(solution)/shard_map/ppermute | solution.py:511
  31.5 0.0 collective-permute-done.8.rest_1_
  31.5 2.9 %collective-permute-start.13 = (f32[32,256]{1,0:T(8,128)S(1)}, f32[32,256]{1,0:T(8,128)S(1)}, u32[]{:S(2)}, u32[]{:S(2)}) collective-permute-start(f32[32,256]{1,0:T(8,128)S(1)} %get-tuple-element.49), channel_id=1, source_target_pairs={{0,64},{1,65},{2,66},{3,67},{4,68},{5,69},{6,70},{7,71},{8,72},{9,... | collective-permute-start | bytes 98312 | tf_op jit(solution)/shard_map/ppermute | solution.py:511
  34.4 6.3 %near.1.rest_8_ = f32[4,128,128]{2,1,0:T(8,128)S(1)} custom-call(f32[4,128,128]{2,1,0:T(8,128)S(1)} %get-tuple-element.50.post_ref.rest_7_, s32[1,128]{1,0:T(1,128)S(1)} %copy-done, s32[1,128]{1,0:T(1,128)S(1)} %copy-done.1, s32[1,128]{1,0:T(1,128)S(1)} %copy-done.2), custom_call_target="tpu_custom_call" | custom-call | flops 8000000000 | bytes 1000000 | tf_op jit(solution)/shard_map/near/pallas_call | solution.py:375
  40.8 0.0 collective-permute-done.9.rest_2_
  40.8 0.0 collective-permute-done.10.rest_3_
  40.8 0.0 collective-permute-done.11.rest_4_
  40.8 0.0 collective-permute-done.13.rest_6_
  40.8 12.1 %field.1 = f32[128,4,128]{2,1,0:T(4,128)} custom-call(bf16[64,352,256]{2,1,0:T(8,128)(2,1)S(1)} %get-tuple-element.31.counts_ref, bf16[21,352,1024]{2,1,0:T(8,128)(2,1)S(1)} %get-tuple-element.32.left_ref, f32[168,128]{1,0:T(8,128)S(1)} %get-tuple-element.42.mt_ref, f32[32,256]{1,0:T(8,128)S(1)} %collective-permute-done.7.rest_0_, ...), custom_call_target="tpu_custom_call" | custom-call | flops 40000000000 | bytes 26000000 | tf_op jit(solution)/shard_map/field/pallas_call | solution.py:471
  (7 shorter events, 0.0 us)
Async XLA Ops:
  1.5 5.9 %collective-permute-start = (f32[16,512]{1,0:T(8,128)S(1)}, f32[16,512]{1,0:T(8,128)S(1)}, u32[]{:S(2)}, u32[]{:S(2)}) collective-permute-start(f32[16,512]{1,0:T(8,128)S(1)} %get-tuple-element.34), channel_id=1, source_target_pairs={{0,1},{1,0},{2,3},{3,2},{4,5},{5,4},{6,7},{7,6},{8,9},{9,8},{10,11... | collective-permute-start | bytes 98312 | tf_op jit(solution)/shard_map/ppermute | solution.py:506
  1.6 9.2 %collective-permute-start.1 = (f32[16,512]{1,0:T(8,128)S(1)}, f32[16,512]{1,0:T(8,128)S(1)}, u32[]{:S(2)}, u32[]{:S(2)}) collective-permute-start(f32[16,512]{1,0:T(8,128)S(1)} %get-tuple-element.35), channel_id=1, source_target_pairs={{0,2},{1,3},{2,0},{3,1},{4,6},{5,7},{6,4},{7,5},{8,10},{9,11},{10,... | collective-permute-start | bytes 98312 | tf_op jit(solution)/shard_map/ppermute | solution.py:506
  3.7 15.4 %collective-permute-start.2 = (f32[16,512]{1,0:T(8,128)S(1)}, f32[16,512]{1,0:T(8,128)S(1)}, u32[]{:S(2)}, u32[]{:S(2)}) collective-permute-start(f32[16,512]{1,0:T(8,128)S(1)} %get-tuple-element.36), channel_id=1, source_target_pairs={{0,3},{1,2},{2,1},{3,0},{4,7},{5,6},{6,5},{7,4},{8,11},{9,10},{10,... | collective-permute-start | bytes 98312 | tf_op jit(solution)/shard_map/ppermute | solution.py:506
  3.8 15.4 %collective-permute-start.3 = (f32[16,512]{1,0:T(8,128)S(1)}, f32[16,512]{1,0:T(8,128)S(1)}, u32[]{:S(2)}, u32[]{:S(2)}) collective-permute-start(f32[16,512]{1,0:T(8,128)S(1)} %get-tuple-element.37), channel_id=1, source_target_pairs={{0,4},{1,5},{2,6},{3,7},{4,0},{5,1},{6,2},{7,3},{8,12},{9,13},{10,... | collective-permute-start | bytes 98312 | tf_op jit(solution)/shard_map/ppermute | solution.py:506
  7.5 11.7 %collective-permute-start.4 = (f32[16,512]{1,0:T(8,128)S(1)}, f32[16,512]{1,0:T(8,128)S(1)}, u32[]{:S(2)}, u32[]{:S(2)}) collective-permute-start(f32[16,512]{1,0:T(8,128)S(1)} %get-tuple-element.38), channel_id=1, source_target_pairs={{0,5},{1,4},{2,7},{3,6},{4,1},{5,0},{6,3},{7,2},{8,13},{9,12},{10,... | collective-permute-start | bytes 98312 | tf_op jit(solution)/shard_map/ppermute | solution.py:506
  7.5 11.7 %collective-permute-start.5 = (f32[16,512]{1,0:T(8,128)S(1)}, f32[16,512]{1,0:T(8,128)S(1)}, u32[]{:S(2)}, u32[]{:S(2)}) collective-permute-start(f32[16,512]{1,0:T(8,128)S(1)} %get-tuple-element.39), channel_id=1, source_target_pairs={{0,6},{1,7},{2,4},{3,5},{4,2},{5,3},{6,0},{7,1},{8,14},{9,15},{10,... | collective-permute-start | bytes 98312 | tf_op jit(solution)/shard_map/ppermute | solution.py:506
  10.8 8.3 %collective-permute-start.6 = (f32[16,512]{1,0:T(8,128)S(1)}, f32[16,512]{1,0:T(8,128)S(1)}, u32[]{:S(2)}, u32[]{:S(2)}) collective-permute-start(f32[16,512]{1,0:T(8,128)S(1)} %get-tuple-element.40), channel_id=1, source_target_pairs={{0,7},{1,6},{2,5},{3,4},{4,3},{5,2},{6,1},{7,0},{8,15},{9,14},{10,... | collective-permute-start | bytes 98312 | tf_op jit(solution)/shard_map/ppermute | solution.py:506
  11.0 23.5 %copy-start = (s32[1,128]{1,0:T(1,128)S(1)}, s32[1,128]{1,0:T(1,128)}, u32[]{:S(2)}) copy-start(s32[1,128]{1,0:T(1,128)} %tgt_ref.1) | copy-start | bytes 1540
  11.0 23.5 %copy-start.1 = (s32[1,128]{1,0:T(1,128)S(1)}, s32[1,128]{1,0:T(1,128)}, u32[]{:S(2)}) copy-start(s32[1,128]{1,0:T(1,128)} %src_ref.1) | copy-start | bytes 1540
  11.0 23.5 %copy-start.2 = (s32[1,128]{1,0:T(1,128)S(1)}, s32[1,128]{1,0:T(1,128)}, u32[]{:S(2)}) copy-start(s32[1,128]{1,0:T(1,128)} %off_ref.1) | copy-start | bytes 1540
  21.0 9.0 %collective-permute-start.7 = (f32[32,256]{1,0:T(8,128)S(1)}, f32[32,256]{1,0:T(8,128)S(1)}, u32[]{:S(2)}, u32[]{:S(2)}) collective-permute-start(f32[32,256]{1,0:T(8,128)S(1)} %get-tuple-element.43), channel_id=1, source_target_pairs={{0,1},{1,0},{2,3},{3,2},{4,5},{5,4},{6,7},{7,6},{8,9},{9,8},{10,11... | collective-permute-start | bytes 98312 | tf_op jit(solution)/shard_map/ppermute | solution.py:511
  21.1 10.4 %collective-permute-start.8 = (f32[32,256]{1,0:T(8,128)S(1)}, f32[32,256]{1,0:T(8,128)S(1)}, u32[]{:S(2)}, u32[]{:S(2)}) collective-permute-start(f32[32,256]{1,0:T(8,128)S(1)} %get-tuple-element.44), channel_id=1, source_target_pairs={{0,2},{1,3},{2,0},{3,1},{4,6},{5,7},{6,4},{7,5},{8,10},{9,11},{10,... | collective-permute-start | bytes 98312 | tf_op jit(solution)/shard_map/ppermute | solution.py:511
  21.2 19.6 %collective-permute-start.9 = (f32[32,256]{1,0:T(8,128)S(1)}, f32[32,256]{1,0:T(8,128)S(1)}, u32[]{:S(2)}, u32[]{:S(2)}) collective-permute-start(f32[32,256]{1,0:T(8,128)S(1)} %get-tuple-element.45), channel_id=1, source_target_pairs={{0,4},{1,5},{2,6},{3,7},{4,0},{5,1},{6,2},{7,3},{8,12},{9,13},{10,... | collective-permute-start | bytes 98312 | tf_op jit(solution)/shard_map/ppermute | solution.py:511
  25.7 15.0 %collective-permute-start.10 = (f32[32,256]{1,0:T(8,128)S(1)}, f32[32,256]{1,0:T(8,128)S(1)}, u32[]{:S(2)}, u32[]{:S(2)}) collective-permute-start(f32[32,256]{1,0:T(8,128)S(1)} %get-tuple-element.46), channel_id=1, source_target_pairs={{0,8},{1,9},{2,10},{3,11},{4,12},{5,13},{6,14},{7,15},{8,0},{9,1},... | collective-permute-start | bytes 98312 | tf_op jit(solution)/shard_map/ppermute | solution.py:511
  27.2 13.6 %collective-permute-start.11 = (f32[32,256]{1,0:T(8,128)S(1)}, f32[32,256]{1,0:T(8,128)S(1)}, u32[]{:S(2)}, u32[]{:S(2)}) collective-permute-start(f32[32,256]{1,0:T(8,128)S(1)} %get-tuple-element.47), channel_id=1, source_target_pairs={{0,16},{1,17},{2,18},{3,19},{4,20},{5,21},{6,22},{7,23},{8,24},{9,... | collective-permute-start | bytes 98312 | tf_op jit(solution)/shard_map/ppermute | solution.py:511
  30.0 10.8 %collective-permute-start.12 = (f32[32,256]{1,0:T(8,128)S(1)}, f32[32,256]{1,0:T(8,128)S(1)}, u32[]{:S(2)}, u32[]{:S(2)}) collective-permute-start(f32[32,256]{1,0:T(8,128)S(1)} %get-tuple-element.48), channel_id=1, source_target_pairs={{0,32},{1,33},{2,34},{3,35},{4,36},{5,37},{6,38},{7,39},{8,40},{9,... | collective-permute-start | bytes 98312 | tf_op jit(solution)/shard_map/ppermute | solution.py:511
  31.5 9.3 %collective-permute-start.13 = (f32[32,256]{1,0:T(8,128)S(1)}, f32[32,256]{1,0:T(8,128)S(1)}, u32[]{:S(2)}, u32[]{:S(2)}) collective-permute-start(f32[32,256]{1,0:T(8,128)S(1)} %get-tuple-element.49), channel_id=1, source_target_pairs={{0,64},{1,65},{2,66},{3,67},{4,68},{5,69},{6,70},{7,71},{8,72},{9,... | collective-permute-start | bytes 98312 | tf_op jit(solution)/shard_map/ppermute | solution.py:511

commit v6 on v5

--- a/solution.py
+++ b/solution.py
@@ -77,7 +77,7 @@
 
 def pack_kernel(owner_hbm, pos_hbm, mass_hbm, tgt_hbm, far_hbm, local_hbm, *rest):
     list_refs, rest = rest[:3], rest[3:]
-    out_refs, (owner_ref, pos_ref, mass_ref, sem, count_ref), slot_refs = rest[:PEERS], rest[PEERS:-4], rest[-4:]
+    out_refs, (owner_ref, pos_ref, mass_ref, sem, count_ref), slot_refs = rest[:2], rest[2:-4], rest[-4:]
     copies = [
         pltpu.make_async_copy(a, b, sem.at[k])
         for k, (a, b) in enumerate(((owner_hbm, owner_ref), (pos_hbm, pos_ref), (mass_hbm, mass_ref)))
@@ -107,9 +107,10 @@
         return carry
 
     lax.fori_loop(0, mass_ref.shape[0], step, 0)
-    for k in range(PEERS):
+    half = SLOTS // 2
+    for k in range(2):
         for a in range(4):
-            out_refs[k][:, a * BODIES : (a + 1) * BODIES] = slot_refs[a][k * CAP : (k + 1) * CAP, :]
+            out_refs[k][:, a * BODIES : (a + 1) * BODIES] = slot_refs[a][k * half : (k + 1) * half, :]
     for c in lists:
         c.wait()
 
@@ -118,9 +119,9 @@
     out = pl.pallas_call(
         pack_kernel,
         out_shape=[VMEM(x.shape, x.dtype) for x in lists]
-        + [jax.ShapeDtypeStruct((CAP, 4 * BODIES), f32)] * PEERS,
+        + [jax.ShapeDtypeStruct((SLOTS // 2, 4 * BODIES), f32)] * 2,
         in_specs=[pl.BlockSpec(memory_space=pltpu.HBM)] * 6,
-        out_specs=[pl.BlockSpec(memory_space=VMEM)] * (3 + PEERS),
+        out_specs=[pl.BlockSpec(memory_space=VMEM)] * 5,
         scratch_shapes=[
             pltpu.SMEM((1, owner.shape[0]), jnp.int32),
             VMEM((3, owner.shape[0], BODIES), f32),
@@ -132,7 +133,25 @@
         compiler_params=small(2),
         name="pack",
     )(*map(in_hbm, (owner.T, positions.transpose(1, 0, 2), masses, *lists)))
-    return out[:3], list(out[3:])
+    return out[:3], out[3], out[4]
+
+
+def merge_kernel(mine_ref, other_ref, after_ref, *out_refs):
+    for q, ref in enumerate(out_refs, start=1):
+        ref[0:CAP] = mine_ref[q * CAP : (q + 1) * CAP]
+        ref[CAP : 2 * CAP] = other_ref[q * CAP : (q + 1) * CAP]
+
+
+def merge(mine, other, after):
+    vm = pl.BlockSpec(memory_space=VMEM)
+    return pl.pallas_call(
+        merge_kernel,
+        out_shape=[jax.ShapeDtypeStruct((2 * CAP, 4 * BODIES), f32)] * 3,
+        in_specs=[vm] * 3,
+        out_specs=[vm] * 3,
+        compiler_params=small(2),
+        name="merge",
+    )(mine, other, after)
 
 
 I_STEP = 16
@@ -144,17 +163,16 @@
 J_BLOCKS = ROWS // J_STEP
 
 
-def prepare_kernel(
-    tgt_ref, far_ref, local_ref, op_hbm, counts_ref, left_ref, done_ref, tt_ref, st_ref, buf_ref, sem
-):
-    def copy(q, size):
-        return pltpu.make_async_copy(
-            op_hbm.at[pl.ds(q * I_STEP, size)], buf_ref.at[q, pl.ds(0, size), pl.ds(0, TERMS)], sem.at[q]
-        )
-
-    for q in range(I_FULL):
-        copy(q, I_STEP).start()
-    copy(I_FULL, TERMS - I_FULL * I_STEP).start()
+def operator_copy(op_hbm, buf_ref, sem, q):
+    size = min(I_STEP, TERMS - q * I_STEP)
+    return pltpu.make_async_copy(
+        op_hbm.at[pl.ds(q * I_STEP, size)], buf_ref.at[q, pl.ds(0, size), pl.ds(0, TERMS)], sem.at[q]
+    )
+
+
+def count_kernel(tgt_ref, far_ref, local_ref, op_hbm, counts_ref, buf_ref, done_ref, tt_ref, st_ref, sem):
+    for q in range(I_FULL + 1):
+        operator_copy(op_hbm, buf_ref, sem, q).start()
 
     order = [7, 0, 1, 2, 3, 4, 5, 6]
     for pair in range(4):
@@ -199,10 +217,16 @@
         return carry
 
     lax.fori_loop(0, CLASSES // 2 // PAIR_STEP, group, 0)
+    done_ref[...] = jnp.zeros_like(done_ref)
+    for q in range(I_FULL + 1):
+        operator_copy(op_hbm, buf_ref, sem, q).wait()
+
+
+def relay_kernel(buf_ref, after_ref, left_ref, done_ref):
     for j in range(TERMS, ROWS):
         left_ref[J_BLOCKS - 1, :, (j % J_STEP) * 128 : (j % J_STEP) * 128 + 128] = jnp.zeros((2 * I_ROWS, 128), bf16)
 
-    def relay(q):
+    def relay(q, carry):
         rows = buf_ref.at[q].reshape(I_STEP * TERMS_PAD, CLASSES)
         at = pl.multiple_of(q * I_STEP, I_STEP)
         for j in range(TERMS):
@@ -211,40 +235,49 @@
             lanes = slice((j % J_STEP) * 128, (j % J_STEP) * 128 + 128)
             left_ref[j // J_STEP, pl.ds(at, I_STEP), lanes] = high
             left_ref[j // J_STEP, pl.ds(at + I_ROWS, I_STEP), lanes] = low
-
-    def chunk(q, carry):
-        copy(q, I_STEP).wait()
-        relay(q)
-        return carry
-
-    lax.fori_loop(0, I_FULL, chunk, 0)
-    copy(I_FULL, TERMS - I_FULL * I_STEP).wait()
-    relay(I_FULL)
+        return carry
+
+    lax.fori_loop(0, I_FULL + 1, relay, 0)
     done_ref[...] = jnp.zeros_like(done_ref)
 
 
-def prepare(m2l_target, far_source, local_source, operators):
+def count_pairs(m2l_target, far_source, local_source, operators):
     vm = pl.BlockSpec(memory_space=VMEM)
-    counts, left = (CLASSES // 2, SOURCES, 256), (J_BLOCKS, 2 * I_ROWS, J_STEP * CLASSES)
     return pl.pallas_call(
-        prepare_kernel,
-        out_shape=[VMEM(counts, bf16), VMEM(left, bf16), VMEM((8, 128), f32)],
+        count_kernel,
+        out_shape=[
+            VMEM((CLASSES // 2, SOURCES, 256), bf16),
+            VMEM((I_FULL + 1, I_STEP, TERMS_PAD, CLASSES), f32),
+            VMEM((8, 128), f32),
+        ],
         in_specs=[vm] * 3 + [pl.BlockSpec(memory_space=pltpu.HBM)],
         out_specs=[vm] * 3,
         scratch_shapes=[
             VMEM((4, 128, 128), f32),
             VMEM((4, 128, 128), f32),
-            VMEM((I_FULL + 1, I_STEP, TERMS_PAD, CLASSES), f32),
             pltpu.SemaphoreType.DMA((I_FULL + 1,)),
         ],
-        compiler_params=small(20),
-        cost_estimate=pl.CostEstimate(flops=12 * 10**9, bytes_accessed=14 * 10**6, transcendentals=0),
-        name="prepare",
+        compiler_params=small(4),
+        cost_estimate=pl.CostEstimate(flops=6 * 10**9, bytes_accessed=14 * 10**6, transcendentals=0),
+        name="counts",
     )(m2l_target, far_source, local_source, in_hbm(operators))
 
 
+def relay_operators(rows, after):
+    vm = pl.BlockSpec(memory_space=VMEM)
+    return pl.pallas_call(
+        relay_kernel,
+        out_shape=[VMEM((J_BLOCKS, 2 * I_ROWS, J_STEP * CLASSES), bf16), VMEM((8, 128), f32)],
+        in_specs=[vm] * 2,
+        out_specs=[vm] * 2,
+        compiler_params=small(4),
+        cost_estimate=pl.CostEstimate(flops=4 * 10**9, bytes_accessed=10**6, transcendentals=0),
+        name="relay",
+    )(rows, after)
+
+
 def multipole_kernel(*refs):
-    pieces, refs = refs[:PEERS], refs[PEERS:]
+    (mine_ref, other_ref, *pieces), refs = refs[:5], refs[5:]
     slots_hbm, _, mt_ref, post_ref, *refs = refs
     exp_refs, (acc_ref, m_ref, rows_ref, slots_ref, sem, recv_ref) = refs[:LEVELS], refs[LEVELS:]
     slots_copy = pltpu.make_async_copy(slots_hbm, slots_ref, sem)
@@ -252,8 +285,12 @@
     me = lax.axis_index("sub")
     for k in range(PEERS):
         rows = pl.ds(pl.multiple_of((me ^ k) * CAP, CAP), CAP)
+        if k % 4:
+            piece, first = pieces[k % 4 - 1], k // 4 * CAP
+        else:
+            piece, first = (mine_ref, other_ref)[k // 4], 0
         for a in range(4):
-            recv_ref[a, rows, :] = pieces[k][:, a * BODIES : (a + 1) * BODIES]
+            recv_ref[a, rows, :] = piece[first : first + CAP, a * BODIES : (a + 1) * BODIES]
     for a in range(4):
         post_ref[a] = recv_ref[a].T
 
@@ -311,7 +348,7 @@
             jax.ShapeDtypeStruct((4, BODIES, SLOTS), f32),
         ]
         + [jax.ShapeDtypeStruct((KEXP, 256), f32)] * LEVELS,
-        in_specs=[vm] * PEERS + [pl.BlockSpec(memory_space=pltpu.HBM), vm],
+        in_specs=[vm] * 5 + [pl.BlockSpec(memory_space=pltpu.HBM), vm],
         out_specs=[vm] * (2 + LEVELS),
         scratch_shapes=[
             pltpu.VMEM((TERMS, 8, SLOTS), f32),
@@ -501,12 +538,17 @@
 ):
     axes = ("dom", "sub")
     devices = lax.axis_size(axes)
-    lists, pieces = pack_tiles(owner, positions, masses, (m2l_target[0], far_source[0], local_source[0]))
-    pieces = pieces[:1] + [
-        lax.ppermute(pieces[k], "sub", [(i, i ^ k) for i in range(PEERS)]) for k in range(1, PEERS)
-    ]
-    counts, left, done = prepare(*lists, operators)
-    mt, post, exported = multipoles_of(pieces, export_slots, done)
+    lists, mine, sent = pack_tiles(owner, positions, masses, (m2l_target[0], far_source[0], local_source[0]))
+
+    def swap(rows, k):
+        return lax.ppermute(rows, "sub", [(i, i ^ k) for i in range(PEERS)])
+
+    other = swap(sent, 4)
+    counts, rows, done = count_pairs(*lists, operators)
+    sent = merge(mine, other, done)
+    pieces = [swap(sent[k - 1], k) for k in (1, 2, 3)]
+    left, done = relay_operators(rows, sent[0])
+    mt, post, exported = multipoles_of((mine, other, *pieces), export_slots, done)
     far = [
         lax.ppermute(rows, axes, [(i, i ^ (1 << level)) for i in range(devices)])
         for level, rows in enumerate(exported)

time: 53.1 us -> 49.6 us (0.934)
  starting transfers between devices: 22.9 us -> 18.4 us
  Pallas kernels: 29.9 us -> 30.9 us
    ppermute x7 -> x4, starting transfers between devices: 9.42 us -> 6.26 us  [swap(): return lax.ppermute(rows, 'sub', [(i, i ^ k) for i in range(PEERS)])]
    ppermute x7, starting transfers between devices: 13.5 us -> 12.1 us  [body(): lax.ppermute(rows, axes, [(i, i ^ 1 << level) for i in range(devices)])]
    pallas_call x1 -> x3, Pallas kernels: 8.13 us -> 9 us  [the longest x1 5.08 us: count_pairs(): pl.pallas_call(count_kernel, out_shape=[VMEM((CLASSES // 2, SOURCES, 256)...]
  transfers between devices with their start and end apart: 14 -> 11, of which waited for: 0 -> 0; matrix products, arithmetic and copies ran while one was open for 0% -> 0% of each run, Pallas kernels for 27% -> 31%
where the time goes in v6:
time: 49.6 us; the launch traced here: 49.4 us
  Pallas kernels  30.9 us (62%)
  starting transfers between devices  18.4 us (37%)
    pallas_call x1, Pallas kernels, field(): pl.pallas_call(field_kernel, out_shape=jax.ShapeDtypeStruct((SLOTS, 4, BO...  12.3 us
    ppermute x7, starting transfers between devices, body(): lax.ppermute(rows, axes, [(i, i ^ 1 << level) for i in range(devices)])  12.1 us
    pallas_call x1, Pallas kernels, near_field(): pl.pallas_call(near_kernel, out_shape=jax.ShapeDtypeStruct((4, BODIES, SL...  6.31 us
    ppermute x4, starting transfers between devices, swap(): return lax.ppermute(rows, 'sub', [(i, i ^ k) for i in range(PEERS)])  6.26 us
    pallas_call x1, Pallas kernels, count_pairs(): pl.pallas_call(count_kernel, out_shape=[VMEM((CLASSES // 2, SOURCES, 256)...  5.08 us
    pallas_call x1, Pallas kernels, relay_operators(): pl.pallas_call(relay_kernel, out_shape=[VMEM((J_BLOCKS, 2 * I_ROWS, J_STE...  3.91 us
    pallas_call x1, Pallas kernels, multipoles_of(): pl.pallas_call(multipole_kernel, out_shape=[jax.ShapeDtypeStruct((ROWS, S...  1.78 us
    pallas_call x1, Pallas kernels, pack_tiles(): pl.pallas_call(pack_kernel, out_shape=[VMEM(x.shape, x.dtype) for x in li...  1.53 us
  transfers between devices with their start and end apart: 11, of which 0 were waited for; matrix products, arithmetic and copies ran while one was open for 0% of the time, Pallas kernels for 31%

profile of v6, /device:TPU:0, one launch (start us, length us, event | category | flops | bytes accessed | tf_op | source)
XLA Modules:
  0.0 49.4 jit_solution(6580165260193669523)
XLA Ops:
  0.0 1.5 %pack.1 = (s32[8,64,128]{2,1,0:T(8,128)S(1)}, s32[7,64,128]{2,1,0:T(8,128)S(1)}, s32[64,128]{1,0:T(8,128)S(1)}, f32[64,512]{1,0:T(8,128)S(1)}, f32[64,512]{1,0:T(8,128)S(1)}) custom-call(s32[1,64]{1,0:T(1,128)} %bitcast.11, f32[3,64,128]{2,1,0:T(8,128)} %bitcast.8, f32[64,128]{1,0:T(8,128)} %mass_hbm.1, s32[8,64,128]{2,1,0:T(8,128)} %bitcast.6, ...), custom_call_target="tpu_custom_call" | custom-call | tf_op jit(solution)/shard_map/pack/pallas_call | solution.py:119
  1.5 4.0 %collective-permute-start = (f32[64,512]{1,0:T(8,128)S(1)}, f32[64,512]{1,0:T(8,128)S(1)}, u32[]{:S(2)}, u32[]{:S(2)}) collective-permute-start(f32[64,512]{1,0:T(8,128)S(1)} %get-tuple-element.33), channel_id=1, source_target_pairs={{0,4},{1,5},{2,6},{3,7},{4,0},{5,1},{6,2},{7,3},{8,12},{9,13},{10,... | collective-permute-start | bytes 393224 | tf_op jit(solution)/shard_map/ppermute | solution.py:544
  5.6 0.0 copy-start.1
  5.6 5.1 %counts.1 = (bf16[64,352,256]{2,1,0:T(8,128)(2,1)S(1)}, f32[11,16,168,128]{3,2,1,0:T(8,128)S(1)}, f32[8,128]{1,0:T(8,128)S(1)}) custom-call(s32[8,64,128]{2,1,0:T(8,128)S(1)} %get-tuple-element.27.tgt_ref, s32[7,64,128]{2,1,0:T(8,128)S(1)} %get-tuple-element.28.far_ref, s32[64,128]{1,0:T(8,128)S(1)} %get-tuple-element.29.local_ref, f32[165,165,128]{2,1,0:T(8,128)} %op_hbm.1), custom_call_target="tpu_custom_call" | custom-call | flops 6000000000 | bytes 14000000 | tf_op jit(solution)/shard_map/counts/pallas_call | solution.py:246
  10.7 0.0 collective-permute-done.other_ref.refs_1_
  10.7 1.1 %collective-permute-start.2 = (f32[32,512]{1,0:T(8,128)S(1)}, f32[32,512]{1,0:T(8,128)S(1)}, u32[]{:S(2)}, u32[]{:S(2)}) collective-permute-start(f32[32,512]{1,0:T(8,128)S(1)} %get-tuple-element.37), channel_id=1, source_target_pairs={{0,2},{1,3},{2,0},{3,1},{4,6},{5,7},{6,4},{7,5},{8,10},{9,11},{10,... | collective-permute-start | bytes 196616 | tf_op jit(solution)/shard_map/ppermute | solution.py:544
  11.8 0.0 collective-permute-start.3
  11.8 1.1 %collective-permute-start.1 = (f32[32,512]{1,0:T(8,128)S(1)}, f32[32,512]{1,0:T(8,128)S(1)}, u32[]{:S(2)}, u32[]{:S(2)}) collective-permute-start(f32[32,512]{1,0:T(8,128)S(1)} %get-tuple-element.35.after_ref), channel_id=1, source_target_pairs={{0,1},{1,0},{2,3},{3,2},{4,5},{5,4},{6,7},{7,6},{8,9},{9,8},{10,11... | collective-permute-start | bytes 196616 | tf_op jit(solution)/shard_map/ppermute | solution.py:544
  12.9 3.9 %relay.1 = (bf16[21,352,1024]{2,1,0:T(8,128)(2,1)S(1)}, f32[8,128]{1,0:T(8,128)S(1)}) custom-call(f32[11,16,168,128]{3,2,1,0:T(8,128)S(1)} %get-tuple-element.31.buf_ref, f32[32,512]{1,0:T(8,128)S(1)} %get-tuple-element.35.after_ref), custom_call_target="tpu_custom_call" | custom-call | flops 4000000000 | bytes 1000000 | tf_op jit(solution)/shard_map/relay/pallas_call | solution.py:268
  16.8 0.0 collective-permute-done.2.refs_3_
  16.9 0.0 collective-permute-done.3.refs_4_
  16.9 0.0 collective-permute-done.1.refs_2_
  16.9 1.8 %multipoles.1 = (f32[168,128]{1,0:T(8,128)S(1)}, f32[4,128,128]{2,1,0:T(8,128)S(1)}, f32[32,256]{1,0:T(8,128)S(1)}, f32[32,256]{1,0:T(8,128)S(1)}, f32[32,256]{1...) custom-call(f32[64,512]{1,0:T(8,128)S(1)} %get-tuple-element.32.mine, ...), custom_call_target="tpu_custom_call" | custom-call | tf_op jit(solution)/shard_map/multipoles/pallas_call | solution.py:344
  18.7 0.1 collective-permute-start.4
  18.8 1.1 %collective-permute-start.5 = (f32[32,256]{1,0:T(8,128)S(1)}, f32[32,256]{1,0:T(8,128)S(1)}, u32[]{:S(2)}, u32[]{:S(2)}) collective-permute-start(f32[32,256]{1,0:T(8,128)S(1)} %get-tuple-element.42), channel_id=1, source_target_pairs={{0,2},{1,3},{2,0},{3,1},{4,6},{5,7},{6,4},{7,5},{8,10},{9,11},{10,... | collective-permute-start | bytes 98312 | tf_op jit(solution)/shard_map/ppermute | solution.py:553
  19.9 2.2 %collective-permute-start.6 = (f32[32,256]{1,0:T(8,128)S(1)}, f32[32,256]{1,0:T(8,128)S(1)}, u32[]{:S(2)}, u32[]{:S(2)}) collective-permute-start(f32[32,256]{1,0:T(8,128)S(1)} %get-tuple-element.43), channel_id=1, source_target_pairs={{0,4},{1,5},{2,6},{3,7},{4,0},{5,1},{6,2},{7,3},{8,12},{9,13},{10,... | collective-permute-start | bytes 98312 | tf_op jit(solution)/shard_map/ppermute | solution.py:553
  22.1 1.5 %collective-permute-start.7 = (f32[32,256]{1,0:T(8,128)S(1)}, f32[32,256]{1,0:T(8,128)S(1)}, u32[]{:S(2)}, u32[]{:S(2)}) collective-permute-start(f32[32,256]{1,0:T(8,128)S(1)} %get-tuple-element.44), channel_id=1, source_target_pairs={{0,8},{1,9},{2,10},{3,11},{4,12},{5,13},{6,14},{7,15},{8,0},{9,1},... | collective-permute-start | bytes 98312 | tf_op jit(solution)/shard_map/ppermute | solution.py:553
  23.6 2.7 %collective-permute-start.8 = (f32[32,256]{1,0:T(8,128)S(1)}, f32[32,256]{1,0:T(8,128)S(1)}, u32[]{:S(2)}, u32[]{:S(2)}) collective-permute-start(f32[32,256]{1,0:T(8,128)S(1)} %get-tuple-element.45), channel_id=1, source_target_pairs={{0,16},{1,17},{2,18},{3,19},{4,20},{5,21},{6,22},{7,23},{8,24},{9,... | collective-permute-start | bytes 98312 | tf_op jit(solution)/shard_map/ppermute | solution.py:553
  26.3 0.0 collective-permute-done.4.rest_0_
  26.3 1.6 %collective-permute-start.9 = (f32[32,256]{1,0:T(8,128)S(1)}, f32[32,256]{1,0:T(8,128)S(1)}, u32[]{:S(2)}, u32[]{:S(2)}) collective-permute-start(f32[32,256]{1,0:T(8,128)S(1)} %get-tuple-element.46), channel_id=1, source_target_pairs={{0,32},{1,33},{2,34},{3,35},{4,36},{5,37},{6,38},{7,39},{8,40},{9,... | collective-permute-start | bytes 98312 | tf_op jit(solution)/shard_map/ppermute | solution.py:553
  27.9 0.0 collective-permute-done.5.rest_1_
  27.9 2.9 %collective-permute-start.10 = (f32[32,256]{1,0:T(8,128)S(1)}, f32[32,256]{1,0:T(8,128)S(1)}, u32[]{:S(2)}, u32[]{:S(2)}) collective-permute-start(f32[32,256]{1,0:T(8,128)S(1)} %get-tuple-element.47), channel_id=1, source_target_pairs={{0,64},{1,65},{2,66},{3,67},{4,68},{5,69},{6,70},{7,71},{8,72},{9,... | collective-permute-start | bytes 98312 | tf_op jit(solution)/shard_map/ppermute | solution.py:553
  30.8 0.0 copy-done
  30.8 0.0 copy-done.1
  30.8 0.0 copy-done.2
  30.8 6.3 %near.1.rest_8_ = f32[4,128,128]{2,1,0:T(8,128)S(1)} custom-call(f32[4,128,128]{2,1,0:T(8,128)S(1)} %get-tuple-element.48.post_ref.rest_7_, s32[1,128]{1,0:T(1,128)S(1)} %copy-done, s32[1,128]{1,0:T(1,128)S(1)} %copy-done.1, s32[1,128]{1,0:T(1,128)S(1)} %copy-done.2), custom_call_target="tpu_custom_call" | custom-call | flops 8000000000 | bytes 1000000 | tf_op jit(solution)/shard_map/near/pallas_call | solution.py:412
  37.1 0.0 collective-permute-done.6.rest_2_
  37.1 0.0 collective-permute-done.7.rest_3_
  37.2 0.0 collective-permute-done.8.rest_4_
  37.2 0.0 collective-permute-done.9.rest_5_
  37.2 0.0 collective-permute-done.10.rest_6_
  37.2 12.3 %field.1 = f32[128,4,128]{2,1,0:T(4,128)} custom-call(bf16[64,352,256]{2,1,0:T(8,128)(2,1)S(1)} %get-tuple-element.30.counts_ref, bf16[21,352,1024]{2,1,0:T(8,128)(2,1)S(1)} %get-tuple-element.36.left_ref, f32[168,128]{1,0:T(8,128)S(1)} %get-tuple-element.40.mt_ref, f32[32,256]{1,0:T(8,128)S(1)} %collective-permute-done.4.rest_0_, ...), custom_call_target="tpu_custom_call" | custom-call | flops 40000000000 | bytes 26000000 | tf_op jit(solution)/shard_map/field/pallas_call | solution.py:508
  (3 shorter events, 0.0 us)
Async XLA Ops:
  1.5 9.1 %collective-permute-start = (f32[64,512]{1,0:T(8,128)S(1)}, f32[64,512]{1,0:T(8,128)S(1)}, u32[]{:S(2)}, u32[]{:S(2)}) collective-permute-start(f32[64,512]{1,0:T(8,128)S(1)} %get-tuple-element.33), channel_id=1, source_target_pairs={{0,4},{1,5},{2,6},{3,7},{4,0},{5,1},{6,2},{7,3},{8,12},{9,13},{10,... | collective-permute-start | bytes 393224 | tf_op jit(solution)/shard_map/ppermute | solution.py:544
  5.6 25.2 %copy-start = (s32[1,128]{1,0:T(1,128)S(1)}, s32[1,128]{1,0:T(1,128)}, u32[]{:S(2)}) copy-start(s32[1,128]{1,0:T(1,128)} %tgt_ref.1) | copy-start | bytes 1540
  5.6 25.2 %copy-start.1 = (s32[1,128]{1,0:T(1,128)S(1)}, s32[1,128]{1,0:T(1,128)}, u32[]{:S(2)}) copy-start(s32[1,128]{1,0:T(1,128)} %src_ref.1) | copy-start | bytes 1540
  5.6 25.2 %copy-start.2 = (s32[1,128]{1,0:T(1,128)S(1)}, s32[1,128]{1,0:T(1,128)}, u32[]{:S(2)}) copy-start(s32[1,128]{1,0:T(1,128)} %off_ref.1) | copy-start | bytes 1540
  10.7 6.1 %collective-permute-start.2 = (f32[32,512]{1,0:T(8,128)S(1)}, f32[32,512]{1,0:T(8,128)S(1)}, u32[]{:S(2)}, u32[]{:S(2)}) collective-permute-start(f32[32,512]{1,0:T(8,128)S(1)} %get-tuple-element.37), channel_id=1, source_target_pairs={{0,2},{1,3},{2,0},{3,1},{4,6},{5,7},{6,4},{7,5},{8,10},{9,11},{10,... | collective-permute-start | bytes 196616 | tf_op jit(solution)/shard_map/ppermute | solution.py:544
  11.8 5.1 %collective-permute-start.3 = (f32[32,512]{1,0:T(8,128)S(1)}, f32[32,512]{1,0:T(8,128)S(1)}, u32[]{:S(2)}, u32[]{:S(2)}) collective-permute-start(f32[32,512]{1,0:T(8,128)S(1)} %get-tuple-element.38), channel_id=1, source_target_pairs={{0,3},{1,2},{2,1},{3,0},{4,7},{5,6},{6,5},{7,4},{8,11},{9,10},{10,... | collective-permute-start | bytes 196616 | tf_op jit(solution)/shard_map/ppermute | solution.py:544
  11.8 5.1 %collective-permute-start.1 = (f32[32,512]{1,0:T(8,128)S(1)}, f32[32,512]{1,0:T(8,128)S(1)}, u32[]{:S(2)}, u32[]{:S(2)}) collective-permute-start(f32[32,512]{1,0:T(8,128)S(1)} %get-tuple-element.35.after_ref), channel_id=1, source_target_pairs={{0,1},{1,0},{2,3},{3,2},{4,5},{5,4},{6,7},{7,6},{8,9},{9,8},{10,11... | collective-permute-start | bytes 196616 | tf_op jit(solution)/shard_map/ppermute | solution.py:544
  18.7 7.7 %collective-permute-start.4 = (f32[32,256]{1,0:T(8,128)S(1)}, f32[32,256]{1,0:T(8,128)S(1)}, u32[]{:S(2)}, u32[]{:S(2)}) collective-permute-start(f32[32,256]{1,0:T(8,128)S(1)} %get-tuple-element.41), channel_id=1, source_target_pairs={{0,1},{1,0},{2,3},{3,2},{4,5},{5,4},{6,7},{7,6},{8,9},{9,8},{10,11... | collective-permute-start | bytes 98312 | tf_op jit(solution)/shard_map/ppermute | solution.py:553
  18.8 9.1 %collective-permute-start.5 = (f32[32,256]{1,0:T(8,128)S(1)}, f32[32,256]{1,0:T(8,128)S(1)}, u32[]{:S(2)}, u32[]{:S(2)}) collective-permute-start(f32[32,256]{1,0:T(8,128)S(1)} %get-tuple-element.42), channel_id=1, source_target_pairs={{0,2},{1,3},{2,0},{3,1},{4,6},{5,7},{6,4},{7,5},{8,10},{9,11},{10,... | collective-permute-start | bytes 98312 | tf_op jit(solution)/shard_map/ppermute | solution.py:553
  19.9 17.3 %collective-permute-start.6 = (f32[32,256]{1,0:T(8,128)S(1)}, f32[32,256]{1,0:T(8,128)S(1)}, u32[]{:S(2)}, u32[]{:S(2)}) collective-permute-start(f32[32,256]{1,0:T(8,128)S(1)} %get-tuple-element.43), channel_id=1, source_target_pairs={{0,4},{1,5},{2,6},{3,7},{4,0},{5,1},{6,2},{7,3},{8,12},{9,13},{10,... | collective-permute-start | bytes 98312 | tf_op jit(solution)/shard_map/ppermute | solution.py:553
  22.1 15.0 %collective-permute-start.7 = (f32[32,256]{1,0:T(8,128)S(1)}, f32[32,256]{1,0:T(8,128)S(1)}, u32[]{:S(2)}, u32[]{:S(2)}) collective-permute-start(f32[32,256]{1,0:T(8,128)S(1)} %get-tuple-element.44), channel_id=1, source_target_pairs={{0,8},{1,9},{2,10},{3,11},{4,12},{5,13},{6,14},{7,15},{8,0},{9,1},... | collective-permute-start | bytes 98312 | tf_op jit(solution)/shard_map/ppermute | solution.py:553
  23.6 13.6 %collective-permute-start.8 = (f32[32,256]{1,0:T(8,128)S(1)}, f32[32,256]{1,0:T(8,128)S(1)}, u32[]{:S(2)}, u32[]{:S(2)}) collective-permute-start(f32[32,256]{1,0:T(8,128)S(1)} %get-tuple-element.45), channel_id=1, source_target_pairs={{0,16},{1,17},{2,18},{3,19},{4,20},{5,21},{6,22},{7,23},{8,24},{9,... | collective-permute-start | bytes 98312 | tf_op jit(solution)/shard_map/ppermute | solution.py:553
  26.3 10.8 %collective-permute-start.9 = (f32[32,256]{1,0:T(8,128)S(1)}, f32[32,256]{1,0:T(8,128)S(1)}, u32[]{:S(2)}, u32[]{:S(2)}) collective-permute-start(f32[32,256]{1,0:T(8,128)S(1)} %get-tuple-element.46), channel_id=1, source_target_pairs={{0,32},{1,33},{2,34},{3,35},{4,36},{5,37},{6,38},{7,39},{8,40},{9,... | collective-permute-start | bytes 98312 | tf_op jit(solution)/shard_map/ppermute | solution.py:553
  27.9 9.3 %collective-permute-start.10 = (f32[32,256]{1,0:T(8,128)S(1)}, f32[32,256]{1,0:T(8,128)S(1)}, u32[]{:S(2)}, u32[]{:S(2)}) collective-permute-start(f32[32,256]{1,0:T(8,128)S(1)} %get-tuple-element.47), channel_id=1, source_target_pairs={{0,64},{1,65},{2,66},{3,67},{4,68},{5,69},{6,70},{7,71},{8,72},{9,... | collective-permute-start | bytes 98312 | tf_op jit(solution)/shard_map/ppermute | solution.py:553

commit v7 on v6

--- a/solution.py
+++ b/solution.py
@@ -43,6 +43,10 @@
 
 def small(mib):
     return pltpu.CompilerParams(vmem_limit_bytes=mib * 2**20)
+
+
+def row(ref, n):
+    return jnp.broadcast_to(ref[pl.ds(n, 1), :], (32, 128))
 
 
 def in_hbm(x):
@@ -423,7 +427,7 @@
 
 def field_kernel(counts_ref, left_ref, mt_ref, *rest):
     far_refs, rest = rest[:LEVELS], rest[LEVELS:]
-    post_ref, near_ref, out_ref, src_ref, bt_ref, acc_ref, e_ref, f_ref = rest
+    post_ref, near_ref, norm_ref, out_ref, src_ref, bt_ref, acc_ref, e_ref, f_ref = rest
 
     far = jnp.concatenate([r[...] for r in far_refs], axis=0)
     far = jnp.concatenate([far, jnp.zeros((32, 256), f32)], axis=0)
@@ -443,7 +447,7 @@
             bt_ref[pl.ds(2 * p + k, ROWS, stride=PITCH), :] = moved[:, k * 128 : k * 128 + 128]
         return carry
 
-    lax.fori_loop(0, CLASSES // 2, move, 0, unroll=16)
+    lax.fori_loop(0, CLASSES // 2, move, 0, unroll=64)
 
     acc_ref[...] = jnp.zeros_like(acc_ref)
 
@@ -458,7 +462,7 @@
     lax.fori_loop(0, J_BLOCKS, contract, 0, unroll=21)
     acc = acc_ref[...]
     e = (acc[I_ROWS:, 128:] + acc[I_ROWS:, :128]) + acc[:I_ROWS, 128:] + acc[:I_ROWS, :128]
-    e_ref[...] = e[0:ROWS]
+    e_ref[...] = e[0:ROWS] * norm_ref[...]
 
     present = jnp.where(post_ref[3, 0:1, :] > 0.0, 1.0, 0.0)
 
@@ -467,8 +471,7 @@
         x, y, z = (post_ref[a, rows, :] for a in range(3))
 
         def coef(a, b, c):
-            n = TERM[a, b, c]
-            return jnp.broadcast_to(e_ref[n : n + 1, :] * NORM[a, b, c], (32, SLOTS))
+            return row(e_ref, TERM[a, b, c])
 
         p = px = py = pz = None
         for a in range(ORDER, -1, -1):
@@ -505,10 +508,13 @@
 
 def field(counts, left, mt, far, post, near):
     vm = pl.BlockSpec(memory_space=VMEM)
+    norms = np.zeros((ROWS, SLOTS), np.float32)
+    for t, n in TERM.items():
+        norms[n] = NORM[t]
     return pl.pallas_call(
         field_kernel,
         out_shape=jax.ShapeDtypeStruct((SLOTS, 4, BODIES), f32),
-        in_specs=[vm] * (5 + LEVELS),
+        in_specs=[vm] * (6 + LEVELS),
         out_specs=vm,
         scratch_shapes=[
             VMEM((ROWS, 768), bf16),
@@ -520,7 +526,7 @@
         compiler_params=small(20),
         cost_estimate=pl.CostEstimate(flops=40 * 10**9, bytes_accessed=26 * 10**6, transcendentals=0),
         name="field",
-    )(counts, left, mt, *far, post, near)
+    )(counts, left, mt, *far, post, near, norms)
 
 
 def body(

time: 49.6 us -> 48.7 us (0.982)
  Pallas kernels: 30.9 us -> 30 us
    pallas_call x1, Pallas kernels: 12.3 us -> 11.4 us  [field(): pl.pallas_call(field_kernel, out_shape=jax.ShapeDtypeStruct((SLOTS, 4, BO...]
where the time goes in v7:
time: 48.7 us; the launch traced here: 48.6 us
  Pallas kernels  30 us (62%)
  starting transfers between devices  18.4 us (38%)
    ppermute x7, starting transfers between devices, body(): lax.ppermute(rows, axes, [(i, i ^ 1 << level) for i in range(devices)])  12.1 us
    pallas_call x1, Pallas kernels, field(): pl.pallas_call(field_kernel, out_shape=jax.ShapeDtypeStruct((SLOTS, 4, BO...  11.4 us
    pallas_call x1, Pallas kernels, near_field(): pl.pallas_call(near_kernel, out_shape=jax.ShapeDtypeStruct((4, BODIES, SL...  6.31 us
    ppermute x4, starting transfers between devices, swap(): return lax.ppermute(rows, 'sub', [(i, i ^ k) for i in range(PEERS)])  6.26 us
    pallas_call x1, Pallas kernels, count_pairs(): pl.pallas_call(count_kernel, out_shape=[VMEM((CLASSES // 2, SOURCES, 256)...  5.08 us
    pallas_call x1, Pallas kernels, relay_operators(): pl.pallas_call(relay_kernel, out_shape=[VMEM((J_BLOCKS, 2 * I_ROWS, J_STE...  3.91 us
    pallas_call x1, Pallas kernels, multipoles_of(): pl.pallas_call(multipole_kernel, out_shape=[jax.ShapeDtypeStruct((ROWS, S...  1.78 us
    pallas_call x1, Pallas kernels, pack_tiles(): pl.pallas_call(pack_kernel, out_shape=[VMEM(x.shape, x.dtype) for x in li...  1.53 us
  transfers between devices with their start and end apart: 11, of which 0 were waited for; matrix products, arithmetic and copies ran while one was open for 0% of the time, Pallas kernels for 31%

profile of v7, /device:TPU:0, one launch (start us, length us, event | category | flops | bytes accessed | tf_op | source)
XLA Modules:
  0.0 48.6 jit_solution(15162631264625205136)
XLA Ops:
  0.0 1.5 %pack.1 = (s32[8,64,128]{2,1,0:T(8,128)S(1)}, s32[7,64,128]{2,1,0:T(8,128)S(1)}, s32[64,128]{1,0:T(8,128)S(1)}, f32[64,512]{1,0:T(8,128)S(1)}, f32[64,512]{1,0:T(8,128)S(1)}) custom-call(s32[1,64]{1,0:T(1,128)} %bitcast.11, f32[3,64,128]{2,1,0:T(8,128)} %bitcast.8, f32[64,128]{1,0:T(8,128)} %mass_hbm.1, s32[8,64,128]{2,1,0:T(8,128)} %bitcast.6, ...), custom_call_target="tpu_custom_call" | custom-call | tf_op jit(solution)/shard_map/pack/pallas_call | solution.py:123
  1.5 4.0 %collective-permute-start = (f32[64,512]{1,0:T(8,128)S(1)}, f32[64,512]{1,0:T(8,128)S(1)}, u32[]{:S(2)}, u32[]{:S(2)}) collective-permute-start(f32[64,512]{1,0:T(8,128)S(1)} %get-tuple-element.33), channel_id=1, source_target_pairs={{0,4},{1,5},{2,6},{3,7},{4,0},{5,1},{6,2},{7,3},{8,12},{9,13},{10,... | collective-permute-start | bytes 393224 | tf_op jit(solution)/shard_map/ppermute | solution.py:550
  5.6 5.1 %counts.1 = (bf16[64,352,256]{2,1,0:T(8,128)(2,1)S(1)}, f32[11,16,168,128]{3,2,1,0:T(8,128)S(1)}, f32[8,128]{1,0:T(8,128)S(1)}) custom-call(s32[8,64,128]{2,1,0:T(8,128)S(1)} %get-tuple-element.27.tgt_ref, s32[7,64,128]{2,1,0:T(8,128)S(1)} %get-tuple-element.28.far_ref, s32[64,128]{1,0:T(8,128)S(1)} %get-tuple-element.29.local_ref, f32[165,165,128]{2,1,0:T(8,128)} %op_hbm.1), custom_call_target="tpu_custom_call" | custom-call | flops 6000000000 | bytes 14000000 | tf_op jit(solution)/shard_map/counts/pallas_call | solution.py:250
  10.7 0.0 collective-permute-done.other_ref.refs_1_
  10.7 1.1 %collective-permute-start.2 = (f32[32,512]{1,0:T(8,128)S(1)}, f32[32,512]{1,0:T(8,128)S(1)}, u32[]{:S(2)}, u32[]{:S(2)}) collective-permute-start(f32[32,512]{1,0:T(8,128)S(1)} %get-tuple-element.37), channel_id=1, source_target_pairs={{0,2},{1,3},{2,0},{3,1},{4,6},{5,7},{6,4},{7,5},{8,10},{9,11},{10,... | collective-permute-start | bytes 196616 | tf_op jit(solution)/shard_map/ppermute | solution.py:550
  11.8 0.0 collective-permute-start.3
  11.8 1.1 %collective-permute-start.1 = (f32[32,512]{1,0:T(8,128)S(1)}, f32[32,512]{1,0:T(8,128)S(1)}, u32[]{:S(2)}, u32[]{:S(2)}) collective-permute-start(f32[32,512]{1,0:T(8,128)S(1)} %get-tuple-element.35.after_ref), channel_id=1, source_target_pairs={{0,1},{1,0},{2,3},{3,2},{4,5},{5,4},{6,7},{7,6},{8,9},{9,8},{10,11... | collective-permute-start | bytes 196616 | tf_op jit(solution)/shard_map/ppermute | solution.py:550
  12.9 3.9 %relay.1 = (bf16[21,352,1024]{2,1,0:T(8,128)(2,1)S(1)}, f32[8,128]{1,0:T(8,128)S(1)}) custom-call(f32[11,16,168,128]{3,2,1,0:T(8,128)S(1)} %get-tuple-element.31.buf_ref, f32[32,512]{1,0:T(8,128)S(1)} %get-tuple-element.35.after_ref), custom_call_target="tpu_custom_call" | custom-call | flops 4000000000 | bytes 1000000 | tf_op jit(solution)/shard_map/relay/pallas_call | solution.py:272
  16.8 0.0 copy-start.3
  16.9 0.0 collective-permute-done.2.refs_3_
  16.9 0.0 collective-permute-done.3.refs_4_
  16.9 0.0 collective-permute-done.1.refs_2_
  16.9 1.8 %multipoles.1 = (f32[168,128]{1,0:T(8,128)S(1)}, f32[4,128,128]{2,1,0:T(8,128)S(1)}, f32[32,256]{1,0:T(8,128)S(1)}, f32[32,256]{1,0:T(8,128)S(1)}, f32[32,256]{1...) custom-call(f32[64,512]{1,0:T(8,128)S(1)} %get-tuple-element.32.mine, ...), custom_call_target="tpu_custom_call" | custom-call | tf_op jit(solution)/shard_map/multipoles/pallas_call | solution.py:348
  18.7 0.1 collective-permute-start.4
  18.8 1.1 %collective-permute-start.5 = (f32[32,256]{1,0:T(8,128)S(1)}, f32[32,256]{1,0:T(8,128)S(1)}, u32[]{:S(2)}, u32[]{:S(2)}) collective-permute-start(f32[32,256]{1,0:T(8,128)S(1)} %get-tuple-element.42), channel_id=1, source_target_pairs={{0,2},{1,3},{2,0},{3,1},{4,6},{5,7},{6,4},{7,5},{8,10},{9,11},{10,... | collective-permute-start | bytes 98312 | tf_op jit(solution)/shard_map/ppermute | solution.py:559
  19.9 2.2 %collective-permute-start.6 = (f32[32,256]{1,0:T(8,128)S(1)}, f32[32,256]{1,0:T(8,128)S(1)}, u32[]{:S(2)}, u32[]{:S(2)}) collective-permute-start(f32[32,256]{1,0:T(8,128)S(1)} %get-tuple-element.43), channel_id=1, source_target_pairs={{0,4},{1,5},{2,6},{3,7},{4,0},{5,1},{6,2},{7,3},{8,12},{9,13},{10,... | collective-permute-start | bytes 98312 | tf_op jit(solution)/shard_map/ppermute | solution.py:559
  22.1 1.5 %collective-permute-start.7 = (f32[32,256]{1,0:T(8,128)S(1)}, f32[32,256]{1,0:T(8,128)S(1)}, u32[]{:S(2)}, u32[]{:S(2)}) collective-permute-start(f32[32,256]{1,0:T(8,128)S(1)} %get-tuple-element.44), channel_id=1, source_target_pairs={{0,8},{1,9},{2,10},{3,11},{4,12},{5,13},{6,14},{7,15},{8,0},{9,1},... | collective-permute-start | bytes 98312 | tf_op jit(solution)/shard_map/ppermute | solution.py:559
  23.6 2.7 %collective-permute-start.8 = (f32[32,256]{1,0:T(8,128)S(1)}, f32[32,256]{1,0:T(8,128)S(1)}, u32[]{:S(2)}, u32[]{:S(2)}) collective-permute-start(f32[32,256]{1,0:T(8,128)S(1)} %get-tuple-element.45), channel_id=1, source_target_pairs={{0,16},{1,17},{2,18},{3,19},{4,20},{5,21},{6,22},{7,23},{8,24},{9,... | collective-permute-start | bytes 98312 | tf_op jit(solution)/shard_map/ppermute | solution.py:559
  26.3 0.0 collective-permute-done.4.rest_0_
  26.3 1.6 %collective-permute-start.9 = (f32[32,256]{1,0:T(8,128)S(1)}, f32[32,256]{1,0:T(8,128)S(1)}, u32[]{:S(2)}, u32[]{:S(2)}) collective-permute-start(f32[32,256]{1,0:T(8,128)S(1)} %get-tuple-element.46), channel_id=1, source_target_pairs={{0,32},{1,33},{2,34},{3,35},{4,36},{5,37},{6,38},{7,39},{8,40},{9,... | collective-permute-start | bytes 98312 | tf_op jit(solution)/shard_map/ppermute | solution.py:559
  27.9 0.0 collective-permute-done.5.rest_1_
  27.9 2.9 %collective-permute-start.10 = (f32[32,256]{1,0:T(8,128)S(1)}, f32[32,256]{1,0:T(8,128)S(1)}, u32[]{:S(2)}, u32[]{:S(2)}) collective-permute-start(f32[32,256]{1,0:T(8,128)S(1)} %get-tuple-element.47), channel_id=1, source_target_pairs={{0,64},{1,65},{2,66},{3,67},{4,68},{5,69},{6,70},{7,71},{8,72},{9,... | collective-permute-start | bytes 98312 | tf_op jit(solution)/shard_map/ppermute | solution.py:559
  30.8 0.0 copy-done
  30.8 0.0 copy-done.1
  30.8 0.0 copy-done.2
  30.8 6.3 %near.1.rest_8_ = f32[4,128,128]{2,1,0:T(8,128)S(1)} custom-call(f32[4,128,128]{2,1,0:T(8,128)S(1)} %get-tuple-element.48.post_ref.rest_7_, s32[1,128]{1,0:T(1,128)S(1)} %copy-done, s32[1,128]{1,0:T(1,128)S(1)} %copy-done.1, s32[1,128]{1,0:T(1,128)S(1)} %copy-done.2), custom_call_target="tpu_custom_call" | custom-call | flops 8000000000 | bytes 1000000 | tf_op jit(solution)/shard_map/near/pallas_call | solution.py:416
  37.1 0.0 collective-permute-done.6.rest_2_
  37.2 0.0 collective-permute-done.7.rest_3_
  37.2 0.0 collective-permute-done.8.rest_4_
  37.2 0.0 collective-permute-done.9.rest_5_
  37.2 0.0 collective-permute-done.10.rest_6_
  37.2 11.4 %field.1 = f32[128,4,128]{2,1,0:T(4,128)} custom-call(bf16[64,352,256]{2,1,0:T(8,128)(2,1)S(1)} %get-tuple-element.30.counts_ref, bf16[21,352,1024]{2,1,0:T(8,128)(2,1)S(1)} %get-tuple-element.36.left_ref, f32[168,128]{1,0:T(8,128)S(1)} %get-tuple-element.40.mt_ref, f32[32,256]{1,0:T(8,128)S(1)} %collective-permute-done.4.rest_0_, ...), custom_call_target="tpu_custom_call" | custom-call | flops 40000000000 | bytes 26000000 | tf_op jit(solution)/shard_map/field/pallas_call | solution.py:514
  (5 shorter events, 0.0 us)
Async XLA Ops:
  1.5 9.1 %collective-permute-start = (f32[64,512]{1,0:T(8,128)S(1)}, f32[64,512]{1,0:T(8,128)S(1)}, u32[]{:S(2)}, u32[]{:S(2)}) collective-permute-start(f32[64,512]{1,0:T(8,128)S(1)} %get-tuple-element.33), channel_id=1, source_target_pairs={{0,4},{1,5},{2,6},{3,7},{4,0},{5,1},{6,2},{7,3},{8,12},{9,13},{10,... | collective-permute-start | bytes 393224 | tf_op jit(solution)/shard_map/ppermute | solution.py:550
  5.6 25.2 %copy-start = (s32[1,128]{1,0:T(1,128)S(1)}, s32[1,128]{1,0:T(1,128)}, u32[]{:S(2)}) copy-start(s32[1,128]{1,0:T(1,128)} %tgt_ref.1) | copy-start | bytes 1540
  5.6 25.2 %copy-start.1 = (s32[1,128]{1,0:T(1,128)S(1)}, s32[1,128]{1,0:T(1,128)}, u32[]{:S(2)}) copy-start(s32[1,128]{1,0:T(1,128)} %src_ref.1) | copy-start | bytes 1540
  5.6 25.2 %copy-start.2 = (s32[1,128]{1,0:T(1,128)S(1)}, s32[1,128]{1,0:T(1,128)}, u32[]{:S(2)}) copy-start(s32[1,128]{1,0:T(1,128)} %off_ref.1) | copy-start | bytes 1540
  10.7 6.2 %collective-permute-start.2 = (f32[32,512]{1,0:T(8,128)S(1)}, f32[32,512]{1,0:T(8,128)S(1)}, u32[]{:S(2)}, u32[]{:S(2)}) collective-permute-start(f32[32,512]{1,0:T(8,128)S(1)} %get-tuple-element.37), channel_id=1, source_target_pairs={{0,2},{1,3},{2,0},{3,1},{4,6},{5,7},{6,4},{7,5},{8,10},{9,11},{10,... | collective-permute-start | bytes 196616 | tf_op jit(solution)/shard_map/ppermute | solution.py:550
  11.8 5.1 %collective-permute-start.3 = (f32[32,512]{1,0:T(8,128)S(1)}, f32[32,512]{1,0:T(8,128)S(1)}, u32[]{:S(2)}, u32[]{:S(2)}) collective-permute-start(f32[32,512]{1,0:T(8,128)S(1)} %get-tuple-element.38), channel_id=1, source_target_pairs={{0,3},{1,2},{2,1},{3,0},{4,7},{5,6},{6,5},{7,4},{8,11},{9,10},{10,... | collective-permute-start | bytes 196616 | tf_op jit(solution)/shard_map/ppermute | solution.py:550
  11.8 5.1 %collective-permute-start.1 = (f32[32,512]{1,0:T(8,128)S(1)}, f32[32,512]{1,0:T(8,128)S(1)}, u32[]{:S(2)}, u32[]{:S(2)}) collective-permute-start(f32[32,512]{1,0:T(8,128)S(1)} %get-tuple-element.35.after_ref), channel_id=1, source_target_pairs={{0,1},{1,0},{2,3},{3,2},{4,5},{5,4},{6,7},{7,6},{8,9},{9,8},{10,11... | collective-permute-start | bytes 196616 | tf_op jit(solution)/shard_map/ppermute | solution.py:550
  16.8 20.4 %copy-start.3 = (f32[168,128]{1,0:T(8,128)S(1)}, f32[168,128]{1,0:T(8,128)}, u32[]{:S(2)}) copy-start(f32[168,128]{1,0:T(8,128)} %constant.2.clone.rest_9_) | copy-start | bytes 258052
  18.7 7.7 %collective-permute-start.4 = (f32[32,256]{1,0:T(8,128)S(1)}, f32[32,256]{1,0:T(8,128)S(1)}, u32[]{:S(2)}, u32[]{:S(2)}) collective-permute-start(f32[32,256]{1,0:T(8,128)S(1)} %get-tuple-element.41), channel_id=1, source_target_pairs={{0,1},{1,0},{2,3},{3,2},{4,5},{5,4},{6,7},{7,6},{8,9},{9,8},{10,11... | collective-permute-start | bytes 98312 | tf_op jit(solution)/shard_map/ppermute | solution.py:559
  18.8 9.1 %collective-permute-start.5 = (f32[32,256]{1,0:T(8,128)S(1)}, f32[32,256]{1,0:T(8,128)S(1)}, u32[]{:S(2)}, u32[]{:S(2)}) collective-permute-start(f32[32,256]{1,0:T(8,128)S(1)} %get-tuple-element.42), channel_id=1, source_target_pairs={{0,2},{1,3},{2,0},{3,1},{4,6},{5,7},{6,4},{7,5},{8,10},{9,11},{10,... | collective-permute-start | bytes 98312 | tf_op jit(solution)/shard_map/ppermute | solution.py:559
  19.9 17.3 %collective-permute-start.6 = (f32[32,256]{1,0:T(8,128)S(1)}, f32[32,256]{1,0:T(8,128)S(1)}, u32[]{:S(2)}, u32[]{:S(2)}) collective-permute-start(f32[32,256]{1,0:T(8,128)S(1)} %get-tuple-element.43), channel_id=1, source_target_pairs={{0,4},{1,5},{2,6},{3,7},{4,0},{5,1},{6,2},{7,3},{8,12},{9,13},{10,... | collective-permute-start | bytes 98312 | tf_op jit(solution)/shard_map/ppermute | solution.py:559
  22.1 15.0 %collective-permute-start.7 = (f32[32,256]{1,0:T(8,128)S(1)}, f32[32,256]{1,0:T(8,128)S(1)}, u32[]{:S(2)}, u32[]{:S(2)}) collective-permute-start(f32[32,256]{1,0:T(8,128)S(1)} %get-tuple-element.44), channel_id=1, source_target_pairs={{0,8},{1,9},{2,10},{3,11},{4,12},{5,13},{6,14},{7,15},{8,0},{9,1},... | collective-permute-start | bytes 98312 | tf_op jit(solution)/shard_map/ppermute | solution.py:559
  23.6 13.6 %collective-permute-start.8 = (f32[32,256]{1,0:T(8,128)S(1)}, f32[32,256]{1,0:T(8,128)S(1)}, u32[]{:S(2)}, u32[]{:S(2)}) collective-permute-start(f32[32,256]{1,0:T(8,128)S(1)} %get-tuple-element.45), channel_id=1, source_target_pairs={{0,16},{1,17},{2,18},{3,19},{4,20},{5,21},{6,22},{7,23},{8,24},{9,... | collective-permute-start | bytes 98312 | tf_op jit(solution)/shard_map/ppermute | solution.py:559
  26.3 10.8 %collective-permute-start.9 = (f32[32,256]{1,0:T(8,128)S(1)}, f32[32,256]{1,0:T(8,128)S(1)}, u32[]{:S(2)}, u32[]{:S(2)}) collective-permute-start(f32[32,256]{1,0:T(8,128)S(1)} %get-tuple-element.46), channel_id=1, source_target_pairs={{0,32},{1,33},{2,34},{3,35},{4,36},{5,37},{6,38},{7,39},{8,40},{9,... | collective-permute-start | bytes 98312 | tf_op jit(solution)/shard_map/ppermute | solution.py:559
  27.9 9.3 %collective-permute-start.10 = (f32[32,256]{1,0:T(8,128)S(1)}, f32[32,256]{1,0:T(8,128)S(1)}, u32[]{:S(2)}, u32[]{:S(2)}) collective-permute-start(f32[32,256]{1,0:T(8,128)S(1)} %get-tuple-element.47), channel_id=1, source_target_pairs={{0,64},{1,65},{2,66},{3,67},{4,68},{5,69},{6,70},{7,71},{8,72},{9,... | collective-permute-start | bytes 98312 | tf_op jit(solution)/shard_map/ppermute | solution.py:559

commit v8 on v7

--- a/solution.py
+++ b/solution.py
@@ -41,6 +41,13 @@
 NORM = {t: float(np.float32(np.sqrt(np.prod(2.0 * np.array(t) + 1.0)))) for t in TERM}
 
 
+def norm_rows():
+    norms = np.zeros((ROWS, SLOTS), np.float32)
+    for t, n in TERM.items():
+        norms[n] = NORM[t]
+    return norms
+
+
 def small(mib):
     return pltpu.CompilerParams(vmem_limit_bytes=mib * 2**20)
 
@@ -79,8 +86,8 @@
     return (parts[2 * n :] + parts[n : 2 * n]) + parts[:n]
 
 
-def pack_kernel(owner_hbm, pos_hbm, mass_hbm, tgt_hbm, far_hbm, local_hbm, *rest):
-    list_refs, rest = rest[:3], rest[3:]
+def pack_kernel(owner_hbm, pos_hbm, mass_hbm, tgt_hbm, far_hbm, local_hbm, slots_hbm, *rest):
+    list_refs, rest = rest[:4], rest[4:]
     out_refs, (owner_ref, pos_ref, mass_ref, sem, count_ref), slot_refs = rest[:2], rest[2:-4], rest[-4:]
     copies = [
         pltpu.make_async_copy(a, b, sem.at[k])
@@ -88,7 +95,7 @@
     ]
     lists = [
         pltpu.make_async_copy(a, b, sem.at[3 + k])
-        for k, (a, b) in enumerate(zip((tgt_hbm, far_hbm, local_hbm), list_refs))
+        for k, (a, b) in enumerate(zip((tgt_hbm, far_hbm, local_hbm, slots_hbm), list_refs))
     ]
     for c in copies + lists:
         c.start()
@@ -124,20 +131,20 @@
         pack_kernel,
         out_shape=[VMEM(x.shape, x.dtype) for x in lists]
         + [jax.ShapeDtypeStruct((SLOTS // 2, 4 * BODIES), f32)] * 2,
-        in_specs=[pl.BlockSpec(memory_space=pltpu.HBM)] * 6,
-        out_specs=[pl.BlockSpec(memory_space=VMEM)] * 5,
+        in_specs=[pl.BlockSpec(memory_space=pltpu.HBM)] * 7,
+        out_specs=[pl.BlockSpec(memory_space=VMEM)] * 6,
         scratch_shapes=[
             pltpu.SMEM((1, owner.shape[0]), jnp.int32),
             VMEM((3, owner.shape[0], BODIES), f32),
             VMEM((owner.shape[0], BODIES), f32),
-            pltpu.SemaphoreType.DMA((6,)),
+            pltpu.SemaphoreType.DMA((7,)),
             pltpu.SMEM((PEERS,), jnp.int32),
         ]
         + [VMEM((SLOTS, BODIES), f32)] * 4,
         compiler_params=small(2),
         name="pack",
     )(*map(in_hbm, (owner.T, positions.transpose(1, 0, 2), masses, *lists)))
-    return out[:3], out[3], out[4]
+    return out[:4], out[4], out[5]
 
 
 def merge_kernel(mine_ref, other_ref, after_ref, *out_refs):
@@ -282,7 +289,7 @@
 
 def multipole_kernel(*refs):
     (mine_ref, other_ref, *pieces), refs = refs[:5], refs[5:]
-    slots_hbm, _, mt_ref, post_ref, *refs = refs
+    slots_hbm, _, norm_ref, mt_ref, post_ref, *refs = refs
     exp_refs, (acc_ref, m_ref, rows_ref, slots_ref, sem, recv_ref) = refs[:LEVELS], refs[LEVELS:]
     slots_copy = pltpu.make_async_copy(slots_hbm, slots_ref, sem)
     slots_copy.start()
@@ -324,9 +331,11 @@
         return carry
 
     lax.fori_loop(0, BODIES // 32, chunk, 0)
-    mt_ref[TERMS - 5 :, :] = jnp.zeros((ROWS - TERMS + 5, SLOTS), f32)
-    for (a, b, c), n in TERM.items():
-        mt_ref[n : n + 1, :] = jnp.sum(acc_ref[n], axis=0, keepdims=True) * NORM[a, b, c]
+    parts = acc_ref.reshape(ROWS * 8, SLOTS)
+    for n in range(0, ROWS, 8):
+        v = [parts[pl.ds(8 * n + k, 8, stride=8), :] for k in range(8)]
+        total = ((v[0] + v[1]) + (v[2] + v[3])) + ((v[4] + v[5]) + (v[6] + v[7]))
+        mt_ref[n : n + 8, :] = total * norm_ref[n : n + 8, :]
     m_ref[0] = mt_ref[0:128, :].T
     m_ref[1] = jnp.concatenate([mt_ref[128:ROWS, :], jnp.zeros((256 - ROWS, SLOTS), f32)], axis=0).T
     slots_copy.wait()
@@ -338,7 +347,7 @@
                 rows_ref[half, pl.ds(k, 1), :] = m_ref[half, pl.ds(slot, 1), :]
             return carry
 
-        lax.fori_loop(0, KEXP, row, 0, unroll=8)
+        lax.fori_loop(0, KEXP, row, 0, unroll=32)
         for half in range(2):
             exp_refs[level][:, half * 128 : half * 128 + 128] = rows_ref[half]
 
@@ -352,10 +361,10 @@
             jax.ShapeDtypeStruct((4, BODIES, SLOTS), f32),
         ]
         + [jax.ShapeDtypeStruct((KEXP, 256), f32)] * LEVELS,
-        in_specs=[vm] * 5 + [pl.BlockSpec(memory_space=pltpu.HBM), vm],
+        in_specs=[vm] * 8,
         out_specs=[vm] * (2 + LEVELS),
         scratch_shapes=[
-            pltpu.VMEM((TERMS, 8, SLOTS), f32),
+            pltpu.VMEM((ROWS, 8, SLOTS), f32),
             pltpu.VMEM((2, SLOTS, 128), f32),
             pltpu.VMEM((2, KEXP, 128), f32),
             pltpu.SMEM((LEVELS, 1, KEXP), jnp.int32),
@@ -364,7 +373,7 @@
         ],
         compiler_params=small(4),
         name="multipoles",
-    )(*pieces, in_hbm(export_slots.transpose(1, 0, 2)), after)
+    )(*pieces, export_slots, after, norm_rows())
     return out[0], out[1], out[2:]
 
 
@@ -508,9 +517,6 @@
 
 def field(counts, left, mt, far, post, near):
     vm = pl.BlockSpec(memory_space=VMEM)
-    norms = np.zeros((ROWS, SLOTS), np.float32)
-    for t, n in TERM.items():
-        norms[n] = NORM[t]
     return pl.pallas_call(
         field_kernel,
         out_shape=jax.ShapeDtypeStruct((SLOTS, 4, BODIES), f32),
@@ -526,7 +532,7 @@
         compiler_params=small(20),
         cost_estimate=pl.CostEstimate(flops=40 * 10**9, bytes_accessed=26 * 10**6, transcendentals=0),
         name="field",
-    )(counts, left, mt, *far, post, near, norms)
+    )(counts, left, mt, *far, post, near, norm_rows())
 
 
 def body(
@@ -544,7 +550,8 @@
 ):
     axes = ("dom", "sub")
     devices = lax.axis_size(axes)
-    lists, mine, sent = pack_tiles(owner, positions, masses, (m2l_target[0], far_source[0], local_source[0]))
+    lists = (m2l_target[0], far_source[0], local_source[0], export_slots.transpose(1, 0, 2))
+    (*lists, exports), mine, sent = pack_tiles(owner, positions, masses, lists)
 
     def swap(rows, k):
         return lax.ppermute(rows, "sub", [(i, i ^ k) for i in range(PEERS)])
@@ -554,7 +561,7 @@
     sent = merge(mine, other, done)
     pieces = [swap(sent[k - 1], k) for k in (1, 2, 3)]
     left, done = relay_operators(rows, sent[0])
-    mt, post, exported = multipoles_of((mine, other, *pieces), export_slots, done)
+    mt, post, exported = multipoles_of((mine, other, *pieces), exports, done)
     far = [
         lax.ppermute(rows, axes, [(i, i ^ (1 << level)) for i in range(devices)])
         for level, rows in enumerate(exported)

time: 48.7 us -> 48.4 us (level)
  transfers between devices with their start and end apart: 11 -> 11, of which waited for: 0 -> 0; matrix products, arithmetic and copies ran while one was open for 0% -> 0% of each run, Pallas kernels for 31% -> 32%
where the time goes in v8:
time: 48.4 us; the launch traced here: 48.3 us
  Pallas kernels  29.7 us (61%)
  starting transfers between devices  18.3 us (38%)
    ppermute x7, starting transfers between devices, body(): lax.ppermute(rows, axes, [(i, i ^ 1 << level) for i in range(devices)])  12.1 us
    pallas_call x1, Pallas kernels, field(): pl.pallas_call(field_kernel, out_shape=jax.ShapeDtypeStruct((SLOTS, 4, BO...  11.5 us
    pallas_call x1, Pallas kernels, near_field(): pl.pallas_call(near_kernel, out_shape=jax.ShapeDtypeStruct((4, BODIES, SL...  6.31 us
    ppermute x4, starting transfers between devices, swap(): return lax.ppermute(rows, 'sub', [(i, i ^ k) for i in range(PEERS)])  6.26 us
    pallas_call x1, Pallas kernels, count_pairs(): pl.pallas_call(count_kernel, out_shape=[VMEM((CLASSES // 2, SOURCES, 256)...  5.11 us
    pallas_call x1, Pallas kernels, relay_operators(): pl.pallas_call(relay_kernel, out_shape=[VMEM((J_BLOCKS, 2 * I_ROWS, J_STE...  3.91 us
    pallas_call x1, Pallas kernels, pack_tiles(): pl.pallas_call(pack_kernel, out_shape=[VMEM(x.shape, x.dtype) for x in li...  1.54 us
    pallas_call x1, Pallas kernels, multipoles_of(): pl.pallas_call(multipole_kernel, out_shape=[jax.ShapeDtypeStruct((ROWS, S...  1.38 us
  transfers between devices with their start and end apart: 11, of which 0 were waited for; matrix products, arithmetic and copies ran while one was open for 0% of the time, Pallas kernels for 32%

profile of v8, /device:TPU:0, one launch (start us, length us, event | category | flops | bytes accessed | tf_op | source)
XLA Modules:
  0.0 48.3 jit_solution(3986445645935059804)
XLA Ops:
  0.0 1.5 %pack.1 = (s32[8,64,128]{2,1,0:T(8,128)S(1)}, s32[7,64,128]{2,1,0:T(8,128)S(1)}, s32[64,128]{1,0:T(8,128)S(1)}, s32[7,1,32]{2,1,0:T(1,128)S(1)}, f32[64,512]{1,0:T(8,128)S(1)}, /*index=5*/f32[64,512]{1,0:T(8,128)S(1)}) custom-call(s32[1,64]{1,0:T(1,128)} %bitcast.11, f32[3,64,128]{2,1,0:T(8,128)} %bitcast.8, f32[64,128]{1,0:T(8,128)} %mass_hbm.1, ...), custom_call_target="tpu_custom_call" | custom-call | tf_op jit(solution)/shard_map/pack/pallas_call | solution.py:130
  1.6 4.0 %collective-permute-start = (f32[64,512]{1,0:T(8,128)S(1)}, f32[64,512]{1,0:T(8,128)S(1)}, u32[]{:S(2)}, u32[]{:S(2)}) collective-permute-start(f32[64,512]{1,0:T(8,128)S(1)} %get-tuple-element.34), channel_id=1, source_target_pairs={{0,4},{1,5},{2,6},{3,7},{4,0},{5,1},{6,2},{7,3},{8,12},{9,13},{10,... | collective-permute-start | bytes 393224 | tf_op jit(solution)/shard_map/ppermute | solution.py:557
  5.6 5.1 %counts.1 = (bf16[64,352,256]{2,1,0:T(8,128)(2,1)S(1)}, f32[11,16,168,128]{3,2,1,0:T(8,128)S(1)}, f32[8,128]{1,0:T(8,128)S(1)}) custom-call(s32[8,64,128]{2,1,0:T(8,128)S(1)} %get-tuple-element.28.tgt_ref, s32[7,64,128]{2,1,0:T(8,128)S(1)} %get-tuple-element.29.far_ref, s32[64,128]{1,0:T(8,128)S(1)} %get-tuple-element.30.local_ref, f32[165,165,128]{2,1,0:T(8,128)} %op_hbm.1), custom_call_target="tpu_custom_call" | custom-call | flops 6000000000 | bytes 14000000 | tf_op jit(solution)/shard_map/counts/pallas_call | solution.py:257
  10.7 0.0 collective-permute-done.other_ref.refs_1_
  10.8 1.1 %collective-permute-start.2 = (f32[32,512]{1,0:T(8,128)S(1)}, f32[32,512]{1,0:T(8,128)S(1)}, u32[]{:S(2)}, u32[]{:S(2)}) collective-permute-start(f32[32,512]{1,0:T(8,128)S(1)} %get-tuple-element.38), channel_id=1, source_target_pairs={{0,2},{1,3},{2,0},{3,1},{4,6},{5,7},{6,4},{7,5},{8,10},{9,11},{10,... | collective-permute-start | bytes 196616 | tf_op jit(solution)/shard_map/ppermute | solution.py:557
  11.8 0.0 collective-permute-start.3
  11.9 1.1 %collective-permute-start.1 = (f32[32,512]{1,0:T(8,128)S(1)}, f32[32,512]{1,0:T(8,128)S(1)}, u32[]{:S(2)}, u32[]{:S(2)}) collective-permute-start(f32[32,512]{1,0:T(8,128)S(1)} %get-tuple-element.36.after_ref), channel_id=1, source_target_pairs={{0,1},{1,0},{2,3},{3,2},{4,5},{5,4},{6,7},{7,6},{8,9},{9,8},{10,11... | collective-permute-start | bytes 196616 | tf_op jit(solution)/shard_map/ppermute | solution.py:557
  13.0 3.9 %relay.1 = (bf16[21,352,1024]{2,1,0:T(8,128)(2,1)S(1)}, f32[8,128]{1,0:T(8,128)S(1)}) custom-call(f32[11,16,168,128]{3,2,1,0:T(8,128)S(1)} %get-tuple-element.32.buf_ref, f32[32,512]{1,0:T(8,128)S(1)} %get-tuple-element.36.after_ref), custom_call_target="tpu_custom_call" | custom-call | flops 4000000000 | bytes 1000000 | tf_op jit(solution)/shard_map/relay/pallas_call | solution.py:279
  16.9 0.0 collective-permute-done.2.refs_3_
  16.9 0.0 collective-permute-done.3.refs_4_
  16.9 0.0 collective-permute-done.1.refs_2_
  16.9 0.0 copy-done
  16.9 1.4 %multipoles.1 = (f32[168,128]{1,0:T(8,128)S(1)}, f32[4,128,128]{2,1,0:T(8,128)S(1)}, f32[32,256]{1,0:T(8,128)S(1)}, f32[32,256]{1,0:T(8,128)S(1)}, f32[32,256]{1...) custom-call(f32[64,512]{1,0:T(8,128)S(1)} %get-tuple-element.33.mine, ...), custom_call_target="tpu_custom_call" | custom-call | tf_op jit(solution)/shard_map/multipoles/pallas_call | solution.py:357
  18.3 0.1 collective-permute-start.4
  18.4 1.1 %collective-permute-start.5 = (f32[32,256]{1,0:T(8,128)S(1)}, f32[32,256]{1,0:T(8,128)S(1)}, u32[]{:S(2)}, u32[]{:S(2)}) collective-permute-start(f32[32,256]{1,0:T(8,128)S(1)} %get-tuple-element.44), channel_id=1, source_target_pairs={{0,2},{1,3},{2,0},{3,1},{4,6},{5,7},{6,4},{7,5},{8,10},{9,11},{10,... | collective-permute-start | bytes 98312 | tf_op jit(solution)/shard_map/ppermute | solution.py:566
  19.5 2.2 %collective-permute-start.6 = (f32[32,256]{1,0:T(8,128)S(1)}, f32[32,256]{1,0:T(8,128)S(1)}, u32[]{:S(2)}, u32[]{:S(2)}) collective-permute-start(f32[32,256]{1,0:T(8,128)S(1)} %get-tuple-element.45), channel_id=1, source_target_pairs={{0,4},{1,5},{2,6},{3,7},{4,0},{5,1},{6,2},{7,3},{8,12},{9,13},{10,... | collective-permute-start | bytes 98312 | tf_op jit(solution)/shard_map/ppermute | solution.py:566
  21.7 1.5 %collective-permute-start.7 = (f32[32,256]{1,0:T(8,128)S(1)}, f32[32,256]{1,0:T(8,128)S(1)}, u32[]{:S(2)}, u32[]{:S(2)}) collective-permute-start(f32[32,256]{1,0:T(8,128)S(1)} %get-tuple-element.46), channel_id=1, source_target_pairs={{0,8},{1,9},{2,10},{3,11},{4,12},{5,13},{6,14},{7,15},{8,0},{9,1},... | collective-permute-start | bytes 98312 | tf_op jit(solution)/shard_map/ppermute | solution.py:566
  23.2 2.7 %collective-permute-start.8 = (f32[32,256]{1,0:T(8,128)S(1)}, f32[32,256]{1,0:T(8,128)S(1)}, u32[]{:S(2)}, u32[]{:S(2)}) collective-permute-start(f32[32,256]{1,0:T(8,128)S(1)} %get-tuple-element.47), channel_id=1, source_target_pairs={{0,16},{1,17},{2,18},{3,19},{4,20},{5,21},{6,22},{7,23},{8,24},{9,... | collective-permute-start | bytes 98312 | tf_op jit(solution)/shard_map/ppermute | solution.py:566
  25.9 0.0 collective-permute-done.4.rest_0_
  25.9 1.6 %collective-permute-start.9 = (f32[32,256]{1,0:T(8,128)S(1)}, f32[32,256]{1,0:T(8,128)S(1)}, u32[]{:S(2)}, u32[]{:S(2)}) collective-permute-start(f32[32,256]{1,0:T(8,128)S(1)} %get-tuple-element.48), channel_id=1, source_target_pairs={{0,32},{1,33},{2,34},{3,35},{4,36},{5,37},{6,38},{7,39},{8,40},{9,... | collective-permute-start | bytes 98312 | tf_op jit(solution)/shard_map/ppermute | solution.py:566
  27.5 0.0 collective-permute-done.5.rest_1_
  27.5 2.9 %collective-permute-start.10 = (f32[32,256]{1,0:T(8,128)S(1)}, f32[32,256]{1,0:T(8,128)S(1)}, u32[]{:S(2)}, u32[]{:S(2)}) collective-permute-start(f32[32,256]{1,0:T(8,128)S(1)} %get-tuple-element.49), channel_id=1, source_target_pairs={{0,64},{1,65},{2,66},{3,67},{4,68},{5,69},{6,70},{7,71},{8,72},{9,... | collective-permute-start | bytes 98312 | tf_op jit(solution)/shard_map/ppermute | solution.py:566
  30.4 0.0 copy-done.1
  30.4 0.0 copy-done.2
  30.4 0.0 copy-done.3
  30.4 6.3 %near.1.rest_8_ = f32[4,128,128]{2,1,0:T(8,128)S(1)} custom-call(f32[4,128,128]{2,1,0:T(8,128)S(1)} %get-tuple-element.50.post_ref.rest_7_, s32[1,128]{1,0:T(1,128)S(1)} %copy-done.1, s32[1,128]{1,0:T(1,128)S(1)} %copy-done.2, s32[1,128]{1,0:T(1,128)S(1)} %copy-done.3), custom_call_target="tpu_custom_call" | custom-call | flops 8000000000 | bytes 1000000 | tf_op jit(solution)/shard_map/near/pallas_call | solution.py:425
  36.7 0.0 collective-permute-done.6.rest_2_
  36.8 0.0 collective-permute-done.7.rest_3_
  36.8 0.0 collective-permute-done.8.rest_4_
  36.8 0.0 collective-permute-done.9.rest_5_
  36.8 0.0 collective-permute-done.10.rest_6_
  36.8 11.5 %field.1 = f32[128,4,128]{2,1,0:T(4,128)} custom-call(bf16[64,352,256]{2,1,0:T(8,128)(2,1)S(1)} %get-tuple-element.31.counts_ref, bf16[21,352,1024]{2,1,0:T(8,128)(2,1)S(1)} %get-tuple-element.37.left_ref, f32[168,128]{1,0:T(8,128)S(1)} %get-tuple-element.42.mt_ref, f32[32,256]{1,0:T(8,128)S(1)} %collective-permute-done.4.rest_0_, ...), custom_call_target="tpu_custom_call" | custom-call | flops 40000000000 | bytes 26000000 | tf_op jit(solution)/shard_map/field/pallas_call | solution.py:520
  (5 shorter events, 0.0 us)
Async XLA Ops:
  1.6 9.2 %collective-permute-start = (f32[64,512]{1,0:T(8,128)S(1)}, f32[64,512]{1,0:T(8,128)S(1)}, u32[]{:S(2)}, u32[]{:S(2)}) collective-permute-start(f32[64,512]{1,0:T(8,128)S(1)} %get-tuple-element.34), channel_id=1, source_target_pairs={{0,4},{1,5},{2,6},{3,7},{4,0},{5,1},{6,2},{7,3},{8,12},{9,13},{10,... | collective-permute-start | bytes 393224 | tf_op jit(solution)/shard_map/ppermute | solution.py:557
  5.6 11.3 %copy-start = (f32[168,128]{1,0:T(8,128)S(1)}, f32[168,128]{1,0:T(8,128)}, u32[]{:S(2)}) copy-start(f32[168,128]{1,0:T(8,128)} %constant.2.clone.refs_7_.rest_9_) | copy-start | bytes 258052
  5.6 24.8 %copy-start.1 = (s32[1,128]{1,0:T(1,128)S(1)}, s32[1,128]{1,0:T(1,128)}, u32[]{:S(2)}) copy-start(s32[1,128]{1,0:T(1,128)} %tgt_ref.1) | copy-start | bytes 1540
  5.6 24.8 %copy-start.2 = (s32[1,128]{1,0:T(1,128)S(1)}, s32[1,128]{1,0:T(1,128)}, u32[]{:S(2)}) copy-start(s32[1,128]{1,0:T(1,128)} %src_ref.1) | copy-start | bytes 1540
  5.6 24.8 %copy-start.3 = (s32[1,128]{1,0:T(1,128)S(1)}, s32[1,128]{1,0:T(1,128)}, u32[]{:S(2)}) copy-start(s32[1,128]{1,0:T(1,128)} %off_ref.1) | copy-start | bytes 1540
  10.8 6.1 %collective-permute-start.2 = (f32[32,512]{1,0:T(8,128)S(1)}, f32[32,512]{1,0:T(8,128)S(1)}, u32[]{:S(2)}, u32[]{:S(2)}) collective-permute-start(f32[32,512]{1,0:T(8,128)S(1)} %get-tuple-element.38), channel_id=1, source_target_pairs={{0,2},{1,3},{2,0},{3,1},{4,6},{5,7},{6,4},{7,5},{8,10},{9,11},{10,... | collective-permute-start | bytes 196616 | tf_op jit(solution)/shard_map/ppermute | solution.py:557
  11.8 5.1 %collective-permute-start.3 = (f32[32,512]{1,0:T(8,128)S(1)}, f32[32,512]{1,0:T(8,128)S(1)}, u32[]{:S(2)}, u32[]{:S(2)}) collective-permute-start(f32[32,512]{1,0:T(8,128)S(1)} %get-tuple-element.39), channel_id=1, source_target_pairs={{0,3},{1,2},{2,1},{3,0},{4,7},{5,6},{6,5},{7,4},{8,11},{9,10},{10,... | collective-permute-start | bytes 196616 | tf_op jit(solution)/shard_map/ppermute | solution.py:557
  11.9 5.1 %collective-permute-start.1 = (f32[32,512]{1,0:T(8,128)S(1)}, f32[32,512]{1,0:T(8,128)S(1)}, u32[]{:S(2)}, u32[]{:S(2)}) collective-permute-start(f32[32,512]{1,0:T(8,128)S(1)} %get-tuple-element.36.after_ref), channel_id=1, source_target_pairs={{0,1},{1,0},{2,3},{3,2},{4,5},{5,4},{6,7},{7,6},{8,9},{9,8},{10,11... | collective-permute-start | bytes 196616 | tf_op jit(solution)/shard_map/ppermute | solution.py:557
  18.3 7.6 %collective-permute-start.4 = (f32[32,256]{1,0:T(8,128)S(1)}, f32[32,256]{1,0:T(8,128)S(1)}, u32[]{:S(2)}, u32[]{:S(2)}) collective-permute-start(f32[32,256]{1,0:T(8,128)S(1)} %get-tuple-element.43), channel_id=1, source_target_pairs={{0,1},{1,0},{2,3},{3,2},{4,5},{5,4},{6,7},{7,6},{8,9},{9,8},{10,11... | collective-permute-start | bytes 98312 | tf_op jit(solution)/shard_map/ppermute | solution.py:566
  18.4 9.1 %collective-permute-start.5 = (f32[32,256]{1,0:T(8,128)S(1)}, f32[32,256]{1,0:T(8,128)S(1)}, u32[]{:S(2)}, u32[]{:S(2)}) collective-permute-start(f32[32,256]{1,0:T(8,128)S(1)} %get-tuple-element.44), channel_id=1, source_target_pairs={{0,2},{1,3},{2,0},{3,1},{4,6},{5,7},{6,4},{7,5},{8,10},{9,11},{10,... | collective-permute-start | bytes 98312 | tf_op jit(solution)/shard_map/ppermute | solution.py:566
  19.5 17.2 %collective-permute-start.6 = (f32[32,256]{1,0:T(8,128)S(1)}, f32[32,256]{1,0:T(8,128)S(1)}, u32[]{:S(2)}, u32[]{:S(2)}) collective-permute-start(f32[32,256]{1,0:T(8,128)S(1)} %get-tuple-element.45), channel_id=1, source_target_pairs={{0,4},{1,5},{2,6},{3,7},{4,0},{5,1},{6,2},{7,3},{8,12},{9,13},{10,... | collective-permute-start | bytes 98312 | tf_op jit(solution)/shard_map/ppermute | solution.py:566
  21.7 15.0 %collective-permute-start.7 = (f32[32,256]{1,0:T(8,128)S(1)}, f32[32,256]{1,0:T(8,128)S(1)}, u32[]{:S(2)}, u32[]{:S(2)}) collective-permute-start(f32[32,256]{1,0:T(8,128)S(1)} %get-tuple-element.46), channel_id=1, source_target_pairs={{0,8},{1,9},{2,10},{3,11},{4,12},{5,13},{6,14},{7,15},{8,0},{9,1},... | collective-permute-start | bytes 98312 | tf_op jit(solution)/shard_map/ppermute | solution.py:566
  23.2 13.6 %collective-permute-start.8 = (f32[32,256]{1,0:T(8,128)S(1)}, f32[32,256]{1,0:T(8,128)S(1)}, u32[]{:S(2)}, u32[]{:S(2)}) collective-permute-start(f32[32,256]{1,0:T(8,128)S(1)} %get-tuple-element.47), channel_id=1, source_target_pairs={{0,16},{1,17},{2,18},{3,19},{4,20},{5,21},{6,22},{7,23},{8,24},{9,... | collective-permute-start | bytes 98312 | tf_op jit(solution)/shard_map/ppermute | solution.py:566
  25.9 10.8 %collective-permute-start.9 = (f32[32,256]{1,0:T(8,128)S(1)}, f32[32,256]{1,0:T(8,128)S(1)}, u32[]{:S(2)}, u32[]{:S(2)}) collective-permute-start(f32[32,256]{1,0:T(8,128)S(1)} %get-tuple-element.48), channel_id=1, source_target_pairs={{0,32},{1,33},{2,34},{3,35},{4,36},{5,37},{6,38},{7,39},{8,40},{9,... | collective-permute-start | bytes 98312 | tf_op jit(solution)/shard_map/ppermute | solution.py:566
  27.5 9.3 %collective-permute-start.10 = (f32[32,256]{1,0:T(8,128)S(1)}, f32[32,256]{1,0:T(8,128)S(1)}, u32[]{:S(2)}, u32[]{:S(2)}) collective-permute-start(f32[32,256]{1,0:T(8,128)S(1)} %get-tuple-element.49), channel_id=1, source_target_pairs={{0,64},{1,65},{2,66},{3,67},{4,68},{5,69},{6,70},{7,71},{8,72},{9,... | collective-permute-start | bytes 98312 | tf_op jit(solution)/shard_map/ppermute | solution.py:566

commit v9 on v8

--- a/solution.py
+++ b/solution.py
@@ -174,15 +174,20 @@
 J_BLOCKS = ROWS // J_STEP
 
 
-def operator_copy(op_hbm, buf_ref, sem, q):
+EARLY = 7
+
+
+def operator_copy(op_hbm, buf_ref, sem, q, first=0):
     size = min(I_STEP, TERMS - q * I_STEP)
     return pltpu.make_async_copy(
-        op_hbm.at[pl.ds(q * I_STEP, size)], buf_ref.at[q, pl.ds(0, size), pl.ds(0, TERMS)], sem.at[q]
+        op_hbm.at[pl.ds(q * I_STEP, size)],
+        buf_ref.at[q - first, pl.ds(0, size), pl.ds(0, TERMS)],
+        sem.at[q - first],
     )
 
 
 def count_kernel(tgt_ref, far_ref, local_ref, op_hbm, counts_ref, buf_ref, done_ref, tt_ref, st_ref, sem):
-    for q in range(I_FULL + 1):
+    for q in range(EARLY):
         operator_copy(op_hbm, buf_ref, sem, q).start()
 
     order = [7, 0, 1, 2, 3, 4, 5, 6]
@@ -229,16 +234,19 @@
 
     lax.fori_loop(0, CLASSES // 2 // PAIR_STEP, group, 0)
     done_ref[...] = jnp.zeros_like(done_ref)
-    for q in range(I_FULL + 1):
+    for q in range(EARLY):
         operator_copy(op_hbm, buf_ref, sem, q).wait()
 
 
-def relay_kernel(buf_ref, after_ref, left_ref, done_ref):
+def relay_kernel(buf_ref, op_hbm, after_ref, left_ref, done_ref, late_ref, sem):
+    late = [operator_copy(op_hbm, late_ref, sem, q, EARLY) for q in range(EARLY, I_FULL + 1)]
+    for c in late:
+        c.start()
     for j in range(TERMS, ROWS):
         left_ref[J_BLOCKS - 1, :, (j % J_STEP) * 128 : (j % J_STEP) * 128 + 128] = jnp.zeros((2 * I_ROWS, 128), bf16)
 
-    def relay(q, carry):
-        rows = buf_ref.at[q].reshape(I_STEP * TERMS_PAD, CLASSES)
+    def relay(q, ref, first):
+        rows = ref.at[q - first].reshape(I_STEP * TERMS_PAD, CLASSES)
         at = pl.multiple_of(q * I_STEP, I_STEP)
         for j in range(TERMS):
             v = rows[pl.ds(j, I_STEP, stride=TERMS_PAD), :]
@@ -246,9 +254,11 @@
             lanes = slice((j % J_STEP) * 128, (j % J_STEP) * 128 + 128)
             left_ref[j // J_STEP, pl.ds(at, I_STEP), lanes] = high
             left_ref[j // J_STEP, pl.ds(at + I_ROWS, I_STEP), lanes] = low
-        return carry
-
-    lax.fori_loop(0, I_FULL + 1, relay, 0)
+
+    lax.fori_loop(0, EARLY, lambda q, _: (relay(q, buf_ref, 0), 0)[1], 0)
+    for c in late:
+        c.wait()
+    lax.fori_loop(EARLY, I_FULL + 1, lambda q, _: (relay(q, late_ref, EARLY), 0)[1], 0)
     done_ref[...] = jnp.zeros_like(done_ref)
 
 
@@ -258,7 +268,7 @@
         count_kernel,
         out_shape=[
             VMEM((CLASSES // 2, SOURCES, 256), bf16),
-            VMEM((I_FULL + 1, I_STEP, TERMS_PAD, CLASSES), f32),
+            VMEM((EARLY, I_STEP, TERMS_PAD, CLASSES), f32),
             VMEM((8, 128), f32),
         ],
         in_specs=[vm] * 3 + [pl.BlockSpec(memory_space=pltpu.HBM)],
@@ -266,7 +276,7 @@
         scratch_shapes=[
             VMEM((4, 128, 128), f32),
             VMEM((4, 128, 128), f32),
-            pltpu.SemaphoreType.DMA((I_FULL + 1,)),
+            pltpu.SemaphoreType.DMA((EARLY,)),
         ],
         compiler_params=small(4),
         cost_estimate=pl.CostEstimate(flops=6 * 10**9, bytes_accessed=14 * 10**6, transcendentals=0),
@@ -274,17 +284,21 @@
     )(m2l_target, far_source, local_source, in_hbm(operators))
 
 
-def relay_operators(rows, after):
+def relay_operators(rows, operators, after):
     vm = pl.BlockSpec(memory_space=VMEM)
     return pl.pallas_call(
         relay_kernel,
         out_shape=[VMEM((J_BLOCKS, 2 * I_ROWS, J_STEP * CLASSES), bf16), VMEM((8, 128), f32)],
-        in_specs=[vm] * 2,
+        in_specs=[vm, pl.BlockSpec(memory_space=pltpu.HBM), vm],
         out_specs=[vm] * 2,
-        compiler_params=small(4),
+        scratch_shapes=[
+            VMEM((I_FULL + 1 - EARLY, I_STEP, TERMS_PAD, CLASSES), f32),
+            pltpu.SemaphoreType.DMA((I_FULL + 1 - EARLY,)),
+        ],
+        compiler_params=small(8),
         cost_estimate=pl.CostEstimate(flops=4 * 10**9, bytes_accessed=10**6, transcendentals=0),
         name="relay",
-    )(rows, after)
+    )(rows, in_hbm(operators), after)
 
 
 def multipole_kernel(*refs):
@@ -560,7 +574,7 @@
     counts, rows, done = count_pairs(*lists, operators)
     sent = merge(mine, other, done)
     pieces = [swap(sent[k - 1], k) for k in (1, 2, 3)]
-    left, done = relay_operators(rows, sent[0])
+    left, done = relay_operators(rows, operators, sent[0])
     mt, post, exported = multipoles_of((mine, other, *pieces), exports, done)
     far = [
         lax.ppermute(rows, axes, [(i, i ^ (1 << level)) for i in range(devices)])

time: 48.4 us -> 48.3 us (level)
  Pallas kernels: 29.7 us -> 28.7 us
  starting transfers between devices: 18.3 us -> 19.2 us
    ppermute x7, starting transfers between devices: 12.1 us -> 13.2 us  [body(): lax.ppermute(rows, axes, [(i, i ^ 1 << level) for i in range(devices)])]
    pallas_call x1, Pallas kernels: 5.11 us -> 4.19 us  [count_pairs(): pl.pallas_call(count_kernel, out_shape=[VMEM((CLASSES // 2, SOURCES, 256)...]
  transfers between devices with their start and end apart: 11 -> 11, of which waited for: 0 -> 0; matrix products, arithmetic and copies ran while one was open for 0% -> 0% of each run, Pallas kernels for 32% -> 30%
where the time goes in v9:
time: 48.3 us; the launch traced here: 48.2 us
  Pallas kernels  28.7 us (59%)
  starting transfers between devices  19.2 us (40%)
    ppermute x7, starting transfers between devices, body(): lax.ppermute(rows, axes, [(i, i ^ 1 << level) for i in range(devices)])  13.2 us
    pallas_call x1, Pallas kernels, field(): pl.pallas_call(field_kernel, out_shape=jax.ShapeDtypeStruct((SLOTS, 4, BO...  11.3 us
    pallas_call x1, Pallas kernels, near_field(): pl.pallas_call(near_kernel, out_shape=jax.ShapeDtypeStruct((4, BODIES, SL...  6.31 us
    ppermute x4, starting transfers between devices, swap(): return lax.ppermute(rows, 'sub', [(i, i ^ k) for i in range(PEERS)])  5.98 us
    pallas_call x1, Pallas kernels, count_pairs(): pl.pallas_call(count_kernel, out_shape=[VMEM((CLASSES // 2, SOURCES, 256)...  4.19 us
    pallas_call x1, Pallas kernels, relay_operators(): pl.pallas_call(relay_kernel, out_shape=[VMEM((J_BLOCKS, 2 * I_ROWS, J_STE...  3.95 us
    pallas_call x1, Pallas kernels, pack_tiles(): pl.pallas_call(pack_kernel, out_shape=[VMEM(x.shape, x.dtype) for x in li...  1.54 us
    pallas_call x1, Pallas kernels, multipoles_of(): pl.pallas_call(multipole_kernel, out_shape=[jax.ShapeDtypeStruct((ROWS, S...  1.36 us
  transfers between devices with their start and end apart: 11, of which 0 were waited for; matrix products, arithmetic and copies ran while one was open for 0% of the time, Pallas kernels for 30%

profile of v9, /device:TPU:0, one launch (start us, length us, event | category | flops | bytes accessed | tf_op | source)
XLA Modules:
  0.0 48.2 jit_solution(17798891270969595804)
XLA Ops:
  0.0 1.5 %pack.1 = (s32[8,64,128]{2,1,0:T(8,128)S(1)}, s32[7,64,128]{2,1,0:T(8,128)S(1)}, s32[64,128]{1,0:T(8,128)S(1)}, s32[7,1,32]{2,1,0:T(1,128)S(1)}, f32[64,512]{1,0:T(8,128)S(1)}, /*index=5*/f32[64,512]{1,0:T(8,128)S(1)}) custom-call(s32[1,64]{1,0:T(1,128)} %bitcast.11, f32[3,64,128]{2,1,0:T(8,128)} %bitcast.8, f32[64,128]{1,0:T(8,128)} %mass_hbm.1, ...), custom_call_target="tpu_custom_call" | custom-call | tf_op jit(solution)/shard_map/pack/pallas_call | solution.py:130
  1.6 4.0 %collective-permute-start = (f32[64,512]{1,0:T(8,128)S(1)}, f32[64,512]{1,0:T(8,128)S(1)}, u32[]{:S(2)}, u32[]{:S(2)}) collective-permute-start(f32[64,512]{1,0:T(8,128)S(1)} %get-tuple-element.34), channel_id=1, source_target_pairs={{0,4},{1,5},{2,6},{3,7},{4,0},{5,1},{6,2},{7,3},{8,12},{9,13},{10,... | collective-permute-start | bytes 393224 | tf_op jit(solution)/shard_map/ppermute | solution.py:571
  5.6 4.2 %counts.1 = (bf16[64,352,256]{2,1,0:T(8,128)(2,1)S(1)}, f32[7,16,168,128]{3,2,1,0:T(8,128)S(1)}, f32[8,128]{1,0:T(8,128)S(1)}) custom-call(s32[8,64,128]{2,1,0:T(8,128)S(1)} %get-tuple-element.28.tgt_ref, s32[7,64,128]{2,1,0:T(8,128)S(1)} %get-tuple-element.29.far_ref, s32[64,128]{1,0:T(8,128)S(1)} %get-tuple-element.30.local_ref, f32[165,165,128]{2,1,0:T(8,128)} %op_hbm.3), custom_call_target="tpu_custom_call" | custom-call | flops 6000000000 | bytes 14000000 | tf_op jit(solution)/shard_map/counts/pallas_call | solution.py:267
  9.8 0.0 copy-start
  9.8 0.0 copy-start.1
  9.8 0.0 copy-start.2
  9.8 0.0 copy-start.3
  9.8 0.0 collective-permute-done.other_ref.refs_1_
  9.9 0.1 collective-permute-start.1
  10.0 1.1 %collective-permute-start.2 = (f32[32,512]{1,0:T(8,128)S(1)}, f32[32,512]{1,0:T(8,128)S(1)}, u32[]{:S(2)}, u32[]{:S(2)}) collective-permute-start(f32[32,512]{1,0:T(8,128)S(1)} %get-tuple-element.38), channel_id=1, source_target_pairs={{0,2},{1,3},{2,0},{3,1},{4,6},{5,7},{6,4},{7,5},{8,10},{9,11},{10,... | collective-permute-start | bytes 196616 | tf_op jit(solution)/shard_map/ppermute | solution.py:571
  11.1 0.8 %collective-permute-start.3 = (f32[32,512]{1,0:T(8,128)S(1)}, f32[32,512]{1,0:T(8,128)S(1)}, u32[]{:S(2)}, u32[]{:S(2)}) collective-permute-start(f32[32,512]{1,0:T(8,128)S(1)} %get-tuple-element.39), channel_id=1, source_target_pairs={{0,3},{1,2},{2,1},{3,0},{4,7},{5,6},{6,5},{7,4},{8,11},{9,10},{10,... | collective-permute-start | bytes 196616 | tf_op jit(solution)/shard_map/ppermute | solution.py:571
  11.8 4.0 %relay.1 = (bf16[21,352,1024]{2,1,0:T(8,128)(2,1)S(1)}, f32[8,128]{1,0:T(8,128)S(1)}) custom-call(f32[7,16,168,128]{3,2,1,0:T(8,128)S(1)} %get-tuple-element.32.buf_ref, f32[165,165,128]{2,1,0:T(8,128)} %op_hbm.3, f32[32,512]{1,0:T(8,128)S(1)} %get-tuple-element.36.after_ref), custom_call_target="tpu_custom_call" | custom-call | flops 4000000000 | bytes 1000000 | tf_op jit(solution)/shard_map/relay/pallas_call | solution.py:289
  15.8 0.0 collective-permute-done.1.refs_2_
  15.8 0.0 collective-permute-done.2.refs_3_
  15.8 0.0 collective-permute-done.3.refs_4_
  15.8 1.4 %multipoles.1 = (f32[168,128]{1,0:T(8,128)S(1)}, f32[4,128,128]{2,1,0:T(8,128)S(1)}, f32[32,256]{1,0:T(8,128)S(1)}, f32[32,256]{1,0:T(8,128)S(1)}, f32[32,256]{1...) custom-call(f32[64,512]{1,0:T(8,128)S(1)} %get-tuple-element.33.mine, ...), custom_call_target="tpu_custom_call" | custom-call | tf_op jit(solution)/shard_map/multipoles/pallas_call | solution.py:371
  17.2 0.4 collective-permute-start.4
  17.6 1.0 %collective-permute-start.5 = (f32[32,256]{1,0:T(8,128)S(1)}, f32[32,256]{1,0:T(8,128)S(1)}, u32[]{:S(2)}, u32[]{:S(2)}) collective-permute-start(f32[32,256]{1,0:T(8,128)S(1)} %get-tuple-element.44), channel_id=1, source_target_pairs={{0,2},{1,3},{2,0},{3,1},{4,6},{5,7},{6,4},{7,5},{8,10},{9,11},{10,... | collective-permute-start | bytes 98312 | tf_op jit(solution)/shard_map/ppermute | solution.py:580
  18.7 3.1 %collective-permute-start.6 = (f32[32,256]{1,0:T(8,128)S(1)}, f32[32,256]{1,0:T(8,128)S(1)}, u32[]{:S(2)}, u32[]{:S(2)}) collective-permute-start(f32[32,256]{1,0:T(8,128)S(1)} %get-tuple-element.45), channel_id=1, source_target_pairs={{0,4},{1,5},{2,6},{3,7},{4,0},{5,1},{6,2},{7,3},{8,12},{9,13},{10,... | collective-permute-start | bytes 98312 | tf_op jit(solution)/shard_map/ppermute | solution.py:580
  21.7 1.5 %collective-permute-start.7 = (f32[32,256]{1,0:T(8,128)S(1)}, f32[32,256]{1,0:T(8,128)S(1)}, u32[]{:S(2)}, u32[]{:S(2)}) collective-permute-start(f32[32,256]{1,0:T(8,128)S(1)} %get-tuple-element.46), channel_id=1, source_target_pairs={{0,8},{1,9},{2,10},{3,11},{4,12},{5,13},{6,14},{7,15},{8,0},{9,1},... | collective-permute-start | bytes 98312 | tf_op jit(solution)/shard_map/ppermute | solution.py:580
  23.2 2.7 %collective-permute-start.8 = (f32[32,256]{1,0:T(8,128)S(1)}, f32[32,256]{1,0:T(8,128)S(1)}, u32[]{:S(2)}, u32[]{:S(2)}) collective-permute-start(f32[32,256]{1,0:T(8,128)S(1)} %get-tuple-element.47), channel_id=1, source_target_pairs={{0,16},{1,17},{2,18},{3,19},{4,20},{5,21},{6,22},{7,23},{8,24},{9,... | collective-permute-start | bytes 98312 | tf_op jit(solution)/shard_map/ppermute | solution.py:580
  26.0 0.0 collective-permute-done.4.rest_0_
  26.0 1.6 %collective-permute-start.9 = (f32[32,256]{1,0:T(8,128)S(1)}, f32[32,256]{1,0:T(8,128)S(1)}, u32[]{:S(2)}, u32[]{:S(2)}) collective-permute-start(f32[32,256]{1,0:T(8,128)S(1)} %get-tuple-element.48), channel_id=1, source_target_pairs={{0,32},{1,33},{2,34},{3,35},{4,36},{5,37},{6,38},{7,39},{8,40},{9,... | collective-permute-start | bytes 98312 | tf_op jit(solution)/shard_map/ppermute | solution.py:580
  27.5 0.0 collective-permute-done.5.rest_1_
  27.5 2.9 %collective-permute-start.10 = (f32[32,256]{1,0:T(8,128)S(1)}, f32[32,256]{1,0:T(8,128)S(1)}, u32[]{:S(2)}, u32[]{:S(2)}) collective-permute-start(f32[32,256]{1,0:T(8,128)S(1)} %get-tuple-element.49), channel_id=1, source_target_pairs={{0,64},{1,65},{2,66},{3,67},{4,68},{5,69},{6,70},{7,71},{8,72},{9,... | collective-permute-start | bytes 98312 | tf_op jit(solution)/shard_map/ppermute | solution.py:580
  30.5 6.3 %near.1.rest_8_ = f32[4,128,128]{2,1,0:T(8,128)S(1)} custom-call(f32[4,128,128]{2,1,0:T(8,128)S(1)} %get-tuple-element.50.post_ref.rest_7_, s32[1,128]{1,0:T(1,128)S(1)} %copy-done.1, s32[1,128]{1,0:T(1,128)S(1)} %copy-done.2, s32[1,128]{1,0:T(1,128)S(1)} %copy-done.3), custom_call_target="tpu_custom_call" | custom-call | flops 8000000000 | bytes 1000000 | tf_op jit(solution)/shard_map/near/pallas_call | solution.py:439
  36.8 0.0 collective-permute-done.6.rest_2_
  36.8 0.0 collective-permute-done.7.rest_3_
  36.8 0.0 collective-permute-done.8.rest_4_
  36.8 0.0 collective-permute-done.9.rest_5_
  36.8 0.0 collective-permute-done.10.rest_6_
  36.8 11.3 %field.1 = f32[128,4,128]{2,1,0:T(4,128)} custom-call(bf16[64,352,256]{2,1,0:T(8,128)(2,1)S(1)} %get-tuple-element.31.counts_ref, bf16[21,352,1024]{2,1,0:T(8,128)(2,1)S(1)} %get-tuple-element.37.left_ref, f32[168,128]{1,0:T(8,128)S(1)} %get-tuple-element.42.mt_ref, f32[32,256]{1,0:T(8,128)S(1)} %collective-permute-done.4.rest_0_, ...), custom_call_target="tpu_custom_call" | custom-call | flops 40000000000 | bytes 26000000 | tf_op jit(solution)/shard_map/field/pallas_call | solution.py:534
  (5 shorter events, 0.0 us)
Async XLA Ops:
  1.6 8.3 %collective-permute-start = (f32[64,512]{1,0:T(8,128)S(1)}, f32[64,512]{1,0:T(8,128)S(1)}, u32[]{:S(2)}, u32[]{:S(2)}) collective-permute-start(f32[64,512]{1,0:T(8,128)S(1)} %get-tuple-element.34), channel_id=1, source_target_pairs={{0,4},{1,5},{2,6},{3,7},{4,0},{5,1},{6,2},{7,3},{8,12},{9,13},{10,... | collective-permute-start | bytes 393224 | tf_op jit(solution)/shard_map/ppermute | solution.py:571
  9.8 6.0 %copy-start = (f32[168,128]{1,0:T(8,128)S(1)}, f32[168,128]{1,0:T(8,128)}, u32[]{:S(2)}) copy-start(f32[168,128]{1,0:T(8,128)} %constant.2.clone.refs_7_.rest_9_) | copy-start | bytes 258052
  9.8 20.6 %copy-start.1 = (s32[1,128]{1,0:T(1,128)S(1)}, s32[1,128]{1,0:T(1,128)}, u32[]{:S(2)}) copy-start(s32[1,128]{1,0:T(1,128)} %tgt_ref.1) | copy-start | bytes 1540
  9.8 20.6 %copy-start.2 = (s32[1,128]{1,0:T(1,128)S(1)}, s32[1,128]{1,0:T(1,128)}, u32[]{:S(2)}) copy-start(s32[1,128]{1,0:T(1,128)} %src_ref.1) | copy-start | bytes 1540
  9.8 20.6 %copy-start.3 = (s32[1,128]{1,0:T(1,128)S(1)}, s32[1,128]{1,0:T(1,128)}, u32[]{:S(2)}) copy-start(s32[1,128]{1,0:T(1,128)} %off_ref.1) | copy-start | bytes 1540
  9.9 5.9 %collective-permute-start.1 = (f32[32,512]{1,0:T(8,128)S(1)}, f32[32,512]{1,0:T(8,128)S(1)}, u32[]{:S(2)}, u32[]{:S(2)}) collective-permute-start(f32[32,512]{1,0:T(8,128)S(1)} %get-tuple-element.36.after_ref), channel_id=1, source_target_pairs={{0,1},{1,0},{2,3},{3,2},{4,5},{5,4},{6,7},{7,6},{8,9},{9,8},{10,11... | collective-permute-start | bytes 196616 | tf_op jit(solution)/shard_map/ppermute | solution.py:571
  10.0 5.8 %collective-permute-start.2 = (f32[32,512]{1,0:T(8,128)S(1)}, f32[32,512]{1,0:T(8,128)S(1)}, u32[]{:S(2)}, u32[]{:S(2)}) collective-permute-start(f32[32,512]{1,0:T(8,128)S(1)} %get-tuple-element.38), channel_id=1, source_target_pairs={{0,2},{1,3},{2,0},{3,1},{4,6},{5,7},{6,4},{7,5},{8,10},{9,11},{10,... | collective-permute-start | bytes 196616 | tf_op jit(solution)/shard_map/ppermute | solution.py:571
  11.1 4.7 %collective-permute-start.3 = (f32[32,512]{1,0:T(8,128)S(1)}, f32[32,512]{1,0:T(8,128)S(1)}, u32[]{:S(2)}, u32[]{:S(2)}) collective-permute-start(f32[32,512]{1,0:T(8,128)S(1)} %get-tuple-element.39), channel_id=1, source_target_pairs={{0,3},{1,2},{2,1},{3,0},{4,7},{5,6},{6,5},{7,4},{8,11},{9,10},{10,... | collective-permute-start | bytes 196616 | tf_op jit(solution)/shard_map/ppermute | solution.py:571
  17.2 8.8 %collective-permute-start.4 = (f32[32,256]{1,0:T(8,128)S(1)}, f32[32,256]{1,0:T(8,128)S(1)}, u32[]{:S(2)}, u32[]{:S(2)}) collective-permute-start(f32[32,256]{1,0:T(8,128)S(1)} %get-tuple-element.43), channel_id=1, source_target_pairs={{0,1},{1,0},{2,3},{3,2},{4,5},{5,4},{6,7},{7,6},{8,9},{9,8},{10,11... | collective-permute-start | bytes 98312 | tf_op jit(solution)/shard_map/ppermute | solution.py:580
  17.6 9.9 %collective-permute-start.5 = (f32[32,256]{1,0:T(8,128)S(1)}, f32[32,256]{1,0:T(8,128)S(1)}, u32[]{:S(2)}, u32[]{:S(2)}) collective-permute-start(f32[32,256]{1,0:T(8,128)S(1)} %get-tuple-element.44), channel_id=1, source_target_pairs={{0,2},{1,3},{2,0},{3,1},{4,6},{5,7},{6,4},{7,5},{8,10},{9,11},{10,... | collective-permute-start | bytes 98312 | tf_op jit(solution)/shard_map/ppermute | solution.py:580
  18.7 18.1 %collective-permute-start.6 = (f32[32,256]{1,0:T(8,128)S(1)}, f32[32,256]{1,0:T(8,128)S(1)}, u32[]{:S(2)}, u32[]{:S(2)}) collective-permute-start(f32[32,256]{1,0:T(8,128)S(1)} %get-tuple-element.45), channel_id=1, source_target_pairs={{0,4},{1,5},{2,6},{3,7},{4,0},{5,1},{6,2},{7,3},{8,12},{9,13},{10,... | collective-permute-start | bytes 98312 | tf_op jit(solution)/shard_map/ppermute | solution.py:580
  21.7 15.0 %collective-permute-start.7 = (f32[32,256]{1,0:T(8,128)S(1)}, f32[32,256]{1,0:T(8,128)S(1)}, u32[]{:S(2)}, u32[]{:S(2)}) collective-permute-start(f32[32,256]{1,0:T(8,128)S(1)} %get-tuple-element.46), channel_id=1, source_target_pairs={{0,8},{1,9},{2,10},{3,11},{4,12},{5,13},{6,14},{7,15},{8,0},{9,1},... | collective-permute-start | bytes 98312 | tf_op jit(solution)/shard_map/ppermute | solution.py:580
  23.2 13.6 %collective-permute-start.8 = (f32[32,256]{1,0:T(8,128)S(1)}, f32[32,256]{1,0:T(8,128)S(1)}, u32[]{:S(2)}, u32[]{:S(2)}) collective-permute-start(f32[32,256]{1,0:T(8,128)S(1)} %get-tuple-element.47), channel_id=1, source_target_pairs={{0,16},{1,17},{2,18},{3,19},{4,20},{5,21},{6,22},{7,23},{8,24},{9,... | collective-permute-start | bytes 98312 | tf_op jit(solution)/shard_map/ppermute | solution.py:580
  26.0 10.8 %collective-permute-start.9 = (f32[32,256]{1,0:T(8,128)S(1)}, f32[32,256]{1,0:T(8,128)S(1)}, u32[]{:S(2)}, u32[]{:S(2)}) collective-permute-start(f32[32,256]{1,0:T(8,128)S(1)} %get-tuple-element.48), channel_id=1, source_target_pairs={{0,32},{1,33},{2,34},{3,35},{4,36},{5,37},{6,38},{7,39},{8,40},{9,... | collective-permute-start | bytes 98312 | tf_op jit(solution)/shard_map/ppermute | solution.py:580
  27.5 9.3 %collective-permute-start.10 = (f32[32,256]{1,0:T(8,128)S(1)}, f32[32,256]{1,0:T(8,128)S(1)}, u32[]{:S(2)}, u32[]{:S(2)}) collective-permute-start(f32[32,256]{1,0:T(8,128)S(1)} %get-tuple-element.49), channel_id=1, source_target_pairs={{0,64},{1,65},{2,66},{3,67},{4,68},{5,69},{6,70},{7,71},{8,72},{9,... | collective-permute-start | bytes 98312 | tf_op jit(solution)/shard_map/ppermute | solution.py:580

commit v10 on v9

--- a/solution.py
+++ b/solution.py
@@ -174,7 +174,7 @@
 J_BLOCKS = ROWS // J_STEP
 
 
-EARLY = 7
+EARLY = 9
 
 
 def operator_copy(op_hbm, buf_ref, sem, q, first=0):

time: 48.3 us -> 48.2 us (level)
  transfers between devices with their start and end apart: 11 -> 11, of which waited for: 0 -> 0; matrix products, arithmetic and copies ran while one was open for 0% -> 0% of each run, Pallas kernels for 30% -> 31%
where the time goes in v10:
time: 48.2 us; the launch traced here: 48.1 us
  Pallas kernels  29.1 us (60%)
  starting transfers between devices  18.8 us (39%)
    ppermute x7, starting transfers between devices, body(): lax.ppermute(rows, axes, [(i, i ^ 1 << level) for i in range(devices)])  12.8 us
    pallas_call x1, Pallas kernels, field(): pl.pallas_call(field_kernel, out_shape=jax.ShapeDtypeStruct((SLOTS, 4, BO...  11.3 us
    pallas_call x1, Pallas kernels, near_field(): pl.pallas_call(near_kernel, out_shape=jax.ShapeDtypeStruct((4, BODIES, SL...  6.31 us
    ppermute x4, starting transfers between devices, swap(): return lax.ppermute(rows, 'sub', [(i, i ^ k) for i in range(PEERS)])  5.98 us
    pallas_call x1, Pallas kernels, count_pairs(): pl.pallas_call(count_kernel, out_shape=[VMEM((CLASSES // 2, SOURCES, 256)...  4.61 us
    pallas_call x1, Pallas kernels, relay_operators(): pl.pallas_call(relay_kernel, out_shape=[VMEM((J_BLOCKS, 2 * I_ROWS, J_STE...  3.93 us
    pallas_call x1, Pallas kernels, pack_tiles(): pl.pallas_call(pack_kernel, out_shape=[VMEM(x.shape, x.dtype) for x in li...  1.54 us
    pallas_call x1, Pallas kernels, multipoles_of(): pl.pallas_call(multipole_kernel, out_shape=[jax.ShapeDtypeStruct((ROWS, S...  1.36 us
  transfers between devices with their start and end apart: 11, of which 0 were waited for; matrix products, arithmetic and copies ran while one was open for 0% of the time, Pallas kernels for 31%

profile of v10, /device:TPU:0, one launch (start us, length us, event | category | flops | bytes accessed | tf_op | source)
XLA Modules:
  0.0 48.1 jit_solution(6122870872154841146)
XLA Ops:
  0.0 1.5 %pack.1 = (s32[8,64,128]{2,1,0:T(8,128)S(1)}, s32[7,64,128]{2,1,0:T(8,128)S(1)}, s32[64,128]{1,0:T(8,128)S(1)}, s32[7,1,32]{2,1,0:T(1,128)S(1)}, f32[64,512]{1,0:T(8,128)S(1)}, /*index=5*/f32[64,512]{1,0:T(8,128)S(1)}) custom-call(s32[1,64]{1,0:T(1,128)} %bitcast.11, f32[3,64,128]{2,1,0:T(8,128)} %bitcast.8, f32[64,128]{1,0:T(8,128)} %mass_hbm.1, ...), custom_call_target="tpu_custom_call" | custom-call | tf_op jit(solution)/shard_map/pack/pallas_call | solution.py:130
  1.5 4.0 %collective-permute-start = (f32[64,512]{1,0:T(8,128)S(1)}, f32[64,512]{1,0:T(8,128)S(1)}, u32[]{:S(2)}, u32[]{:S(2)}) collective-permute-start(f32[64,512]{1,0:T(8,128)S(1)} %get-tuple-element.34), channel_id=1, source_target_pairs={{0,4},{1,5},{2,6},{3,7},{4,0},{5,1},{6,2},{7,3},{8,12},{9,13},{10,... | collective-permute-start | bytes 393224 | tf_op jit(solution)/shard_map/ppermute | solution.py:571
  5.6 4.6 %counts.1 = (bf16[64,352,256]{2,1,0:T(8,128)(2,1)S(1)}, f32[9,16,168,128]{3,2,1,0:T(8,128)S(1)}, f32[8,128]{1,0:T(8,128)S(1)}) custom-call(s32[8,64,128]{2,1,0:T(8,128)S(1)} %get-tuple-element.28.tgt_ref, s32[7,64,128]{2,1,0:T(8,128)S(1)} %get-tuple-element.29.far_ref, s32[64,128]{1,0:T(8,128)S(1)} %get-tuple-element.30.local_ref, f32[165,165,128]{2,1,0:T(8,128)} %op_hbm.3), custom_call_target="tpu_custom_call" | custom-call | flops 6000000000 | bytes 14000000 | tf_op jit(solution)/shard_map/counts/pallas_call | solution.py:267
  10.2 0.0 copy-start
  10.2 0.0 copy-start.1
  10.2 0.0 copy-start.2
  10.2 0.0 copy-start.3
  10.3 0.0 collective-permute-done.other_ref.refs_1_
  10.3 0.1 collective-permute-start.1
  10.4 1.1 %collective-permute-start.2 = (f32[32,512]{1,0:T(8,128)S(1)}, f32[32,512]{1,0:T(8,128)S(1)}, u32[]{:S(2)}, u32[]{:S(2)}) collective-permute-start(f32[32,512]{1,0:T(8,128)S(1)} %get-tuple-element.38), channel_id=1, source_target_pairs={{0,2},{1,3},{2,0},{3,1},{4,6},{5,7},{6,4},{7,5},{8,10},{9,11},{10,... | collective-permute-start | bytes 196616 | tf_op jit(solution)/shard_map/ppermute | solution.py:571
  11.5 0.8 %collective-permute-start.3 = (f32[32,512]{1,0:T(8,128)S(1)}, f32[32,512]{1,0:T(8,128)S(1)}, u32[]{:S(2)}, u32[]{:S(2)}) collective-permute-start(f32[32,512]{1,0:T(8,128)S(1)} %get-tuple-element.39), channel_id=1, source_target_pairs={{0,3},{1,2},{2,1},{3,0},{4,7},{5,6},{6,5},{7,4},{8,11},{9,10},{10,... | collective-permute-start | bytes 196616 | tf_op jit(solution)/shard_map/ppermute | solution.py:571
  12.2 3.9 %relay.1 = (bf16[21,352,1024]{2,1,0:T(8,128)(2,1)S(1)}, f32[8,128]{1,0:T(8,128)S(1)}) custom-call(f32[9,16,168,128]{3,2,1,0:T(8,128)S(1)} %get-tuple-element.32.buf_ref, f32[165,165,128]{2,1,0:T(8,128)} %op_hbm.3, f32[32,512]{1,0:T(8,128)S(1)} %get-tuple-element.36.after_ref), custom_call_target="tpu_custom_call" | custom-call | flops 4000000000 | bytes 1000000 | tf_op jit(solution)/shard_map/relay/pallas_call | solution.py:289
  16.2 0.0 collective-permute-done.1.refs_2_
  16.2 0.0 collective-permute-done.2.refs_3_
  16.2 0.0 collective-permute-done.3.refs_4_
  16.2 1.4 %multipoles.1 = (f32[168,128]{1,0:T(8,128)S(1)}, f32[4,128,128]{2,1,0:T(8,128)S(1)}, f32[32,256]{1,0:T(8,128)S(1)}, f32[32,256]{1,0:T(8,128)S(1)}, f32[32,256]{1...) custom-call(f32[64,512]{1,0:T(8,128)S(1)} %get-tuple-element.33.mine, ...), custom_call_target="tpu_custom_call" | custom-call | tf_op jit(solution)/shard_map/multipoles/pallas_call | solution.py:371
  17.6 0.4 collective-permute-start.4
  18.0 1.0 %collective-permute-start.5 = (f32[32,256]{1,0:T(8,128)S(1)}, f32[32,256]{1,0:T(8,128)S(1)}, u32[]{:S(2)}, u32[]{:S(2)}) collective-permute-start(f32[32,256]{1,0:T(8,128)S(1)} %get-tuple-element.44), channel_id=1, source_target_pairs={{0,2},{1,3},{2,0},{3,1},{4,6},{5,7},{6,4},{7,5},{8,10},{9,11},{10,... | collective-permute-start | bytes 98312 | tf_op jit(solution)/shard_map/ppermute | solution.py:580
  19.0 2.7 %collective-permute-start.6 = (f32[32,256]{1,0:T(8,128)S(1)}, f32[32,256]{1,0:T(8,128)S(1)}, u32[]{:S(2)}, u32[]{:S(2)}) collective-permute-start(f32[32,256]{1,0:T(8,128)S(1)} %get-tuple-element.45), channel_id=1, source_target_pairs={{0,4},{1,5},{2,6},{3,7},{4,0},{5,1},{6,2},{7,3},{8,12},{9,13},{10,... | collective-permute-start | bytes 98312 | tf_op jit(solution)/shard_map/ppermute | solution.py:580
  21.7 1.5 %collective-permute-start.7 = (f32[32,256]{1,0:T(8,128)S(1)}, f32[32,256]{1,0:T(8,128)S(1)}, u32[]{:S(2)}, u32[]{:S(2)}) collective-permute-start(f32[32,256]{1,0:T(8,128)S(1)} %get-tuple-element.46), channel_id=1, source_target_pairs={{0,8},{1,9},{2,10},{3,11},{4,12},{5,13},{6,14},{7,15},{8,0},{9,1},... | collective-permute-start | bytes 98312 | tf_op jit(solution)/shard_map/ppermute | solution.py:580
  23.2 2.7 %collective-permute-start.8 = (f32[32,256]{1,0:T(8,128)S(1)}, f32[32,256]{1,0:T(8,128)S(1)}, u32[]{:S(2)}, u32[]{:S(2)}) collective-permute-start(f32[32,256]{1,0:T(8,128)S(1)} %get-tuple-element.47), channel_id=1, source_target_pairs={{0,16},{1,17},{2,18},{3,19},{4,20},{5,21},{6,22},{7,23},{8,24},{9,... | collective-permute-start | bytes 98312 | tf_op jit(solution)/shard_map/ppermute | solution.py:580
  25.9 0.0 collective-permute-done.4.rest_0_
  25.9 1.6 %collective-permute-start.9 = (f32[32,256]{1,0:T(8,128)S(1)}, f32[32,256]{1,0:T(8,128)S(1)}, u32[]{:S(2)}, u32[]{:S(2)}) collective-permute-start(f32[32,256]{1,0:T(8,128)S(1)} %get-tuple-element.48), channel_id=1, source_target_pairs={{0,32},{1,33},{2,34},{3,35},{4,36},{5,37},{6,38},{7,39},{8,40},{9,... | collective-permute-start | bytes 98312 | tf_op jit(solution)/shard_map/ppermute | solution.py:580
  27.5 0.0 collective-permute-done.5.rest_1_
  27.5 2.9 %collective-permute-start.10 = (f32[32,256]{1,0:T(8,128)S(1)}, f32[32,256]{1,0:T(8,128)S(1)}, u32[]{:S(2)}, u32[]{:S(2)}) collective-permute-start(f32[32,256]{1,0:T(8,128)S(1)} %get-tuple-element.49), channel_id=1, source_target_pairs={{0,64},{1,65},{2,66},{3,67},{4,68},{5,69},{6,70},{7,71},{8,72},{9,... | collective-permute-start | bytes 98312 | tf_op jit(solution)/shard_map/ppermute | solution.py:580
  30.4 6.3 %near.1.rest_8_ = f32[4,128,128]{2,1,0:T(8,128)S(1)} custom-call(f32[4,128,128]{2,1,0:T(8,128)S(1)} %get-tuple-element.50.post_ref.rest_7_, s32[1,128]{1,0:T(1,128)S(1)} %copy-done.1, s32[1,128]{1,0:T(1,128)S(1)} %copy-done.2, s32[1,128]{1,0:T(1,128)S(1)} %copy-done.3), custom_call_target="tpu_custom_call" | custom-call | flops 8000000000 | bytes 1000000 | tf_op jit(solution)/shard_map/near/pallas_call | solution.py:439
  36.7 0.0 collective-permute-done.6.rest_2_
  36.8 0.0 collective-permute-done.7.rest_3_
  36.8 0.0 collective-permute-done.8.rest_4_
  36.8 0.0 collective-permute-done.9.rest_5_
  36.8 0.0 collective-permute-done.10.rest_6_
  36.8 11.3 %field.1 = f32[128,4,128]{2,1,0:T(4,128)} custom-call(bf16[64,352,256]{2,1,0:T(8,128)(2,1)S(1)} %get-tuple-element.31.counts_ref, bf16[21,352,1024]{2,1,0:T(8,128)(2,1)S(1)} %get-tuple-element.37.left_ref, f32[168,128]{1,0:T(8,128)S(1)} %get-tuple-element.42.mt_ref, f32[32,256]{1,0:T(8,128)S(1)} %collective-permute-done.4.rest_0_, ...), custom_call_target="tpu_custom_call" | custom-call | flops 40000000000 | bytes 26000000 | tf_op jit(solution)/shard_map/field/pallas_call | solution.py:534
  (5 shorter events, 0.0 us)
Async XLA Ops:
  1.5 8.7 %collective-permute-start = (f32[64,512]{1,0:T(8,128)S(1)}, f32[64,512]{1,0:T(8,128)S(1)}, u32[]{:S(2)}, u32[]{:S(2)}) collective-permute-start(f32[64,512]{1,0:T(8,128)S(1)} %get-tuple-element.34), channel_id=1, source_target_pairs={{0,4},{1,5},{2,6},{3,7},{4,0},{5,1},{6,2},{7,3},{8,12},{9,13},{10,... | collective-permute-start | bytes 393224 | tf_op jit(solution)/shard_map/ppermute | solution.py:571
  10.2 6.0 %copy-start = (f32[168,128]{1,0:T(8,128)S(1)}, f32[168,128]{1,0:T(8,128)}, u32[]{:S(2)}) copy-start(f32[168,128]{1,0:T(8,128)} %constant.2.clone.refs_7_.rest_9_) | copy-start | bytes 258052
  10.2 20.2 %copy-start.1 = (s32[1,128]{1,0:T(1,128)S(1)}, s32[1,128]{1,0:T(1,128)}, u32[]{:S(2)}) copy-start(s32[1,128]{1,0:T(1,128)} %tgt_ref.1) | copy-start | bytes 1540
  10.2 20.2 %copy-start.2 = (s32[1,128]{1,0:T(1,128)S(1)}, s32[1,128]{1,0:T(1,128)}, u32[]{:S(2)}) copy-start(s32[1,128]{1,0:T(1,128)} %src_ref.1) | copy-start | bytes 1540
  10.2 20.2 %copy-start.3 = (s32[1,128]{1,0:T(1,128)S(1)}, s32[1,128]{1,0:T(1,128)}, u32[]{:S(2)}) copy-start(s32[1,128]{1,0:T(1,128)} %off_ref.1) | copy-start | bytes 1540
  10.3 5.9 %collective-permute-start.1 = (f32[32,512]{1,0:T(8,128)S(1)}, f32[32,512]{1,0:T(8,128)S(1)}, u32[]{:S(2)}, u32[]{:S(2)}) collective-permute-start(f32[32,512]{1,0:T(8,128)S(1)} %get-tuple-element.36.after_ref), channel_id=1, source_target_pairs={{0,1},{1,0},{2,3},{3,2},{4,5},{5,4},{6,7},{7,6},{8,9},{9,8},{10,11... | collective-permute-start | bytes 196616 | tf_op jit(solution)/shard_map/ppermute | solution.py:571
  10.4 5.8 %collective-permute-start.2 = (f32[32,512]{1,0:T(8,128)S(1)}, f32[32,512]{1,0:T(8,128)S(1)}, u32[]{:S(2)}, u32[]{:S(2)}) collective-permute-start(f32[32,512]{1,0:T(8,128)S(1)} %get-tuple-element.38), channel_id=1, source_target_pairs={{0,2},{1,3},{2,0},{3,1},{4,6},{5,7},{6,4},{7,5},{8,10},{9,11},{10,... | collective-permute-start | bytes 196616 | tf_op jit(solution)/shard_map/ppermute | solution.py:571
  11.5 4.7 %collective-permute-start.3 = (f32[32,512]{1,0:T(8,128)S(1)}, f32[32,512]{1,0:T(8,128)S(1)}, u32[]{:S(2)}, u32[]{:S(2)}) collective-permute-start(f32[32,512]{1,0:T(8,128)S(1)} %get-tuple-element.39), channel_id=1, source_target_pairs={{0,3},{1,2},{2,1},{3,0},{4,7},{5,6},{6,5},{7,4},{8,11},{9,10},{10,... | collective-permute-start | bytes 196616 | tf_op jit(solution)/shard_map/ppermute | solution.py:571
  17.6 8.4 %collective-permute-start.4 = (f32[32,256]{1,0:T(8,128)S(1)}, f32[32,256]{1,0:T(8,128)S(1)}, u32[]{:S(2)}, u32[]{:S(2)}) collective-permute-start(f32[32,256]{1,0:T(8,128)S(1)} %get-tuple-element.43), channel_id=1, source_target_pairs={{0,1},{1,0},{2,3},{3,2},{4,5},{5,4},{6,7},{7,6},{8,9},{9,8},{10,11... | collective-permute-start | bytes 98312 | tf_op jit(solution)/shard_map/ppermute | solution.py:580
  18.0 9.5 %collective-permute-start.5 = (f32[32,256]{1,0:T(8,128)S(1)}, f32[32,256]{1,0:T(8,128)S(1)}, u32[]{:S(2)}, u32[]{:S(2)}) collective-permute-start(f32[32,256]{1,0:T(8,128)S(1)} %get-tuple-element.44), channel_id=1, source_target_pairs={{0,2},{1,3},{2,0},{3,1},{4,6},{5,7},{6,4},{7,5},{8,10},{9,11},{10,... | collective-permute-start | bytes 98312 | tf_op jit(solution)/shard_map/ppermute | solution.py:580
  19.0 17.7 %collective-permute-start.6 = (f32[32,256]{1,0:T(8,128)S(1)}, f32[32,256]{1,0:T(8,128)S(1)}, u32[]{:S(2)}, u32[]{:S(2)}) collective-permute-start(f32[32,256]{1,0:T(8,128)S(1)} %get-tuple-element.45), channel_id=1, source_target_pairs={{0,4},{1,5},{2,6},{3,7},{4,0},{5,1},{6,2},{7,3},{8,12},{9,13},{10,... | collective-permute-start | bytes 98312 | tf_op jit(solution)/shard_map/ppermute | solution.py:580
  21.7 15.0 %collective-permute-start.7 = (f32[32,256]{1,0:T(8,128)S(1)}, f32[32,256]{1,0:T(8,128)S(1)}, u32[]{:S(2)}, u32[]{:S(2)}) collective-permute-start(f32[32,256]{1,0:T(8,128)S(1)} %get-tuple-element.46), channel_id=1, source_target_pairs={{0,8},{1,9},{2,10},{3,11},{4,12},{5,13},{6,14},{7,15},{8,0},{9,1},... | collective-permute-start | bytes 98312 | tf_op jit(solution)/shard_map/ppermute | solution.py:580
  23.2 13.6 %collective-permute-start.8 = (f32[32,256]{1,0:T(8,128)S(1)}, f32[32,256]{1,0:T(8,128)S(1)}, u32[]{:S(2)}, u32[]{:S(2)}) collective-permute-start(f32[32,256]{1,0:T(8,128)S(1)} %get-tuple-element.47), channel_id=1, source_target_pairs={{0,16},{1,17},{2,18},{3,19},{4,20},{5,21},{6,22},{7,23},{8,24},{9,... | collective-permute-start | bytes 98312 | tf_op jit(solution)/shard_map/ppermute | solution.py:580
  25.9 10.8 %collective-permute-start.9 = (f32[32,256]{1,0:T(8,128)S(1)}, f32[32,256]{1,0:T(8,128)S(1)}, u32[]{:S(2)}, u32[]{:S(2)}) collective-permute-start(f32[32,256]{1,0:T(8,128)S(1)} %get-tuple-element.48), channel_id=1, source_target_pairs={{0,32},{1,33},{2,34},{3,35},{4,36},{5,37},{6,38},{7,39},{8,40},{9,... | collective-permute-start | bytes 98312 | tf_op jit(solution)/shard_map/ppermute | solution.py:580
  27.5 9.3 %collective-permute-start.10 = (f32[32,256]{1,0:T(8,128)S(1)}, f32[32,256]{1,0:T(8,128)S(1)}, u32[]{:S(2)}, u32[]{:S(2)}) collective-permute-start(f32[32,256]{1,0:T(8,128)S(1)} %get-tuple-element.49), channel_id=1, source_target_pairs={{0,64},{1,65},{2,66},{3,67},{4,68},{5,69},{6,70},{7,71},{8,72},{9,... | collective-permute-start | bytes 98312 | tf_op jit(solution)/shard_map/ppermute | solution.py:580
